TPU v7x, 32 devices: a whole 2x2x4 slice. The times are simulated.
32 devices in a mesh: grp: 4 (over y, x), box: 8 (over z, core).
Axes of the slice: x: 2, y: 2, z: 4, core: 2. Of those that a mesh axis runs over, the one named last changes fastest.
Arguments:
- volume: bfloat16 [256, 8, 256], P('grp', 'box'), may hold values from 0.19921875 to 1
- apertures: bfloat16 [6, 256, 8, 256], P(None, 'grp', 'box'), may hold values from 0.09 to 1
- conductivity: bfloat16 [256, 8, 256], P('grp', 'box'), may hold values from 0.19921875 to 5
- source: float32 [256, 8, 256], P('grp', 'box'), may hold values from -8 to 8
- previous: float32 [256, 8, 256], P('grp', 'box'), may hold values from -6 to 6
- cut_flags: int32 [16, 8], replicated, may hold values from 0 to 2
- new_group: int32 [16], replicated, may hold values from 0 to 3, as said below
Outputs:
- smoothed: float32 [384, 8, 256], P('grp', 'box')
Inputs may be any that keep to these rules, and one draw needn't show every extreme that they name: new_group never decreases along the layers; every boundary between consecutive groups lies at most one layer away from its place before the regrid, a multiple of 4; every group owns at least 2 and at most 6 layers, and some group exactly 6.
All inputs are finite; a program needn't handle non-finite values.
Results may differ from a plain program's by a relative error of at most 0.0007.
Values may be sent and summed in bfloat16 or wider, within the bound.
No kernel may reach another device: no remote copies, remote signals or barrier semaphores. Data moves between devices by JAX's collectives and lax.ppermute only.
A program may use at most 64 MiB of HBM per device.

v0:
```python
import jax
import jax.numpy as jnp
from jax import lax
from jax.sharding import PartitionSpec as P

SIDE = 16
LPD = 4
SWEEPS = 3


SIGMA = 0.05


def passed_along(value, axis, steps):
    count = lax.axis_size(axis)
    leading, last = (max(0, -steps), min(count, count - steps))
    return lax.ppermute(value, axis, [(source, source + steps) for source in range(leading, last)])


def new_block(from_below, owned_rows, from_above, offset_rows, axis_pos):
    padding_box = jnp.zeros_like(from_below)
    extended = jnp.concatenate(
        [from_below, owned_rows, from_above, padding_box, padding_box], axis=axis_pos
    )
    return lax.dynamic_slice_in_dim(extended, offset_rows, (LPD + 2) * SIDE, axis=axis_pos)


def per_device(volume, apertures, conductivity, source, previous, cut_flags, new_group):
    group_index = lax.axis_index("grp")
    column = lax.axis_index("box")
    box_count = lax.axis_size("box")
    box_rows = max(2, min(8, box_count // 4))
    box_cols = box_count // box_rows
    plane_size = SIDE * SIDE
    column_rows = (LPD + 2) * SIDE
    layers_here = jnp.sum((new_group == group_index).astype(jnp.int32))
    first_layer = jnp.sum((new_group < group_index).astype(jnp.int32))
    offset_rows = (first_layer - group_index * LPD + 1) * SIDE
    fraction_old = volume[:, 0, :]
    aperture_old = apertures[:, :, 0, :]
    conduct_old = conductivity[:, 0, :]
    source_old = source[:, 0, :]
    state_old = previous[:, 0, :]
    top_start = (LPD - 1) * SIDE
    geometry_top = (fraction_old[top_start:], aperture_old[:, top_start:], conduct_old[top_start:])
    geometry_bottom = (fraction_old[:SIDE], aperture_old[:, :SIDE], conduct_old[:SIDE])
    state_top = (source_old[top_start:], state_old[top_start:])
    state_bottom = (source_old[:SIDE], state_old[:SIDE])
    arrivals = []
    for offset, geometry_piece, state_piece in (
        (1, geometry_top, state_top),
        (-1, geometry_bottom, state_bottom),
    ):
        geometry_moved = passed_along(
            (geometry_piece[0], geometry_piece[1], geometry_piece[2]), "grp", offset
        )
        state_moved = passed_along((state_piece[0], state_piece[1]), "grp", offset)
        arrivals.append((geometry_moved, state_moved))
    geometry_below, state_below = arrivals[0]
    geometry_above, state_above = arrivals[1]
    fraction_new = new_block(geometry_below[0], fraction_old, geometry_above[0], offset_rows, 0)
    aperture_new = new_block(geometry_below[1], aperture_old, geometry_above[1], offset_rows, 1)
    conduct_new = new_block(geometry_below[2], conduct_old, geometry_above[2], offset_rows, 0)
    source_new = new_block(state_below[0], source_old, state_above[0], offset_rows, 0)
    state_new = new_block(state_below[1], state_old, state_above[1], offset_rows, 0)
    row_index = jnp.arange(column_rows, dtype=jnp.int32)
    valid_rows = (row_index < layers_here * SIDE)[:, None]
    flag_column = lax.dynamic_index_in_dim(cut_flags, column, 1, keepdims=False)
    flag_padded = jnp.concatenate([flag_column, jnp.zeros((LPD + 2,), jnp.int32)])
    flag_block = lax.dynamic_slice_in_dim(flag_padded, first_layer, LPD + 2)
    flag_rows = jnp.repeat(flag_block, SIDE)[:, None]
    regular = flag_rows == 1
    active_cells = valid_rows & (flag_rows != 0)
    fraction = jnp.where(regular, 1.0, fraction_new.astype(jnp.float32))
    conduct = conduct_new.astype(jnp.float32)
    weights = [
        jnp.where(regular, 1.0, aperture_new[face_index].astype(jnp.float32)) * conduct
        for face_index in range(6)
    ]
    diagonal = (
        SIGMA * fraction
        + weights[0]
        + weights[1]
        + weights[2]
        + weights[3]
        + weights[4]
        + weights[5]
    )
    diagonal = jnp.where(active_cells, diagonal, 1.0)
    forcing = fraction * source_new
    potential = jnp.where(valid_rows, state_new, 0.0)
    top_row = layers_here * SIDE - 1
    left_open = column % box_cols != 0
    right_open = column % box_cols != box_cols - 1
    cell_index = jnp.arange(plane_size, dtype=jnp.int32)
    parity = (row_index[:, None] + cell_index[None, :] // SIDE + cell_index[None, :] % SIDE) % 2
    lead_low = row_index % 2
    lead_high = (row_index + SIDE - 1) % 2
    plane_low = jnp.arange(SIDE, dtype=jnp.int32) % 2
    plane_high = (jnp.arange(SIDE, dtype=jnp.int32) + 1) % 2
    for sweep_index in range(SWEEPS):
        for colour in (0, 1):
            blocked = potential.reshape(column_rows, SIDE, SIDE)
            lateral = []
            for offset, rim_cells, leading in (
                (1, blocked[:, :, SIDE - 1], lead_high),
                (-1, blocked[:, :, 0], lead_low),
                (box_cols, blocked[:, SIDE - 1, :], lead_high),
                (-box_cols, blocked[:, 0, :], lead_low),
            ):
                payload = rim_cells
                arrived = passed_along(payload, "box", offset)
                lateral.append(arrived)
            plane_top = lax.dynamic_index_in_dim(potential, top_row, 0, keepdims=False).reshape(
                SIDE, SIDE
            )
            plane_bottom = potential[0].reshape(SIDE, SIDE)
            vertical = []
            for offset, face_plane, leading in (
                (1, plane_top, plane_high),
                (-1, plane_bottom, plane_low),
            ):
                payload = face_plane
                arrived = passed_along(payload, "grp", offset)
                vertical.append(arrived.reshape(plane_size))
            ghost_left = jnp.where(left_open, lateral[0], 0.0)
            ghost_right = jnp.where(right_open, lateral[1], 0.0)
            below_z = jnp.concatenate([vertical[0][None, :], potential[:-1]], axis=0)
            above_z = jnp.concatenate(
                [potential[1:], jnp.zeros((1, plane_size), jnp.float32)], axis=0
            )
            above_z = jnp.where((row_index == top_row)[:, None], vertical[1][None, :], above_z)
            low_y = jnp.concatenate([lateral[2][:, None, :], blocked[:, :-1, :]], axis=1).reshape(
                column_rows, plane_size
            )
            high_y = jnp.concatenate([blocked[:, 1:, :], lateral[3][:, None, :]], axis=1).reshape(
                column_rows, plane_size
            )
            low_x = jnp.concatenate([ghost_left[:, :, None], blocked[:, :, :-1]], axis=2).reshape(
                column_rows, plane_size
            )
            high_x = jnp.concatenate([blocked[:, :, 1:], ghost_right[:, :, None]], axis=2).reshape(
                column_rows, plane_size
            )
            gathered = (
                forcing
                + weights[0] * below_z
                + weights[1] * above_z
                + weights[2] * low_y
                + weights[3] * high_y
                + weights[4] * low_x
                + weights[5] * high_x
            )
            potential = jnp.where(active_cells & (parity == colour), gathered / diagonal, potential)
    return potential[:, None, :]


def solution(mesh):
    in_specs = (
        P("grp", "box", None),
        P(None, "grp", "box", None),
        P("grp", "box", None),
        P("grp", "box", None),
        P("grp", "box", None),
        P(),
        P(),
    )
    out_specs = P("grp", "box", None)
    return jax.shard_map(
        per_device, mesh=mesh, in_specs=in_specs, out_specs=out_specs, check_vma=False
    )
```

profile of v0, /device:TPU:5, one launch (start us, length us, event | category | flops | bytes accessed | tf_op | source)
XLA Modules:
  0.0 175.1 jit_solution(14017011872788100836)
XLA Ops:
  0.0 0.9 copy.93
  1.1 3.1 %collective-permute-start.9 = (f32[16,256]{0,1:T(8,128)S(1)}, f32[16,256]{0,1:T(8,128)S(1)}, u32[]{:S(2)}, u32[]{:S(2)}) collective-permute-start(f32[16,256]{0,1:T(8,128)S(1)} %get-tuple-element.88), channel_id=1, source_target_pairs={{8,0},{16,8},{24,16},{9,1},{17,9},{25,17},{10,2},{18,10},{26,18},{... | collective-permute-start | bytes 49160 | tf_op jit(solution)/shard_map/ppermute | solution.py:17
  4.1 2.2 %collective-permute-start.8 = (f32[16,256]{0,1:T(8,128)S(1)}, f32[16,256]{0,1:T(8,128)S(1)}, u32[]{:S(2)}, u32[]{:S(2)}) collective-permute-start(f32[16,256]{0,1:T(8,128)S(1)} %get-tuple-element.87), channel_id=1, source_target_pairs={{0,8},{8,16},{16,24},{1,9},{9,17},{17,25},{2,10},{10,18},{18,26},{... | collective-permute-start | bytes 49160 | tf_op jit(solution)/shard_map/ppermute | solution.py:17
  6.8 4.0 %collective-permute-start.5 = (bf16[6,16,256]{1,2,0:T(8,128)(2,1)S(1)}, bf16[6,16,256]{1,2,0:T(8,128)(2,1)S(1)}, u32[]{:S(2)}, u32[]{:S(2)}) collective-permute-start(bf16[6,16,256]{1,2,0:T(8,128)(2,1)S(1)} %get-tuple-element.24), channel_id=1, source_target_pairs={{8,0},{16,8},{24,16},{9,1},{17,9},{25,17},{10,2},{18,10},{26,18},{... | collective-permute-start | bytes 147464 | tf_op jit(solution)/shard_map/ppermute | solution.py:17
  10.8 1.9 %collective-permute-start.4 = (bf16[6,16,256]{1,2,0:T(8,128)(2,1)S(1)}, bf16[6,16,256]{1,2,0:T(8,128)(2,1)S(1)}, u32[]{:S(2)}, u32[]{:S(2)}) collective-permute-start(bf16[6,16,256]{1,2,0:T(8,128)(2,1)S(1)} %get-tuple-element.23), channel_id=1, source_target_pairs={{0,8},{8,16},{16,24},{1,9},{9,17},{17,25},{2,10},{10,18},{18,26},{... | collective-permute-start | bytes 147464 | tf_op jit(solution)/shard_map/ppermute | solution.py:17
  12.7 0.7 fusion.58
  17.0 0.7 slice_bitcast_fusion.10
  18.1 0.7 copy-done.6
  18.9 0.7 slice_bitcast_fusion.13
  20.8 0.6 fusion.88
  21.7 1.9 %collective-permute-start.10 = (f32[16,16]{1,0:T(8,128)S(1)}, f32[16,16]{1,0:T(8,128)S(1)}, u32[]{:S(2)}, u32[]{:S(2)}) collective-permute-start(f32[16,16]{1,0:T(8,128)S(1)} %reshape.222), channel_id=1, source_target_pairs={{0,8},{8,16},{16,24},{1,9},{9,17},{17,25},{2,10},{10,18},{18,26},{... | collective-permute-start | bytes 3080 | tf_op jit(solution)/shard_map/ppermute | solution.py:17
  23.6 4.6 %collective-permute-start.14 = (f32[96,16]{0,1:T(8,128)}, f32[96,16]{0,1:T(8,128)}, u32[]{:S(2)}, u32[]{:S(2)}) collective-permute-start(f32[96,16]{0,1:T(8,128)} %bitcast.26), channel_id=1, source_target_pairs={{0,1},{1,2},{2,3},{3,4},{4,5},{5,6},{6,7},{8,9},{9,10},{10,11},{11... | collective-permute-start | bytes 18440 | tf_op jit(solution)/shard_map/ppermute | solution.py:17
  28.2 0.7 reshape_squeeze.18
  28.9 4.5 %collective-permute-start.11 = (f32[16,16]{1,0:T(8,128)}, f32[16,16]{1,0:T(8,128)}, u32[]{:S(2)}, u32[]{:S(2)}) collective-permute-start(f32[16,16]{1,0:T(8,128)} %reshape_squeeze.18), channel_id=1, source_target_pairs={{8,0},{16,8},{24,16},{9,1},{17,9},{25,17},{10,2},{18,10},{26,18},{... | collective-permute-start | bytes 3080 | tf_op jit(solution)/shard_map/ppermute | solution.py:17
  33.4 0.6 slice_bitcast_fusion.25
  34.0 3.6 %collective-permute-start.7 = (bf16[16,256]{0,1:T(8,128)(2,1)}, bf16[16,256]{0,1:T(8,128)(2,1)}, u32[]{:S(2)}, u32[]{:S(2)}) collective-permute-start(bf16[16,256]{0,1:T(8,128)(2,1)} %get-tuple-element.92), channel_id=1, source_target_pairs={{8,0},{16,8},{24,16},{9,1},{17,9},{25,17},{10,2},{18,10},{26,18},{... | collective-permute-start | bytes 24584 | tf_op jit(solution)/shard_map/ppermute | solution.py:17
  37.8 2.2 %collective-permute-start.6 = (bf16[16,256]{0,1:T(8,128)(2,1)}, bf16[16,256]{0,1:T(8,128)(2,1)}, u32[]{:S(2)}, u32[]{:S(2)}) collective-permute-start(bf16[16,256]{0,1:T(8,128)(2,1)} %get-tuple-element.91), channel_id=1, source_target_pairs={{0,8},{8,16},{16,24},{1,9},{9,17},{17,25},{2,10},{10,18},{18,26},{... | collective-permute-start | bytes 24584 | tf_op jit(solution)/shard_map/ppermute | solution.py:17
  40.1 1.3 broadcast_in_dim.232
  41.4 2.1 %collective-permute-start.15 = (f32[96,16]{0,1:T(8,128)S(1)}, f32[96,16]{0,1:T(8,128)S(1)}, u32[]{:S(2)}, u32[]{:S(2)}) collective-permute-start(f32[96,16]{0,1:T(8,128)S(1)} %bitcast.392), channel_id=1, source_target_pairs={{1,0},{2,1},{3,2},{4,3},{5,4},{6,5},{7,6},{9,8},{10,9},{11,10},{12... | collective-permute-start | bytes 18440 | tf_op jit(solution)/shard_map/ppermute | solution.py:17
  43.5 0.7 broadcast_select_fusion.11
  44.2 2.3 %collective-permute-done.15 = f32[96,16]{0,1:T(8,128)S(1)} collective-permute-done((f32[96,16]{0,1:T(8,128)S(1)}, f32[96,16]{0,1:T(8,128)S(1)}, u32[]{:S(2)}, u32[]{:S(2)}) %collective-permute-start.15) | collective-permute-done | bytes 6176 | tf_op jit(solution)/shard_map/ppermute | solution.py:17
  46.5 1.3 collective-permute-start.13
  47.9 3.9 %collective-permute-done.13 = f32[96,16]{0,1:T(8,128)S(1)} collective-permute-done((f32[96,16]{0,1:T(8,128)S(1)}, f32[96,16]{0,1:T(8,128)S(1)}, u32[]{:S(2)}, u32[]{:S(2)}) %collective-permute-start.13) | collective-permute-done | bytes 6176 | tf_op jit(solution)/shard_map/ppermute | solution.py:17
  51.8 1.7 collective-permute-start.12
  53.5 0.8 collective-permute-done.12
  54.2 3.9 %collective-permute-start.3 = (f32[16,256]{0,1:T(8,128)S(1)}, f32[16,256]{0,1:T(8,128)S(1)}, u32[]{:S(2)}, u32[]{:S(2)}) collective-permute-start(f32[16,256]{0,1:T(8,128)S(1)} %get-tuple-element.76), channel_id=1, source_target_pairs={{8,0},{16,8},{24,16},{9,1},{17,9},{25,17},{10,2},{18,10},{26,18},{... | collective-permute-start | bytes 49160 | tf_op jit(solution)/shard_map/ppermute | solution.py:17
  58.2 1.9 %collective-permute-start.2 = (f32[16,256]{0,1:T(8,128)S(1)}, f32[16,256]{0,1:T(8,128)S(1)}, u32[]{:S(2)}, u32[]{:S(2)}) collective-permute-start(f32[16,256]{0,1:T(8,128)S(1)} %get-tuple-element.75), channel_id=1, source_target_pairs={{0,8},{8,16},{16,24},{1,9},{9,17},{17,25},{2,10},{10,18},{18,26},{... | collective-permute-start | bytes 49160 | tf_op jit(solution)/shard_map/ppermute | solution.py:17
  60.2 4.3 %collective-permute-start.1 = (bf16[16,256]{0,1:T(8,128)(2,1)S(1)}, bf16[16,256]{0,1:T(8,128)(2,1)S(1)}, u32[]{:S(2)}, u32[]{:S(2)}) collective-permute-start(bf16[16,256]{0,1:T(8,128)(2,1)S(1)} %copy-done.4), channel_id=1, source_target_pairs={{8,0},{16,8},{24,16},{9,1},{17,9},{25,17},{10,2},{18,10},{26,18},{... | collective-permute-start | bytes 24584 | tf_op jit(solution)/shard_map/ppermute | solution.py:17
  64.5 1.9 %collective-permute-start = (bf16[16,256]{0,1:T(8,128)(2,1)S(1)}, bf16[16,256]{0,1:T(8,128)(2,1)S(1)}, u32[]{:S(2)}, u32[]{:S(2)}) collective-permute-start(bf16[16,256]{0,1:T(8,128)(2,1)S(1)} %copy-done.3), channel_id=1, source_target_pairs={{0,8},{8,16},{16,24},{1,9},{9,17},{17,25},{2,10},{10,18},{18,26},{... | collective-permute-start | bytes 24584 | tf_op jit(solution)/shard_map/ppermute | solution.py:17
  66.4 0.7 fusion
  67.1 3.3 %collective-permute-done = bf16[16,256]{0,1:T(8,128)(2,1)S(1)} collective-permute-done((bf16[16,256]{0,1:T(8,128)(2,1)S(1)}, bf16[16,256]{0,1:T(8,128)(2,1)S(1)}, u32[]{:S(2)}, u32[]{:S(2)}) %collective-permute-start) | collective-permute-done | bytes 8224 | tf_op jit(solution)/shard_map/ppermute | solution.py:17
  70.4 0.6 copy-done.10
  71.1 1.5 fusion.13
  73.0 1.9 %collective-permute-start.16 = (f32[16,16]{1,0:T(8,128)S(1)}, f32[16,16]{1,0:T(8,128)S(1)}, u32[]{:S(2)}, u32[]{:S(2)}) collective-permute-start(f32[16,16]{1,0:T(8,128)S(1)} %reshape.228), channel_id=1, source_target_pairs={{0,8},{8,16},{16,24},{1,9},{9,17},{17,25},{2,10},{10,18},{18,26},{... | collective-permute-start | bytes 3080 | tf_op jit(solution)/shard_map/ppermute | solution.py:17
  75.0 3.7 %collective-permute-start.21 = (f32[96,16]{0,1:T(8,128)S(1)}, f32[96,16]{0,1:T(8,128)S(1)}, u32[]{:S(2)}, u32[]{:S(2)}) collective-permute-start(f32[96,16]{0,1:T(8,128)S(1)} %bitcast.393), channel_id=1, source_target_pairs={{1,0},{2,1},{3,2},{4,3},{5,4},{6,5},{7,6},{9,8},{10,9},{11,10},{12... | collective-permute-start | bytes 18440 | tf_op jit(solution)/shard_map/ppermute | solution.py:17
  78.8 4.5 %collective-permute-start.17 = (f32[16,16]{1,0:T(8,128)S(1)}, f32[16,16]{1,0:T(8,128)S(1)}, u32[]{:S(2)}, u32[]{:S(2)}) collective-permute-start(f32[16,16]{1,0:T(8,128)S(1)} %reshape_squeeze.19), channel_id=1, source_target_pairs={{8,0},{16,8},{24,16},{9,1},{17,9},{25,17},{10,2},{18,10},{26,18},{... | collective-permute-start | bytes 3080 | tf_op jit(solution)/shard_map/ppermute | solution.py:17
  83.3 4.1 %collective-permute-start.20 = (f32[96,16]{0,1:T(8,128)S(1)}, f32[96,16]{0,1:T(8,128)S(1)}, u32[]{:S(2)}, u32[]{:S(2)}) collective-permute-start(f32[96,16]{0,1:T(8,128)S(1)} %bitcast.388), channel_id=1, source_target_pairs={{0,1},{1,2},{2,3},{3,4},{4,5},{5,6},{6,7},{8,9},{9,10},{10,11},{11... | collective-permute-start | bytes 18440 | tf_op jit(solution)/shard_map/ppermute | solution.py:17
  87.4 1.3 collective-permute-start.19
  88.8 4.9 %collective-permute-start.18 = (f32[96,16]{0,1:T(8,128)S(1)}, f32[96,16]{0,1:T(8,128)S(1)}, u32[]{:S(2)}, u32[]{:S(2)}) collective-permute-start(f32[96,16]{0,1:T(8,128)S(1)} %get-tuple-element.67), channel_id=1, source_target_pairs={{0,4},{1,5},{2,6},{3,7},{8,12},{9,13},{10,14},{11,15},{16,20},{17,... | collective-permute-start | bytes 18440 | tf_op jit(solution)/shard_map/ppermute | solution.py:17
  95.2 1.9 %collective-permute-start.22 = (f32[16,16]{1,0:T(8,128)S(1)}, f32[16,16]{1,0:T(8,128)S(1)}, u32[]{:S(2)}, u32[]{:S(2)}) collective-permute-start(f32[16,16]{1,0:T(8,128)S(1)} %reshape.234), channel_id=1, source_target_pairs={{0,8},{8,16},{16,24},{1,9},{9,17},{17,25},{2,10},{10,18},{18,26},{... | collective-permute-start | bytes 3080 | tf_op jit(solution)/shard_map/ppermute | solution.py:17
  97.1 1.9 %collective-permute-start.27 = (f32[96,16]{0,1:T(8,128)S(1)}, f32[96,16]{0,1:T(8,128)S(1)}, u32[]{:S(2)}, u32[]{:S(2)}) collective-permute-start(f32[96,16]{0,1:T(8,128)S(1)} %bitcast.394), channel_id=1, source_target_pairs={{1,0},{2,1},{3,2},{4,3},{5,4},{6,5},{7,6},{9,8},{10,9},{11,10},{12... | collective-permute-start | bytes 18440 | tf_op jit(solution)/shard_map/ppermute | solution.py:17
  99.1 4.3 %collective-permute-start.23 = (f32[16,16]{1,0:T(8,128)S(1)}, f32[16,16]{1,0:T(8,128)S(1)}, u32[]{:S(2)}, u32[]{:S(2)}) collective-permute-start(f32[16,16]{1,0:T(8,128)S(1)} %reshape_squeeze.20), channel_id=1, source_target_pairs={{8,0},{16,8},{24,16},{9,1},{17,9},{25,17},{10,2},{18,10},{26,18},{... | collective-permute-start | bytes 3080 | tf_op jit(solution)/shard_map/ppermute | solution.py:17
  103.4 3.9 %collective-permute-start.26 = (f32[96,16]{0,1:T(8,128)S(1)}, f32[96,16]{0,1:T(8,128)S(1)}, u32[]{:S(2)}, u32[]{:S(2)}) collective-permute-start(f32[96,16]{0,1:T(8,128)S(1)} %bitcast.389), channel_id=1, source_target_pairs={{0,1},{1,2},{2,3},{3,4},{4,5},{5,6},{6,7},{8,9},{9,10},{10,11},{11... | collective-permute-start | bytes 18440 | tf_op jit(solution)/shard_map/ppermute | solution.py:17
  107.3 1.3 collective-permute-start.25
  108.7 4.9 %collective-permute-start.24 = (f32[96,16]{0,1:T(8,128)S(1)}, f32[96,16]{0,1:T(8,128)S(1)}, u32[]{:S(2)}, u32[]{:S(2)}) collective-permute-start(f32[96,16]{0,1:T(8,128)S(1)} %get-tuple-element.57), channel_id=1, source_target_pairs={{0,4},{1,5},{2,6},{3,7},{8,12},{9,13},{10,14},{11,15},{16,20},{17,... | collective-permute-start | bytes 18440 | tf_op jit(solution)/shard_map/ppermute | solution.py:17
  115.1 1.9 %collective-permute-start.28 = (f32[16,16]{1,0:T(8,128)S(1)}, f32[16,16]{1,0:T(8,128)S(1)}, u32[]{:S(2)}, u32[]{:S(2)}) collective-permute-start(f32[16,16]{1,0:T(8,128)S(1)} %reshape.240), channel_id=1, source_target_pairs={{0,8},{8,16},{16,24},{1,9},{9,17},{17,25},{2,10},{10,18},{18,26},{... | collective-permute-start | bytes 3080 | tf_op jit(solution)/shard_map/ppermute | solution.py:17
  117.0 1.9 %collective-permute-start.33 = (f32[96,16]{0,1:T(8,128)S(1)}, f32[96,16]{0,1:T(8,128)S(1)}, u32[]{:S(2)}, u32[]{:S(2)}) collective-permute-start(f32[96,16]{0,1:T(8,128)S(1)} %bitcast.395), channel_id=1, source_target_pairs={{1,0},{2,1},{3,2},{4,3},{5,4},{6,5},{7,6},{9,8},{10,9},{11,10},{12... | collective-permute-start | bytes 18440 | tf_op jit(solution)/shard_map/ppermute | solution.py:17
  119.0 4.3 %collective-permute-start.29 = (f32[16,16]{1,0:T(8,128)S(1)}, f32[16,16]{1,0:T(8,128)S(1)}, u32[]{:S(2)}, u32[]{:S(2)}) collective-permute-start(f32[16,16]{1,0:T(8,128)S(1)} %reshape_squeeze.21), channel_id=1, source_target_pairs={{8,0},{16,8},{24,16},{9,1},{17,9},{25,17},{10,2},{18,10},{26,18},{... | collective-permute-start | bytes 3080 | tf_op jit(solution)/shard_map/ppermute | solution.py:17
  123.3 3.9 %collective-permute-start.32 = (f32[96,16]{0,1:T(8,128)S(1)}, f32[96,16]{0,1:T(8,128)S(1)}, u32[]{:S(2)}, u32[]{:S(2)}) collective-permute-start(f32[96,16]{0,1:T(8,128)S(1)} %bitcast.390), channel_id=1, source_target_pairs={{0,1},{1,2},{2,3},{3,4},{4,5},{5,6},{6,7},{8,9},{9,10},{10,11},{11... | collective-permute-start | bytes 18440 | tf_op jit(solution)/shard_map/ppermute | solution.py:17
  127.2 1.3 collective-permute-start.31
  128.5 4.9 %collective-permute-start.30 = (f32[96,16]{0,1:T(8,128)S(1)}, f32[96,16]{0,1:T(8,128)S(1)}, u32[]{:S(2)}, u32[]{:S(2)}) collective-permute-start(f32[96,16]{0,1:T(8,128)S(1)} %get-tuple-element.47), channel_id=1, source_target_pairs={{0,4},{1,5},{2,6},{3,7},{8,12},{9,13},{10,14},{11,15},{16,20},{17,... | collective-permute-start | bytes 18440 | tf_op jit(solution)/shard_map/ppermute | solution.py:17
  135.0 1.9 %collective-permute-start.34 = (f32[16,16]{1,0:T(8,128)S(1)}, f32[16,16]{1,0:T(8,128)S(1)}, u32[]{:S(2)}, u32[]{:S(2)}) collective-permute-start(f32[16,16]{1,0:T(8,128)S(1)} %reshape.246), channel_id=1, source_target_pairs={{0,8},{8,16},{16,24},{1,9},{9,17},{17,25},{2,10},{10,18},{18,26},{... | collective-permute-start | bytes 3080 | tf_op jit(solution)/shard_map/ppermute | solution.py:17
  136.9 1.9 %collective-permute-start.39 = (f32[96,16]{0,1:T(8,128)S(1)}, f32[96,16]{0,1:T(8,128)S(1)}, u32[]{:S(2)}, u32[]{:S(2)}) collective-permute-start(f32[96,16]{0,1:T(8,128)S(1)} %bitcast.396), channel_id=1, source_target_pairs={{1,0},{2,1},{3,2},{4,3},{5,4},{6,5},{7,6},{9,8},{10,9},{11,10},{12... | collective-permute-start | bytes 18440 | tf_op jit(solution)/shard_map/ppermute | solution.py:17
  138.9 4.3 %collective-permute-start.35 = (f32[16,16]{1,0:T(8,128)S(1)}, f32[16,16]{1,0:T(8,128)S(1)}, u32[]{:S(2)}, u32[]{:S(2)}) collective-permute-start(f32[16,16]{1,0:T(8,128)S(1)} %reshape_squeeze.22), channel_id=1, source_target_pairs={{8,0},{16,8},{24,16},{9,1},{17,9},{25,17},{10,2},{18,10},{26,18},{... | collective-permute-start | bytes 3080 | tf_op jit(solution)/shard_map/ppermute | solution.py:17
  143.2 3.9 %collective-permute-start.38 = (f32[96,16]{0,1:T(8,128)S(1)}, f32[96,16]{0,1:T(8,128)S(1)}, u32[]{:S(2)}, u32[]{:S(2)}) collective-permute-start(f32[96,16]{0,1:T(8,128)S(1)} %bitcast.391), channel_id=1, source_target_pairs={{0,1},{1,2},{2,3},{3,4},{4,5},{5,6},{6,7},{8,9},{9,10},{10,11},{11... | collective-permute-start | bytes 18440 | tf_op jit(solution)/shard_map/ppermute | solution.py:17
  147.1 1.3 collective-permute-start.37
  148.4 4.9 %collective-permute-start.36 = (f32[96,16]{0,1:T(8,128)S(1)}, f32[96,16]{0,1:T(8,128)S(1)}, u32[]{:S(2)}, u32[]{:S(2)}) collective-permute-start(f32[96,16]{0,1:T(8,128)S(1)} %get-tuple-element.37), channel_id=1, source_target_pairs={{0,4},{1,5},{2,6},{3,7},{8,12},{9,13},{10,14},{11,15},{16,20},{17,... | collective-permute-start | bytes 18440 | tf_op jit(solution)/shard_map/ppermute | solution.py:17
  154.9 1.9 %collective-permute-start.40 = (f32[16,16]{1,0:T(8,128)S(1)}, f32[16,16]{1,0:T(8,128)S(1)}, u32[]{:S(2)}, u32[]{:S(2)}) collective-permute-start(f32[16,16]{1,0:T(8,128)S(1)} %reshape.252), channel_id=1, source_target_pairs={{0,8},{8,16},{16,24},{1,9},{9,17},{17,25},{2,10},{10,18},{18,26},{... | collective-permute-start | bytes 3080 | tf_op jit(solution)/shard_map/ppermute | solution.py:17
  156.8 1.9 %collective-permute-start.45 = (f32[96,16]{0,1:T(8,128)S(1)}, f32[96,16]{0,1:T(8,128)S(1)}, u32[]{:S(2)}, u32[]{:S(2)}) collective-permute-start(f32[96,16]{0,1:T(8,128)S(1)} %bitcast.397), channel_id=1, source_target_pairs={{1,0},{2,1},{3,2},{4,3},{5,4},{6,5},{7,6},{9,8},{10,9},{11,10},{12... | collective-permute-start | bytes 18440 | tf_op jit(solution)/shard_map/ppermute | solution.py:17
  158.8 4.3 %collective-permute-start.41 = (f32[16,16]{1,0:T(8,128)S(1)}, f32[16,16]{1,0:T(8,128)S(1)}, u32[]{:S(2)}, u32[]{:S(2)}) collective-permute-start(f32[16,16]{1,0:T(8,128)S(1)} %reshape_squeeze.23), channel_id=1, source_target_pairs={{8,0},{16,8},{24,16},{9,1},{17,9},{25,17},{10,2},{18,10},{26,18},{... | collective-permute-start | bytes 3080 | tf_op jit(solution)/shard_map/ppermute | solution.py:17
  163.1 3.9 %collective-permute-start.44 = (f32[96,16]{0,1:T(8,128)S(1)}, f32[96,16]{0,1:T(8,128)S(1)}, u32[]{:S(2)}, u32[]{:S(2)}) collective-permute-start(f32[96,16]{0,1:T(8,128)S(1)} %bitcast.387), channel_id=1, source_target_pairs={{0,1},{1,2},{2,3},{3,4},{4,5},{5,6},{6,7},{8,9},{9,10},{10,11},{11... | collective-permute-start | bytes 18440 | tf_op jit(solution)/shard_map/ppermute | solution.py:17
  167.0 1.3 collective-permute-start.43
  168.3 4.9 %collective-permute-start.42 = (f32[96,16]{0,1:T(8,128)S(1)}, f32[96,16]{0,1:T(8,128)S(1)}, u32[]{:S(2)}, u32[]{:S(2)}) collective-permute-start(f32[96,16]{0,1:T(8,128)S(1)} %get-tuple-element.27), channel_id=1, source_target_pairs={{0,4},{1,5},{2,6},{3,7},{8,12},{9,13},{10,14},{11,15},{16,20},{17,... | collective-permute-start | bytes 18440 | tf_op jit(solution)/shard_map/ppermute | solution.py:17
  174.3 0.7 copy.124
  (186 shorter events, 10.7 us)
Async XLA Ops:
  0.0 16.6 %copy-start = (s32[16,8]{0,1:T(8,128)S(1)}, s32[16,8]{0,1:T(8,128)}, u32[]{:S(2)}) copy-start(s32[16,8]{0,1:T(8,128)} %param.12) | copy-start | bytes 1540
  1.0 5.4 %copy-start.1 = (bf16[6,64,1,256]{3,1,2,0:T(8,128)(2,1)S(1)}, bf16[6,64,1,256]{3,1,2,0:T(8,128)(2,1)}, u32[]{:S(2)}) copy-start(bf16[6,64,1,256]{3,1,2,0:T(8,128)(2,1)} %param.8) | copy-start | bytes 589828
  1.1 19.4 %collective-permute-start.9 = (f32[16,256]{0,1:T(8,128)S(1)}, f32[16,256]{0,1:T(8,128)S(1)}, u32[]{:S(2)}, u32[]{:S(2)}) collective-permute-start(f32[16,256]{0,1:T(8,128)S(1)} %get-tuple-element.88), channel_id=1, source_target_pairs={{8,0},{16,8},{24,16},{9,1},{17,9},{25,17},{10,2},{18,10},{26,18},{... | collective-permute-start | bytes 49160 | tf_op jit(solution)/shard_map/ppermute | solution.py:17
  4.1 16.3 %collective-permute-start.8 = (f32[16,256]{0,1:T(8,128)S(1)}, f32[16,256]{0,1:T(8,128)S(1)}, u32[]{:S(2)}, u32[]{:S(2)}) collective-permute-start(f32[16,256]{0,1:T(8,128)S(1)} %get-tuple-element.87), channel_id=1, source_target_pairs={{0,8},{8,16},{16,24},{1,9},{9,17},{17,25},{2,10},{10,18},{18,26},{... | collective-permute-start | bytes 49160 | tf_op jit(solution)/shard_map/ppermute | solution.py:17
  6.6 6.1 %copy-start.14 = (s32[16]{0:T(128)S(1)}, s32[16]{0:T(128)}, u32[]{:S(2)}) copy-start(s32[16]{0:T(128)} %param.13) | copy-start | bytes 196
  6.8 10.1 %copy-start.5 = (bf16[64,1,256]{2,0,1:T(8,128)(2,1)S(1)}, bf16[64,1,256]{2,0,1:T(8,128)(2,1)}, u32[]{:S(2)}) copy-start(bf16[64,1,256]{2,0,1:T(8,128)(2,1)} %param.9) | copy-start | bytes 98308
  6.8 53.3 %collective-permute-start.5 = (bf16[6,16,256]{1,2,0:T(8,128)(2,1)S(1)}, bf16[6,16,256]{1,2,0:T(8,128)(2,1)S(1)}, u32[]{:S(2)}, u32[]{:S(2)}) collective-permute-start(bf16[6,16,256]{1,2,0:T(8,128)(2,1)S(1)} %get-tuple-element.24), channel_id=1, source_target_pairs={{8,0},{16,8},{24,16},{9,1},{17,9},{25,17},{10,2},{18,10},{26,18},{... | collective-permute-start | bytes 147464 | tf_op jit(solution)/shard_map/ppermute | solution.py:17
  10.8 53.7 %collective-permute-start.4 = (bf16[6,16,256]{1,2,0:T(8,128)(2,1)S(1)}, bf16[6,16,256]{1,2,0:T(8,128)(2,1)S(1)}, u32[]{:S(2)}, u32[]{:S(2)}) collective-permute-start(bf16[6,16,256]{1,2,0:T(8,128)(2,1)S(1)} %get-tuple-element.23), channel_id=1, source_target_pairs={{0,8},{8,16},{16,24},{1,9},{9,17},{17,25},{2,10},{10,18},{18,26},{... | collective-permute-start | bytes 147464 | tf_op jit(solution)/shard_map/ppermute | solution.py:17
  17.0 0.8 copy-start.2
  18.0 0.8 copy-start.6
  19.7 0.8 copy-start.11
  21.7 12.4 %collective-permute-start.10 = (f32[16,16]{1,0:T(8,128)S(1)}, f32[16,16]{1,0:T(8,128)S(1)}, u32[]{:S(2)}, u32[]{:S(2)}) collective-permute-start(f32[16,16]{1,0:T(8,128)S(1)} %reshape.222), channel_id=1, source_target_pairs={{0,8},{8,16},{16,24},{1,9},{9,17},{17,25},{2,10},{10,18},{18,26},{... | collective-permute-start | bytes 3080 | tf_op jit(solution)/shard_map/ppermute | solution.py:17
  23.6 17.8 %collective-permute-start.14 = (f32[96,16]{0,1:T(8,128)}, f32[96,16]{0,1:T(8,128)}, u32[]{:S(2)}, u32[]{:S(2)}) collective-permute-start(f32[96,16]{0,1:T(8,128)} %bitcast.26), channel_id=1, source_target_pairs={{0,1},{1,2},{2,3},{3,4},{4,5},{5,6},{6,7},{8,9},{9,10},{10,11},{11... | collective-permute-start | bytes 18440 | tf_op jit(solution)/shard_map/ppermute | solution.py:17
  28.9 8.9 %collective-permute-start.11 = (f32[16,16]{1,0:T(8,128)}, f32[16,16]{1,0:T(8,128)}, u32[]{:S(2)}, u32[]{:S(2)}) collective-permute-start(f32[16,16]{1,0:T(8,128)} %reshape_squeeze.18), channel_id=1, source_target_pairs={{8,0},{16,8},{24,16},{9,1},{17,9},{25,17},{10,2},{18,10},{26,18},{... | collective-permute-start | bytes 3080 | tf_op jit(solution)/shard_map/ppermute | solution.py:17
  34.0 24.2 %collective-permute-start.7 = (bf16[16,256]{0,1:T(8,128)(2,1)}, bf16[16,256]{0,1:T(8,128)(2,1)}, u32[]{:S(2)}, u32[]{:S(2)}) collective-permute-start(bf16[16,256]{0,1:T(8,128)(2,1)} %get-tuple-element.92), channel_id=1, source_target_pairs={{8,0},{16,8},{24,16},{9,1},{17,9},{25,17},{10,2},{18,10},{26,18},{... | collective-permute-start | bytes 24584 | tf_op jit(solution)/shard_map/ppermute | solution.py:17
  37.8 3.6 %copy-start.8 = (f32[96,16,1]{0,2,1:T(1,128)S(1)}, f32[96,16,1]{0,2,1:T(1,128)}, u32[]{:S(2)}) copy-start(f32[96,16,1]{0,2,1:T(1,128)} %get-tuple-element.84) | copy-start | bytes 18436
  37.8 29.3 %collective-permute-start.6 = (bf16[16,256]{0,1:T(8,128)(2,1)}, bf16[16,256]{0,1:T(8,128)(2,1)}, u32[]{:S(2)}, u32[]{:S(2)}) collective-permute-start(bf16[16,256]{0,1:T(8,128)(2,1)} %get-tuple-element.91), channel_id=1, source_target_pairs={{0,8},{8,16},{16,24},{1,9},{9,17},{17,25},{2,10},{10,18},{18,26},{... | collective-permute-start | bytes 24584 | tf_op jit(solution)/shard_map/ppermute | solution.py:17
  41.4 5.1 %copy-start.9 = (f32[96,16]{0,1:T(8,128)S(1)}, f32[96,16]{0,1:T(8,128)}, u32[]{:S(2)}) copy-start(f32[96,16]{0,1:T(8,128)} %get-tuple-element.80) | copy-start | bytes 18436
  41.4 5.1 %collective-permute-start.15 = (f32[96,16]{0,1:T(8,128)S(1)}, f32[96,16]{0,1:T(8,128)S(1)}, u32[]{:S(2)}, u32[]{:S(2)}) collective-permute-start(f32[96,16]{0,1:T(8,128)S(1)} %bitcast.392), channel_id=1, source_target_pairs={{1,0},{2,1},{3,2},{4,3},{5,4},{6,5},{7,6},{9,8},{10,9},{11,10},{12... | collective-permute-start | bytes 18440 | tf_op jit(solution)/shard_map/ppermute | solution.py:17
  46.5 5.3 %collective-permute-start.13 = (f32[96,16]{0,1:T(8,128)S(1)}, f32[96,16]{0,1:T(8,128)S(1)}, u32[]{:S(2)}, u32[]{:S(2)}) collective-permute-start(f32[96,16]{0,1:T(8,128)S(1)} %copy-done.9), channel_id=1, source_target_pairs={{4,0},{5,1},{6,2},{7,3},{12,8},{13,9},{14,10},{15,11},{20,16},{21,... | collective-permute-start | bytes 18440 | tf_op jit(solution)/shard_map/ppermute | solution.py:17
  47.8 4.0 %copy-start.7 = (f32[96,16]{0,1:T(8,128)S(1)}, f32[96,16]{0,1:T(8,128)}, u32[]{:S(2)}) copy-start(f32[96,16]{0,1:T(8,128)} %get-tuple-element.79) | copy-start | bytes 18436
  51.8 2.4 %collective-permute-start.12 = (f32[96,16]{0,1:T(8,128)S(1)}, f32[96,16]{0,1:T(8,128)S(1)}, u32[]{:S(2)}, u32[]{:S(2)}) collective-permute-start(f32[96,16]{0,1:T(8,128)S(1)} %copy-done.7), channel_id=1, source_target_pairs={{0,4},{1,5},{2,6},{3,7},{8,12},{9,13},{10,14},{11,15},{16,20},{17,... | collective-permute-start | bytes 18440 | tf_op jit(solution)/shard_map/ppermute | solution.py:17
  54.2 16.2 %collective-permute-start.3 = (f32[16,256]{0,1:T(8,128)S(1)}, f32[16,256]{0,1:T(8,128)S(1)}, u32[]{:S(2)}, u32[]{:S(2)}) collective-permute-start(f32[16,256]{0,1:T(8,128)S(1)} %get-tuple-element.76), channel_id=1, source_target_pairs={{8,0},{16,8},{24,16},{9,1},{17,9},{25,17},{10,2},{18,10},{26,18},{... | collective-permute-start | bytes 49160 | tf_op jit(solution)/shard_map/ppermute | solution.py:17
  58.2 2.0 %copy-start.4 = (bf16[16,256]{0,1:T(8,128)(2,1)S(1)}, bf16[16,256]{0,1:T(8,128)(2,1)}, u32[]{:S(2)}) copy-start(bf16[16,256]{0,1:T(8,128)(2,1)} %get-tuple-element.90) | copy-start | bytes 24580
  58.2 6.3 %copy-start.3 = (bf16[16,256]{0,1:T(8,128)(2,1)S(1)}, bf16[16,256]{0,1:T(8,128)(2,1)}, u32[]{:S(2)}) copy-start(bf16[16,256]{0,1:T(8,128)(2,1)} %get-tuple-element.89) | copy-start | bytes 24580
  58.2 12.2 %collective-permute-start.2 = (f32[16,256]{0,1:T(8,128)S(1)}, f32[16,256]{0,1:T(8,128)S(1)}, u32[]{:S(2)}, u32[]{:S(2)}) collective-permute-start(f32[16,256]{0,1:T(8,128)S(1)} %get-tuple-element.75), channel_id=1, source_target_pairs={{0,8},{8,16},{16,24},{1,9},{9,17},{17,25},{2,10},{10,18},{18,26},{... | collective-permute-start | bytes 49160 | tf_op jit(solution)/shard_map/ppermute | solution.py:17
  60.2 6.2 %copy-start.13 = (bf16[96]{0:T(256)(128)(2,1)S(1)}, bf16[96]{0:T(256)(128)(2,1)}, u32[]{:S(2)}) copy-start(bf16[96]{0:T(256)(128)(2,1)} %pad_dynamic-slice_fusion.1) | copy-start | bytes 580
  60.2 6.9 %collective-permute-start.1 = (bf16[16,256]{0,1:T(8,128)(2,1)S(1)}, bf16[16,256]{0,1:T(8,128)(2,1)S(1)}, u32[]{:S(2)}, u32[]{:S(2)}) collective-permute-start(bf16[16,256]{0,1:T(8,128)(2,1)S(1)} %copy-done.4), channel_id=1, source_target_pairs={{8,0},{16,8},{24,16},{9,1},{17,9},{25,17},{10,2},{18,10},{26,18},{... | collective-permute-start | bytes 24584 | tf_op jit(solution)/shard_map/ppermute | solution.py:17
  64.5 5.9 %collective-permute-start = (bf16[16,256]{0,1:T(8,128)(2,1)S(1)}, bf16[16,256]{0,1:T(8,128)(2,1)S(1)}, u32[]{:S(2)}, u32[]{:S(2)}) collective-permute-start(bf16[16,256]{0,1:T(8,128)(2,1)S(1)} %copy-done.3), channel_id=1, source_target_pairs={{0,8},{8,16},{16,24},{1,9},{9,17},{17,25},{2,10},{10,18},{18,26},{... | collective-permute-start | bytes 24584 | tf_op jit(solution)/shard_map/ppermute | solution.py:17
  70.4 0.7 copy-start.10
  70.4 0.7 copy-start.12
  73.0 15.7 %collective-permute-start.16 = (f32[16,16]{1,0:T(8,128)S(1)}, f32[16,16]{1,0:T(8,128)S(1)}, u32[]{:S(2)}, u32[]{:S(2)}) collective-permute-start(f32[16,16]{1,0:T(8,128)S(1)} %reshape.228), channel_id=1, source_target_pairs={{0,8},{8,16},{16,24},{1,9},{9,17},{17,25},{2,10},{10,18},{18,26},{... | collective-permute-start | bytes 3080 | tf_op jit(solution)/shard_map/ppermute | solution.py:17
  75.0 18.9 %collective-permute-start.21 = (f32[96,16]{0,1:T(8,128)S(1)}, f32[96,16]{0,1:T(8,128)S(1)}, u32[]{:S(2)}, u32[]{:S(2)}) collective-permute-start(f32[96,16]{0,1:T(8,128)S(1)} %bitcast.393), channel_id=1, source_target_pairs={{1,0},{2,1},{3,2},{4,3},{5,4},{6,5},{7,6},{9,8},{10,9},{11,10},{12... | collective-permute-start | bytes 18440 | tf_op jit(solution)/shard_map/ppermute | solution.py:17
  78.8 15.0 %collective-permute-start.17 = (f32[16,16]{1,0:T(8,128)S(1)}, f32[16,16]{1,0:T(8,128)S(1)}, u32[]{:S(2)}, u32[]{:S(2)}) collective-permute-start(f32[16,16]{1,0:T(8,128)S(1)} %reshape_squeeze.19), channel_id=1, source_target_pairs={{8,0},{16,8},{24,16},{9,1},{17,9},{25,17},{10,2},{18,10},{26,18},{... | collective-permute-start | bytes 3080 | tf_op jit(solution)/shard_map/ppermute | solution.py:17
  83.3 10.6 %collective-permute-start.20 = (f32[96,16]{0,1:T(8,128)S(1)}, f32[96,16]{0,1:T(8,128)S(1)}, u32[]{:S(2)}, u32[]{:S(2)}) collective-permute-start(f32[96,16]{0,1:T(8,128)S(1)} %bitcast.388), channel_id=1, source_target_pairs={{0,1},{1,2},{2,3},{3,4},{4,5},{5,6},{6,7},{8,9},{9,10},{10,11},{11... | collective-permute-start | bytes 18440 | tf_op jit(solution)/shard_map/ppermute | solution.py:17
  87.4 6.5 %collective-permute-start.19 = (f32[96,16]{0,1:T(8,128)S(1)}, f32[96,16]{0,1:T(8,128)S(1)}, u32[]{:S(2)}, u32[]{:S(2)}) collective-permute-start(f32[96,16]{0,1:T(8,128)S(1)} %get-tuple-element.68), channel_id=1, source_target_pairs={{4,0},{5,1},{6,2},{7,3},{12,8},{13,9},{14,10},{15,11},{20,16},{21,... | collective-permute-start | bytes 18440 | tf_op jit(solution)/shard_map/ppermute | solution.py:17
  88.8 5.7 %collective-permute-start.18 = (f32[96,16]{0,1:T(8,128)S(1)}, f32[96,16]{0,1:T(8,128)S(1)}, u32[]{:S(2)}, u32[]{:S(2)}) collective-permute-start(f32[96,16]{0,1:T(8,128)S(1)} %get-tuple-element.67), channel_id=1, source_target_pairs={{0,4},{1,5},{2,6},{3,7},{8,12},{9,13},{10,14},{11,15},{16,20},{17,... | collective-permute-start | bytes 18440 | tf_op jit(solution)/shard_map/ppermute | solution.py:17
  95.2 13.4 %collective-permute-start.22 = (f32[16,16]{1,0:T(8,128)S(1)}, f32[16,16]{1,0:T(8,128)S(1)}, u32[]{:S(2)}, u32[]{:S(2)}) collective-permute-start(f32[16,16]{1,0:T(8,128)S(1)} %reshape.234), channel_id=1, source_target_pairs={{0,8},{8,16},{16,24},{1,9},{9,17},{17,25},{2,10},{10,18},{18,26},{... | collective-permute-start | bytes 3080 | tf_op jit(solution)/shard_map/ppermute | solution.py:17
  97.1 16.6 %collective-permute-start.27 = (f32[96,16]{0,1:T(8,128)S(1)}, f32[96,16]{0,1:T(8,128)S(1)}, u32[]{:S(2)}, u32[]{:S(2)}) collective-permute-start(f32[96,16]{0,1:T(8,128)S(1)} %bitcast.394), channel_id=1, source_target_pairs={{1,0},{2,1},{3,2},{4,3},{5,4},{6,5},{7,6},{9,8},{10,9},{11,10},{12... | collective-permute-start | bytes 18440 | tf_op jit(solution)/shard_map/ppermute | solution.py:17
  99.1 14.5 %collective-permute-start.23 = (f32[16,16]{1,0:T(8,128)S(1)}, f32[16,16]{1,0:T(8,128)S(1)}, u32[]{:S(2)}, u32[]{:S(2)}) collective-permute-start(f32[16,16]{1,0:T(8,128)S(1)} %reshape_squeeze.20), channel_id=1, source_target_pairs={{8,0},{16,8},{24,16},{9,1},{17,9},{25,17},{10,2},{18,10},{26,18},{... | collective-permute-start | bytes 3080 | tf_op jit(solution)/shard_map/ppermute | solution.py:17
  103.4 10.4 %collective-permute-start.26 = (f32[96,16]{0,1:T(8,128)S(1)}, f32[96,16]{0,1:T(8,128)S(1)}, u32[]{:S(2)}, u32[]{:S(2)}) collective-permute-start(f32[96,16]{0,1:T(8,128)S(1)} %bitcast.389), channel_id=1, source_target_pairs={{0,1},{1,2},{2,3},{3,4},{4,5},{5,6},{6,7},{8,9},{9,10},{10,11},{11... | collective-permute-start | bytes 18440 | tf_op jit(solution)/shard_map/ppermute | solution.py:17
  107.3 6.5 %collective-permute-start.25 = (f32[96,16]{0,1:T(8,128)S(1)}, f32[96,16]{0,1:T(8,128)S(1)}, u32[]{:S(2)}, u32[]{:S(2)}) collective-permute-start(f32[96,16]{0,1:T(8,128)S(1)} %get-tuple-element.58), channel_id=1, source_target_pairs={{4,0},{5,1},{6,2},{7,3},{12,8},{13,9},{14,10},{15,11},{20,16},{21,... | collective-permute-start | bytes 18440 | tf_op jit(solution)/shard_map/ppermute | solution.py:17
  108.7 5.7 %collective-permute-start.24 = (f32[96,16]{0,1:T(8,128)S(1)}, f32[96,16]{0,1:T(8,128)S(1)}, u32[]{:S(2)}, u32[]{:S(2)}) collective-permute-start(f32[96,16]{0,1:T(8,128)S(1)} %get-tuple-element.57), channel_id=1, source_target_pairs={{0,4},{1,5},{2,6},{3,7},{8,12},{9,13},{10,14},{11,15},{16,20},{17,... | collective-permute-start | bytes 18440 | tf_op jit(solution)/shard_map/ppermute | solution.py:17
  115.1 13.4 %collective-permute-start.28 = (f32[16,16]{1,0:T(8,128)S(1)}, f32[16,16]{1,0:T(8,128)S(1)}, u32[]{:S(2)}, u32[]{:S(2)}) collective-permute-start(f32[16,16]{1,0:T(8,128)S(1)} %reshape.240), channel_id=1, source_target_pairs={{0,8},{8,16},{16,24},{1,9},{9,17},{17,25},{2,10},{10,18},{18,26},{... | collective-permute-start | bytes 3080 | tf_op jit(solution)/shard_map/ppermute | solution.py:17
  117.0 16.6 %collective-permute-start.33 = (f32[96,16]{0,1:T(8,128)S(1)}, f32[96,16]{0,1:T(8,128)S(1)}, u32[]{:S(2)}, u32[]{:S(2)}) collective-permute-start(f32[96,16]{0,1:T(8,128)S(1)} %bitcast.395), channel_id=1, source_target_pairs={{1,0},{2,1},{3,2},{4,3},{5,4},{6,5},{7,6},{9,8},{10,9},{11,10},{12... | collective-permute-start | bytes 18440 | tf_op jit(solution)/shard_map/ppermute | solution.py:17
  119.0 14.5 %collective-permute-start.29 = (f32[16,16]{1,0:T(8,128)S(1)}, f32[16,16]{1,0:T(8,128)S(1)}, u32[]{:S(2)}, u32[]{:S(2)}) collective-permute-start(f32[16,16]{1,0:T(8,128)S(1)} %reshape_squeeze.21), channel_id=1, source_target_pairs={{8,0},{16,8},{24,16},{9,1},{17,9},{25,17},{10,2},{18,10},{26,18},{... | collective-permute-start | bytes 3080 | tf_op jit(solution)/shard_map/ppermute | solution.py:17
  123.3 10.4 %collective-permute-start.32 = (f32[96,16]{0,1:T(8,128)S(1)}, f32[96,16]{0,1:T(8,128)S(1)}, u32[]{:S(2)}, u32[]{:S(2)}) collective-permute-start(f32[96,16]{0,1:T(8,128)S(1)} %bitcast.390), channel_id=1, source_target_pairs={{0,1},{1,2},{2,3},{3,4},{4,5},{5,6},{6,7},{8,9},{9,10},{10,11},{11... | collective-permute-start | bytes 18440 | tf_op jit(solution)/shard_map/ppermute | solution.py:17
  127.2 6.5 %collective-permute-start.31 = (f32[96,16]{0,1:T(8,128)S(1)}, f32[96,16]{0,1:T(8,128)S(1)}, u32[]{:S(2)}, u32[]{:S(2)}) collective-permute-start(f32[96,16]{0,1:T(8,128)S(1)} %get-tuple-element.48), channel_id=1, source_target_pairs={{4,0},{5,1},{6,2},{7,3},{12,8},{13,9},{14,10},{15,11},{20,16},{21,... | collective-permute-start | bytes 18440 | tf_op jit(solution)/shard_map/ppermute | solution.py:17
  128.5 5.7 %collective-permute-start.30 = (f32[96,16]{0,1:T(8,128)S(1)}, f32[96,16]{0,1:T(8,128)S(1)}, u32[]{:S(2)}, u32[]{:S(2)}) collective-permute-start(f32[96,16]{0,1:T(8,128)S(1)} %get-tuple-element.47), channel_id=1, source_target_pairs={{0,4},{1,5},{2,6},{3,7},{8,12},{9,13},{10,14},{11,15},{16,20},{17,... | collective-permute-start | bytes 18440 | tf_op jit(solution)/shard_map/ppermute | solution.py:17
  135.0 13.4 %collective-permute-start.34 = (f32[16,16]{1,0:T(8,128)S(1)}, f32[16,16]{1,0:T(8,128)S(1)}, u32[]{:S(2)}, u32[]{:S(2)}) collective-permute-start(f32[16,16]{1,0:T(8,128)S(1)} %reshape.246), channel_id=1, source_target_pairs={{0,8},{8,16},{16,24},{1,9},{9,17},{17,25},{2,10},{10,18},{18,26},{... | collective-permute-start | bytes 3080 | tf_op jit(solution)/shard_map/ppermute | solution.py:17
  136.9 16.6 %collective-permute-start.39 = (f32[96,16]{0,1:T(8,128)S(1)}, f32[96,16]{0,1:T(8,128)S(1)}, u32[]{:S(2)}, u32[]{:S(2)}) collective-permute-start(f32[96,16]{0,1:T(8,128)S(1)} %bitcast.396), channel_id=1, source_target_pairs={{1,0},{2,1},{3,2},{4,3},{5,4},{6,5},{7,6},{9,8},{10,9},{11,10},{12... | collective-permute-start | bytes 18440 | tf_op jit(solution)/shard_map/ppermute | solution.py:17
  138.9 14.5 %collective-permute-start.35 = (f32[16,16]{1,0:T(8,128)S(1)}, f32[16,16]{1,0:T(8,128)S(1)}, u32[]{:S(2)}, u32[]{:S(2)}) collective-permute-start(f32[16,16]{1,0:T(8,128)S(1)} %reshape_squeeze.22), channel_id=1, source_target_pairs={{8,0},{16,8},{24,16},{9,1},{17,9},{25,17},{10,2},{18,10},{26,18},{... | collective-permute-start | bytes 3080 | tf_op jit(solution)/shard_map/ppermute | solution.py:17
  143.2 10.4 %collective-permute-start.38 = (f32[96,16]{0,1:T(8,128)S(1)}, f32[96,16]{0,1:T(8,128)S(1)}, u32[]{:S(2)}, u32[]{:S(2)}) collective-permute-start(f32[96,16]{0,1:T(8,128)S(1)} %bitcast.391), channel_id=1, source_target_pairs={{0,1},{1,2},{2,3},{3,4},{4,5},{5,6},{6,7},{8,9},{9,10},{10,11},{11... | collective-permute-start | bytes 18440 | tf_op jit(solution)/shard_map/ppermute | solution.py:17
  147.1 6.5 %collective-permute-start.37 = (f32[96,16]{0,1:T(8,128)S(1)}, f32[96,16]{0,1:T(8,128)S(1)}, u32[]{:S(2)}, u32[]{:S(2)}) collective-permute-start(f32[96,16]{0,1:T(8,128)S(1)} %get-tuple-element.38), channel_id=1, source_target_pairs={{4,0},{5,1},{6,2},{7,3},{12,8},{13,9},{14,10},{15,11},{20,16},{21,... | collective-permute-start | bytes 18440 | tf_op jit(solution)/shard_map/ppermute | solution.py:17
  148.4 5.7 %collective-permute-start.36 = (f32[96,16]{0,1:T(8,128)S(1)}, f32[96,16]{0,1:T(8,128)S(1)}, u32[]{:S(2)}, u32[]{:S(2)}) collective-permute-start(f32[96,16]{0,1:T(8,128)S(1)} %get-tuple-element.37), channel_id=1, source_target_pairs={{0,4},{1,5},{2,6},{3,7},{8,12},{9,13},{10,14},{11,15},{16,20},{17,... | collective-permute-start | bytes 18440 | tf_op jit(solution)/shard_map/ppermute | solution.py:17
  154.9 13.4 %collective-permute-start.40 = (f32[16,16]{1,0:T(8,128)S(1)}, f32[16,16]{1,0:T(8,128)S(1)}, u32[]{:S(2)}, u32[]{:S(2)}) collective-permute-start(f32[16,16]{1,0:T(8,128)S(1)} %reshape.252), channel_id=1, source_target_pairs={{0,8},{8,16},{16,24},{1,9},{9,17},{17,25},{2,10},{10,18},{18,26},{... | collective-permute-start | bytes 3080 | tf_op jit(solution)/shard_map/ppermute | solution.py:17
  156.8 16.6 %collective-permute-start.45 = (f32[96,16]{0,1:T(8,128)S(1)}, f32[96,16]{0,1:T(8,128)S(1)}, u32[]{:S(2)}, u32[]{:S(2)}) collective-permute-start(f32[96,16]{0,1:T(8,128)S(1)} %bitcast.397), channel_id=1, source_target_pairs={{1,0},{2,1},{3,2},{4,3},{5,4},{6,5},{7,6},{9,8},{10,9},{11,10},{12... | collective-permute-start | bytes 18440 | tf_op jit(solution)/shard_map/ppermute | solution.py:17
  158.8 14.5 %collective-permute-start.41 = (f32[16,16]{1,0:T(8,128)S(1)}, f32[16,16]{1,0:T(8,128)S(1)}, u32[]{:S(2)}, u32[]{:S(2)}) collective-permute-start(f32[16,16]{1,0:T(8,128)S(1)} %reshape_squeeze.23), channel_id=1, source_target_pairs={{8,0},{16,8},{24,16},{9,1},{17,9},{25,17},{10,2},{18,10},{26,18},{... | collective-permute-start | bytes 3080 | tf_op jit(solution)/shard_map/ppermute | solution.py:17
  163.1 10.4 %collective-permute-start.44 = (f32[96,16]{0,1:T(8,128)S(1)}, f32[96,16]{0,1:T(8,128)S(1)}, u32[]{:S(2)}, u32[]{:S(2)}) collective-permute-start(f32[96,16]{0,1:T(8,128)S(1)} %bitcast.387), channel_id=1, source_target_pairs={{0,1},{1,2},{2,3},{3,4},{4,5},{5,6},{6,7},{8,9},{9,10},{10,11},{11... | collective-permute-start | bytes 18440 | tf_op jit(solution)/shard_map/ppermute | solution.py:17
  167.0 6.5 %collective-permute-start.43 = (f32[96,16]{0,1:T(8,128)S(1)}, f32[96,16]{0,1:T(8,128)S(1)}, u32[]{:S(2)}, u32[]{:S(2)}) collective-permute-start(f32[96,16]{0,1:T(8,128)S(1)} %get-tuple-element.28), channel_id=1, source_target_pairs={{4,0},{5,1},{6,2},{7,3},{12,8},{13,9},{14,10},{15,11},{20,16},{21,... | collective-permute-start | bytes 18440 | tf_op jit(solution)/shard_map/ppermute | solution.py:17
  168.3 5.7 %collective-permute-start.42 = (f32[96,16]{0,1:T(8,128)S(1)}, f32[96,16]{0,1:T(8,128)S(1)}, u32[]{:S(2)}, u32[]{:S(2)}) collective-permute-start(f32[96,16]{0,1:T(8,128)S(1)} %get-tuple-element.27), channel_id=1, source_target_pairs={{0,4},{1,5},{2,6},{3,7},{8,12},{9,13},{10,14},{11,15},{16,20},{17,... | collective-permute-start | bytes 18440 | tf_op jit(solution)/shard_map/ppermute | solution.py:17
where the time goes:
time: 177 us; the launch traced here: 175 us
  starting transfers between devices  138 us (78%)
  local copies, waits for them, and re-layouts  13.7 us (8%)
  waiting for transfers between devices  12.6 us (7%)
  other arithmetic  5.97 us (3%)
  between operations  4.53 us (3%)
    ppermute x46, starting transfers between devices, passed_along(): lax.ppermute(value, axis, [(source, source + steps) for source in range(l...  138 us
    ppermute x46, waiting for transfers between devices, passed_along(): lax.ppermute(value, axis, [(source, source + steps) for source in range(l...  12.6 us
  transfers between devices with their start and end apart: 46, of which 9 were waited for; matrix products, arithmetic and copies ran while one was open for 6% of the time, Pallas kernels for 0%

commit v1 on v0

v1 whole, which is shorter than its diff:
```python
import jax
import jax.numpy as jnp
from jax import lax
from jax.experimental import pallas as pl
from jax.experimental.pallas import tpu as pltpu
from jax.sharding import PartitionSpec as P

SIDE = 16
LPD = 4
SWEEPS = 3
SIGMA = 0.05
CELLS = SIDE * SIDE
ROWS = LPD * SIDE
OUT_ROWS = (LPD + 2) * SIDE
DEPTH = 2 * SWEEPS
REACH = 24
LANES = 128
XPOS = 32
COEFS = 8
RIM = COEFS * (DEPTH - 1) * SIDE + DEPTH * SIDE
CORNER = 96
F32 = jnp.float32
BF16 = jnp.bfloat16


def box_grid(box_count):
    box_rows = max(2, min(8, box_count // 4))
    return box_rows, box_count // box_rows


def split(value):
    high = value.astype(BF16)
    return high, (value - high.astype(F32)).astype(BF16)


def pack_kernel(vol, ap, cond, src, prev, flags, send_a, send_b, own_ap, own_qrp):
    group = lax.axis_index("grp")
    column = lax.axis_index("box")
    for layer in range(LPD):
        rows = pl.ds(layer * SIDE, SIDE)
        flag = flags[group * LPD + layer, column]
        regular = flag == 1
        covered = flag == 0
        inverse = 1.0 / cond[rows, :].astype(F32)
        fraction = jnp.where(regular, 1.0, vol[rows, :].astype(F32))
        q = jnp.where(covered, 1.0, (SIGMA * fraction) * inverse)
        own_qrp[0, rows, :] = q
        for half in range(2):
            cells = pl.ds(half * LANES, LANES)
            picked = pl.ds(layer * 2 * SIDE + half, SIDE, stride=2)
            before = prev[picked, :]
            scaled = fraction[:, half * LANES : (half + 1) * LANES] * inverse[:, half * LANES : (half + 1) * LANES]
            own_qrp[1, rows, cells] = jnp.where(covered, before, scaled * src[picked, :])
            own_qrp[2, rows, cells] = before
        for face in range(6):
            value = ap[face, rows, :].astype(F32)
            value = jnp.where(regular, 1.0, jnp.where(covered, 0.0, value))
            own_ap[face, rows, :] = value.astype(BF16)
    even = group % 2 == 0

    def emit(out, start):
        for face in range(6):
            out[face, :, :] = own_ap[face, pl.ds(start, REACH), :]
        for plane in range(3):
            high, low = split(own_qrp[plane, pl.ds(start, REACH), :])
            out[6 + 2 * plane, :, :] = high
            out[7 + 2 * plane, :, :] = low

    @pl.when(even)
    def _():
        emit(send_a, ROWS - REACH)
        emit(send_b, 0)

    @pl.when(jnp.logical_not(even))
    def _():
        emit(send_a, 0)
        emit(send_b, ROWS - REACH)


def corner_runs():
    runs = []
    row = 0
    for plane in range(COEFS + 1):
        reach = DEPTH - 1 if plane < COEFS else DEPTH
        for dy in range(1, reach):
            runs.append((plane, dy, reach - dy, row))
            row += reach - dy
    return runs


def turn_kernel(box_rows, box_cols, own_ap, own_qrp, from_a, from_b, *refs):
    n_rim = 3 if box_rows == 2 else 4
    turned = refs[0]
    rims = refs[1 : 1 + n_rim]
    corners = refs[1 + n_rim : -2]
    stage, corner_stage = refs[-2:]
    group = lax.axis_index("grp")
    column = lax.axis_index("box")
    even_group = group % 2 == 0
    box_x = column % box_cols
    box_y = column // box_cols
    stage[pl.ds(REACH + ROWS + REACH, LANES - REACH - ROWS - REACH), :] = jnp.zeros(
        (LANES - REACH - ROWS - REACH, CELLS), F32
    )
    for plane in range(9):
        if plane < 6:
            a = from_a[plane, :, :].astype(F32)
            b = from_b[plane, :, :].astype(F32)
            own = own_ap[plane, :, :].astype(F32)
        else:
            at = 6 + 2 * (plane - 6)
            a = from_a[at, :, :].astype(F32) + from_a[at + 1, :, :].astype(F32)
            b = from_b[at, :, :].astype(F32) + from_b[at + 1, :, :].astype(F32)
            own = own_qrp[plane - 6, :, :]
        stage[pl.ds(0, REACH), :] = jnp.where(even_group, b, a)
        stage[pl.ds(REACH, ROWS), :] = own
        stage[pl.ds(REACH + ROWS, REACH), :] = jnp.where(even_group, a, b)
        for half in range(2):
            turned[plane, pl.ds(half * LANES, LANES), :] = stage[:, pl.ds(half * LANES, LANES)].T

    def rim_y(out, high):
        for plane in range(COEFS + 1):
            reach = DEPTH - 1 if plane < COEFS else DEPTH
            start = (SIDE - reach) * SIDE if high else 0
            out[pl.ds(plane * (DEPTH - 1) * SIDE, reach * SIDE), :] = turned[
                plane, pl.ds(start, reach * SIDE), :
            ].astype(BF16)

    def rim_x(out, high):
        for plane in range(COEFS + 1):
            reach = DEPTH - 1 if plane < COEFS else DEPTH
            for i in range(reach):
                x = SIDE - reach + i if high else i
                out[pl.ds((plane * (DEPTH - 1) + i) * SIDE, SIDE), :] = turned[
                    plane, pl.ds(x, SIDE, stride=SIDE), :
                ].astype(BF16)

    def corner(out, high_y, high_x):
        for plane, dy, run, row in corner_runs():
            y = SIDE - dy if high_y else dy - 1
            x = SIDE - run if high_x else 0
            corner_stage[pl.ds(row, run), :] = turned[plane, pl.ds(y * SIDE + x, run), :]
        corner_stage[pl.ds(CORNER - 1, 1), :] = jnp.zeros((1, LANES), F32)
        out[...] = corner_stage[...].astype(BF16)

    for odd_x in (0, 1):

        @pl.when(box_x % 2 == odd_x)
        def _():
            rim_x(rims[0], odd_x == 0)
            rim_x(rims[1], odd_x == 1)

    for odd_y in (0, 1):

        @pl.when(box_y % 2 == odd_y)
        def _():
            rim_y(rims[2], odd_y == 0)
            if box_rows > 2:
                rim_y(rims[3], odd_y == 1)

        for odd_x in (0, 1):

            @pl.when((box_y % 2 == odd_y) & (box_x % 2 == odd_x))
            def _():
                corner(corners[0], odd_y == 0, odd_x == 0)
                corner(corners[1], odd_y == 0, odd_x == 1)
                if box_rows > 2:
                    corner(corners[2], odd_y == 1, odd_x == 0)
                    corner(corners[3], odd_y == 1, odd_x == 1)


def smooth_kernel(box_rows, box_cols, turned, *refs):
    n_rim = 3 if box_rows == 2 else 4
    n_corner = 2 if box_rows == 2 else 4
    rims = refs[:n_rim]
    corners = refs[n_rim : n_rim + n_corner]
    groups, out, planes, result = refs[n_rim + n_corner :]
    y_count = SIDE + DEPTH * (1 if box_rows == 2 else 2)
    low_base = y_count - DEPTH
    group = lax.axis_index("grp")
    column = lax.axis_index("box")
    box_x = column % box_cols
    box_y = column // box_cols

    for plane in range(9):
        for y in range(y_count):
            planes[plane, pl.ds(y * XPOS + SIDE, SIDE), :] = jnp.zeros((SIDE, LANES), F32)
            if y >= SIDE:
                planes[plane, pl.ds(y * XPOS, SIDE), :] = jnp.zeros((SIDE, LANES), F32)
            else:
                planes[plane, pl.ds(y * XPOS, SIDE), :] = turned[plane, pl.ds(y * SIDE, SIDE), :]

    def place_y(rim, high):
        for plane in range(COEFS + 1):
            reach = DEPTH - 1 if plane < COEFS else DEPTH
            for i in range(reach):
                y = SIDE + i if high else low_base + DEPTH - reach + i
                planes[plane, pl.ds(y * XPOS, SIDE), :] = rim[
                    pl.ds((plane * (DEPTH - 1) + i) * SIDE, SIDE), :
                ].astype(F32)

    def place_x(rim, high):
        for plane in range(COEFS + 1):
            reach = DEPTH - 1 if plane < COEFS else DEPTH
            for i in range(reach):
                x = SIDE + i if high else XPOS - reach + i
                planes[plane, pl.ds(x, SIDE, stride=XPOS), :] = rim[
                    pl.ds((plane * (DEPTH - 1) + i) * SIDE, SIDE), :
                ].astype(F32)

    def place_corner(piece, high_y, high_x):
        values = piece[...].astype(F32)
        for plane, dy, run, row in corner_runs():
            y = SIDE + dy - 1 if high_y else low_base + DEPTH - dy
            x = SIDE if high_x else XPOS - run
            planes[plane, pl.ds(y * XPOS + x, run), :] = values[row : row + run, :]

    for odd_x in (0, 1):

        @pl.when(box_x % 2 == odd_x)
        def _():
            place_x(rims[0], odd_x == 0)
            place_x(rims[1], odd_x == 1)

    for odd_y in (0, 1):

        @pl.when(box_y % 2 == odd_y)
        def _():
            place_y(rims[2], odd_y == 0)
            if box_rows > 2:
                place_y(rims[3], odd_y == 1)

        for odd_x in (0, 1):

            @pl.when((box_y % 2 == odd_y) & (box_x % 2 == odd_x))
            def _():
                place_corner(corners[0], odd_y == 0, odd_x == 0)
                place_corner(corners[1], odd_y == 0, odd_x == 1)
                if box_rows > 2:
                    place_corner(corners[2], odd_y == 1, odd_x == 0)
                    place_corner(corners[3], odd_y == 1, odd_x == 1)

    low_open = jnp.where(box_y > 0, 1.0, 0.0).astype(F32)
    high_open = jnp.where(box_y < box_rows - 1, 1.0, 0.0).astype(F32)
    for y in range(y_count):
        rows = pl.ds(y * XPOS, XPOS)
        weights = [planes[face, rows, :] for face in range(6)]
        total = planes[6, rows, :] + weights[0] + weights[1] + weights[2] + weights[3] + weights[4] + weights[5]
        inverse = 1.0 / jnp.where(total > 0.0, total, 1.0)
        for face in range(6):
            value = weights[face] * inverse
            if face == 2 and y == 0:
                value = value * low_open
            if face == 3 and y == SIDE - 1:
                value = value * high_open
            planes[face, rows, :] = value
        planes[7, rows, :] = planes[7, rows, :] * inverse

    parity = (
        lax.broadcasted_iota(jnp.int32, (XPOS, LANES), 0) + lax.broadcasted_iota(jnp.int32, (XPOS, LANES), 1)
    ) % 2
    for sweep in range(SWEEPS):
        for colour in (0, 1):
            for y in range(y_count):
                rows = pl.ds(y * XPOS, XPOS)
                here = planes[8, rows, :]
                low = planes[8, pl.ds((y - 1) % y_count * XPOS, XPOS), :]
                high = planes[8, pl.ds((y + 1) % y_count * XPOS, XPOS), :]
                gathered = (
                    planes[7, rows, :]
                    + planes[0, rows, :] * pltpu.roll(here, 1, 1)
                    + planes[1, rows, :] * pltpu.roll(here, LANES - 1, 1)
                    + planes[2, rows, :] * low
                    + planes[3, rows, :] * high
                    + planes[4, rows, :] * pltpu.roll(here, 1, 0)
                    + planes[5, rows, :] * pltpu.roll(here, XPOS - 1, 0)
                )
                planes[8, rows, :] = jnp.where(parity == (colour + y) % 2, gathered, here)

    for half in range(2):
        pieces = [planes[8, pl.ds((half * 8 + y) * XPOS, SIDE), :] for y in range(8)]
        result[pl.ds(0, LANES), pl.ds(half * LANES, LANES)] = jnp.concatenate(pieces, axis=0).T
    count = jnp.int32(0)
    first = jnp.int32(0)
    for layer in range(groups.shape[0]):
        owner = groups[layer]
        count = count + jnp.where(owner == group, 1, 0)
        first = first + jnp.where(owner < group, 1, 0)
    start = pl.multiple_of(REACH + (first - group * LPD) * SIDE, 8)
    valid = lax.broadcasted_iota(jnp.int32, (OUT_ROWS, LANES), 0) < count * SIDE
    for half in range(2):
        value = result[pl.ds(start, OUT_ROWS), pl.ds(half * LANES, LANES)]
        out[pl.ds(half, OUT_ROWS, stride=2), :] = jnp.where(valid, value, 0.0)


def swaps(count, kind):
    pairs = []
    for low in range(kind, count - 1, 2):
        pairs += [(low, low + 1), (low + 1, low)]
    return pairs


def lateral_pairs(box_rows, box_cols, kind_y, kind_x):
    move_y = dict(swaps(box_rows, kind_y)) if kind_y is not None else {i: i for i in range(box_rows)}
    move_x = dict(swaps(box_cols, kind_x)) if kind_x is not None else {i: i for i in range(box_cols)}
    return [
        (y * box_cols + x, move_y[y] * box_cols + move_x[x])
        for y in range(box_rows)
        for x in range(box_cols)
        if y in move_y and x in move_x
    ]


def vmem(count):
    return [pl.BlockSpec(memory_space=pltpu.VMEM)] * count


def per_device(volume, apertures, conductivity, source, previous, cut_flags, new_group):
    group_count = lax.axis_size("grp")
    box_rows, box_cols = box_grid(lax.axis_size("box"))
    smem = pl.BlockSpec(memory_space=pltpu.SMEM)
    piece = jax.ShapeDtypeStruct((12, REACH, CELLS), BF16)
    send_a, send_b, own_ap, own_qrp = pl.pallas_call(
        pack_kernel,
        out_shape=[
            piece,
            piece,
            jax.ShapeDtypeStruct((6, ROWS, CELLS), BF16),
            jax.ShapeDtypeStruct((3, ROWS, CELLS), F32),
        ],
        in_specs=vmem(5) + [smem],
        out_specs=vmem(4),
        name="pack",
    )(
        volume.reshape(ROWS, CELLS),
        apertures.reshape(6, ROWS, CELLS),
        conductivity.reshape(ROWS, CELLS),
        source.reshape(2 * ROWS, LANES),
        previous.reshape(2 * ROWS, LANES),
        cut_flags,
    )
    from_a = lax.ppermute(send_a, "grp", swaps(group_count, 0))
    from_b = lax.ppermute(send_b, "grp", swaps(group_count, 1))

    kinds = [(None, 0), (None, 1), (0, None), (0, 0), (0, 1)]
    if box_rows > 2:
        kinds = [(None, 0), (None, 1), (0, None), (1, None), (0, 0), (0, 1), (1, 0), (1, 1)]
    shapes = [
        jax.ShapeDtypeStruct((RIM if None in kind else CORNER, LANES), BF16) for kind in kinds
    ]
    turned, *sends = pl.pallas_call(
        lambda *refs: turn_kernel(box_rows, box_cols, *refs),
        out_shape=[jax.ShapeDtypeStruct((9, CELLS, LANES), F32)] + shapes,
        in_specs=vmem(4),
        out_specs=vmem(1 + len(kinds)),
        scratch_shapes=[pltpu.VMEM((LANES, CELLS), F32), pltpu.VMEM((CORNER, LANES), F32)],
        name="turn",
    )(own_ap, own_qrp, from_a, from_b)
    arrived = {}
    for index in sorted(range(len(kinds)), key=lambda i: (i != 2, kinds[i] == (None, 0))):
        arrived[index] = lax.ppermute(sends[index], "box", lateral_pairs(box_rows, box_cols, *kinds[index]))
    y_count = SIDE + DEPTH * (1 if box_rows == 2 else 2)
    smoothed = pl.pallas_call(
        lambda *refs: smooth_kernel(box_rows, box_cols, *refs),
        out_shape=jax.ShapeDtypeStruct((2 * OUT_ROWS, LANES), F32),
        in_specs=vmem(1 + len(kinds)) + [smem],
        out_specs=vmem(1)[0],
        scratch_shapes=[
            pltpu.VMEM((9, y_count * XPOS, LANES), F32),
            pltpu.VMEM((REACH + SIDE + OUT_ROWS, CELLS), F32),
        ],
        name="smooth",
    )(turned, *[arrived[index] for index in range(len(kinds))], new_group)
    return smoothed.reshape(OUT_ROWS, 1, CELLS)


def solution(mesh):
    in_specs = (
        P("grp", "box", None),
        P(None, "grp", "box", None),
        P("grp", "box", None),
        P("grp", "box", None),
        P("grp", "box", None),
        P(),
        P(),
    )
    out_specs = P("grp", "box", None)
    return jax.shard_map(
        per_device, mesh=mesh, in_specs=in_specs, out_specs=out_specs, check_vma=False
    )
```

time: 177 us -> 37.4 us (0.21)
  the two profiles are of different devices: /device:TPU:5 before, /device:TPU:2 now
where the time goes in v1:
time: 37.4 us; the launch traced here: 37.2 us
  waiting for transfers between devices  13.2 us (35%)
  starting transfers between devices  11.5 us (31%)
  Pallas kernels  9.58 us (26%)
  local copies, waits for them, and re-layouts  2.8 us (7%)
    ppermute x5, waiting for transfers between devices, per_device(): lax.ppermute(sends[index], 'box', lateral_pairs(box_rows, box_cols, *kind...  8.22 us
    ppermute x5, starting transfers between devices, per_device(): lax.ppermute(sends[index], 'box', lateral_pairs(box_rows, box_cols, *kind...  6.59 us
    ppermute x1, starting transfers between devices, per_device(): from_b = lax.ppermute(send_b, 'grp', swaps(group_count, 1))  4.88 us
    pallas_call x1, Pallas kernels, per_device(): pl.pallas_call(lambda *refs: smooth_kernel(box_rows, box_cols, *refs), ou...  4.63 us
    ppermute x1, waiting for transfers between devices, per_device(): from_b = lax.ppermute(send_b, 'grp', swaps(group_count, 1))  4.11 us
    pallas_call x1, Pallas kernels, per_device(): pl.pallas_call(lambda *refs: turn_kernel(box_rows, box_cols, *refs), out_...  2.96 us
    unnamed x15, local copies, waits for them, and re-layouts  2.8 us
    pallas_call x1, Pallas kernels, per_device(): pl.pallas_call(pack_kernel, out_shape=[piece, piece, jax.ShapeDtypeStruct...  1.99 us
  transfers between devices with their start and end apart: 7, of which 3 were waited for; matrix products, arithmetic and copies ran while one was open for 0% of the time, Pallas kernels for 0%

profile of v1, /device:TPU:2, one launch (start us, length us, event | category | flops | bytes accessed | tf_op | source)
XLA Modules:
  0.0 37.2 jit_solution(17598245114129267483)
XLA Ops:
  0.0 1.4 %copy.8.flags = s32[16,8]{1,0:T(8,128)} copy(s32[16,8]{0,1:T(8,128)} %param.12) | data formatting | bytes 1024 | tf_op args[5]
  1.4 2.0 %pack.1 = (bf16[12,24,256]{2,1,0:T(8,128)(2,1)}, bf16[12,24,256]{2,1,0:T(8,128)(2,1)}, bf16[6,64,256]{2,1,0:T(8,128)(2,1)}, f32[3,64,256]{2,1,0:T(8,128)}) custom-call(bf16[64,256]{1,0:T(8,128)(2,1)} %bitcast.9, bf16[6,64,256]{2,1,0:T(8,128)(2,1)} %bitcast.6, bf16[64,256]{1,0:T(8,128)(2,1)} %bitcast.10, f32[128,128]{1,0:T(8,128)} %bitcast.7, ...), custom_call_target="tpu_custom_call" | custom-call | tf_op jit(solution)/shard_map/pack/pallas_call | solution.py:323
  3.3 0.0 collective-permute-start
  3.3 4.9 %collective-permute-start.1 = (bf16[12,24,256]{2,1,0:T(8,128)(2,1)}, bf16[12,24,256]{2,1,0:T(8,128)(2,1)S(1)}, u32[]{:S(2)}, u32[]{:S(2)}) collective-permute-start(bf16[12,24,256]{2,1,0:T(8,128)(2,1)} %get-tuple-element.18), channel_id=1, source_target_pairs={{8,16},{16,8},{9,17},{17,9},{10,18},{18,10},{11,19},{19,11},{12,20... | collective-permute-start | bytes 442376 | tf_op jit(solution)/shard_map/ppermute | solution.py:343
  8.2 0.9 %collective-permute-done.refs_2_ = bf16[12,24,256]{2,1,0:T(8,128)(2,1)S(1)} collective-permute-done((bf16[12,24,256]{2,1,0:T(8,128)(2,1)}, bf16[12,24,256]{2,1,0:T(8,128)(2,1)S(1)}, u32[]{:S(2)}, u32[]{:S(2)}) %collective-permute-start) | collective-permute-done | bytes 147488 | tf_op jit(solution)/shard_map/ppermute | solution.py:342
  9.1 0.0 copy-start.3
  9.1 4.1 %collective-permute-done.1.refs_3_ = bf16[12,24,256]{2,1,0:T(8,128)(2,1)S(1)} collective-permute-done((bf16[12,24,256]{2,1,0:T(8,128)(2,1)}, bf16[12,24,256]{2,1,0:T(8,128)(2,1)S(1)}, u32[]{:S(2)}, u32[]{:S(2)}) %collective-permute-start.1) | collective-permute-done | bytes 147488 | tf_op jit(solution)/shard_map/ppermute | solution.py:343
  13.3 0.0 copy-start.4
  13.3 0.0 copy-done.3
  13.3 0.6 %copy-done.4 = bf16[12,24,256]{2,1,0:T(8,128)(2,1)} copy-done((bf16[12,24,256]{2,1,0:T(8,128)(2,1)}, bf16[12,24,256]{2,1,0:T(8,128)(2,1)S(1)}, u32[]{:S(2)}) %copy-start.4) | copy-done | bytes 147480
  13.9 3.0 %turn.1 = (f32[9,256,128]{2,1,0:T(8,128)}, bf16[736,128]{1,0:T(8,128)(2,1)}, bf16[736,128]{1,0:T(8,128)(2,1)}, bf16[736,128]{1,0:T(8,128)(2,1)}, bf16[96,128]{1,0:T(8,128)(2,1)}, /*index=5*/bf16[96,128]{1,0:T(8,128)(2,1)}) custom-call(bf16[6,64,256]{2,1,0:T(8,128)(2,1)} %get-tuple-element.15.refs_0_, f32[3,64,256]{2,1,0:T(8,128)} %get-tuple-element.16.refs_1_, ...), custom_call_target="tpu_custom_call" | custom-call | tf_op jit(solution)/shard_map/turn/pallas_call | solution.py:351
  16.9 0.0 collective-permute-start.2
  16.9 0.7 %collective-permute-start.3 = (bf16[736,128]{1,0:T(8,128)(2,1)}, bf16[736,128]{1,0:T(8,128)(2,1)S(1)}, u32[]{:S(2)}, u32[]{:S(2)}) collective-permute-start(bf16[736,128]{1,0:T(8,128)(2,1)} %get-tuple-element.21), channel_id=1, source_target_pairs={{1,2},{2,1},{5,6},{6,5},{9,10},{10,9},{13,14},{14,13},{17,18},{18,... | collective-permute-start | bytes 565256 | tf_op jit(solution)/shard_map/ppermute | solution.py:361
  17.6 2.7 %collective-permute-start.4 = (bf16[736,128]{1,0:T(8,128)(2,1)}, bf16[736,128]{1,0:T(8,128)(2,1)S(1)}, u32[]{:S(2)}, u32[]{:S(2)}) collective-permute-start(bf16[736,128]{1,0:T(8,128)(2,1)} %get-tuple-element.22), channel_id=1, source_target_pairs={{0,4},{1,5},{2,6},{3,7},{4,0},{5,1},{6,2},{7,3},{8,12},{9,13},{10,... | collective-permute-start | bytes 565256 | tf_op jit(solution)/shard_map/ppermute | solution.py:361
  20.2 2.6 %collective-permute-start.5 = (bf16[96,128]{1,0:T(8,128)(2,1)}, bf16[96,128]{1,0:T(8,128)(2,1)S(1)}, u32[]{:S(2)}, u32[]{:S(2)}) collective-permute-start(bf16[96,128]{1,0:T(8,128)(2,1)} %get-tuple-element.23), channel_id=1, source_target_pairs={{0,5},{1,4},{2,7},{3,6},{4,1},{5,0},{6,3},{7,2},{8,13},{9,12},{10,... | collective-permute-start | bytes 73736 | tf_op jit(solution)/shard_map/ppermute | solution.py:361
  22.8 0.7 %collective-permute-start.6 = (bf16[96,128]{1,0:T(8,128)(2,1)}, bf16[96,128]{1,0:T(8,128)(2,1)S(1)}, u32[]{:S(2)}, u32[]{:S(2)}) collective-permute-start(bf16[96,128]{1,0:T(8,128)(2,1)} %get-tuple-element.24), channel_id=1, source_target_pairs={{1,6},{2,5},{5,2},{6,1},{9,14},{10,13},{13,10},{14,9},{17,22},{18,... | collective-permute-start | bytes 73736 | tf_op jit(solution)/shard_map/ppermute | solution.py:361
  23.5 8.2 %collective-permute-done.5.refs_4_ = bf16[96,128]{1,0:T(8,128)(2,1)S(1)} collective-permute-done((bf16[96,128]{1,0:T(8,128)(2,1)}, bf16[96,128]{1,0:T(8,128)(2,1)S(1)}, u32[]{:S(2)}, u32[]{:S(2)}) %collective-permute-start.5) | collective-permute-done | bytes 24608 | tf_op jit(solution)/shard_map/ppermute | solution.py:361
  31.7 0.0 copy-start.5
  31.7 0.0 collective-permute-done.6.refs_5_
  31.7 0.0 copy-start.6
  31.7 0.0 collective-permute-done.2.refs_1_
  31.7 0.0 copy-start
  31.7 0.0 collective-permute-done.3.refs_2_
  31.7 0.0 copy-start.1
  31.7 0.0 collective-permute-done.4.refs_3_
  31.7 0.0 copy-start.2
  31.7 0.5 %copy-done.5 = bf16[96,128]{1,0:T(8,128)(2,1)} copy-done((bf16[96,128]{1,0:T(8,128)(2,1)}, bf16[96,128]{1,0:T(8,128)(2,1)S(1)}, u32[]{:S(2)}) %copy-start.5) | copy-done | bytes 24600
  32.3 0.0 copy-done.6
  32.3 0.1 copy-done
  32.4 0.1 copy-done.1
  32.5 0.1 copy-done.2
  32.5 4.6 %smooth.1 = f32[192,128]{1,0:T(8,128)} custom-call(f32[9,256,128]{2,1,0:T(8,128)} %get-tuple-element.19.refs_0_, bf16[736,128]{1,0:T(8,128)(2,1)} %copy-done, bf16[736,128]{1,0:T(8,128)(2,1)} %copy-done.1, bf16[736,128]{1,0:T(8,128)(2,1)} %copy-done.2, bf16[96,128]{1,0:T(8,128)(2,1)} %copy-done.5, bf16[96,128]{1,0:T(8,128)(2,1)} %copy-done.6, s32[16]{0:T(128)} %refs_6_.1), custom_call_target="tpu_custom_call" | custom-call | tf_op jit(solution)/shard_map/smooth/pallas_call | solution.py:363
Async XLA Ops:
  3.3 5.8 %collective-permute-start = (bf16[12,24,256]{2,1,0:T(8,128)(2,1)}, bf16[12,24,256]{2,1,0:T(8,128)(2,1)S(1)}, u32[]{:S(2)}, u32[]{:S(2)}) collective-permute-start(bf16[12,24,256]{2,1,0:T(8,128)(2,1)} %get-tuple-element.17), channel_id=1, source_target_pairs={{0,8},{8,0},{16,24},{24,16},{1,9},{9,1},{17,25},{25,17},{2,10},{10... | collective-permute-start | bytes 442376 | tf_op jit(solution)/shard_map/ppermute | solution.py:342
  3.3 9.9 %collective-permute-start.1 = (bf16[12,24,256]{2,1,0:T(8,128)(2,1)}, bf16[12,24,256]{2,1,0:T(8,128)(2,1)S(1)}, u32[]{:S(2)}, u32[]{:S(2)}) collective-permute-start(bf16[12,24,256]{2,1,0:T(8,128)(2,1)} %get-tuple-element.18), channel_id=1, source_target_pairs={{8,16},{16,8},{9,17},{17,9},{10,18},{18,10},{11,19},{19,11},{12,20... | collective-permute-start | bytes 442376 | tf_op jit(solution)/shard_map/ppermute | solution.py:343
  9.1 4.1 %copy-start.3 = (bf16[12,24,256]{2,1,0:T(8,128)(2,1)}, bf16[12,24,256]{2,1,0:T(8,128)(2,1)S(1)}, u32[]{:S(2)}) copy-start(bf16[12,24,256]{2,1,0:T(8,128)(2,1)S(1)} %collective-permute-done.refs_2_) | copy-start | bytes 442372
  13.3 0.6 %copy-start.4 = (bf16[12,24,256]{2,1,0:T(8,128)(2,1)}, bf16[12,24,256]{2,1,0:T(8,128)(2,1)S(1)}, u32[]{:S(2)}) copy-start(bf16[12,24,256]{2,1,0:T(8,128)(2,1)S(1)} %collective-permute-done.1.refs_3_) | copy-start | bytes 442372
  16.9 14.8 %collective-permute-start.2 = (bf16[736,128]{1,0:T(8,128)(2,1)}, bf16[736,128]{1,0:T(8,128)(2,1)S(1)}, u32[]{:S(2)}, u32[]{:S(2)}) collective-permute-start(bf16[736,128]{1,0:T(8,128)(2,1)} %get-tuple-element.20), channel_id=1, source_target_pairs={{0,1},{1,0},{2,3},{3,2},{4,5},{5,4},{6,7},{7,6},{8,9},{9,8},{10,11... | collective-permute-start | bytes 565256 | tf_op jit(solution)/shard_map/ppermute | solution.py:361
  16.9 14.8 %collective-permute-start.3 = (bf16[736,128]{1,0:T(8,128)(2,1)}, bf16[736,128]{1,0:T(8,128)(2,1)S(1)}, u32[]{:S(2)}, u32[]{:S(2)}) collective-permute-start(bf16[736,128]{1,0:T(8,128)(2,1)} %get-tuple-element.21), channel_id=1, source_target_pairs={{1,2},{2,1},{5,6},{6,5},{9,10},{10,9},{13,14},{14,13},{17,18},{18,... | collective-permute-start | bytes 565256 | tf_op jit(solution)/shard_map/ppermute | solution.py:361
  17.6 14.2 %collective-permute-start.4 = (bf16[736,128]{1,0:T(8,128)(2,1)}, bf16[736,128]{1,0:T(8,128)(2,1)S(1)}, u32[]{:S(2)}, u32[]{:S(2)}) collective-permute-start(bf16[736,128]{1,0:T(8,128)(2,1)} %get-tuple-element.22), channel_id=1, source_target_pairs={{0,4},{1,5},{2,6},{3,7},{4,0},{5,1},{6,2},{7,3},{8,12},{9,13},{10,... | collective-permute-start | bytes 565256 | tf_op jit(solution)/shard_map/ppermute | solution.py:361
  20.2 11.5 %collective-permute-start.5 = (bf16[96,128]{1,0:T(8,128)(2,1)}, bf16[96,128]{1,0:T(8,128)(2,1)S(1)}, u32[]{:S(2)}, u32[]{:S(2)}) collective-permute-start(bf16[96,128]{1,0:T(8,128)(2,1)} %get-tuple-element.23), channel_id=1, source_target_pairs={{0,5},{1,4},{2,7},{3,6},{4,1},{5,0},{6,3},{7,2},{8,13},{9,12},{10,... | collective-permute-start | bytes 73736 | tf_op jit(solution)/shard_map/ppermute | solution.py:361
  22.8 8.9 %collective-permute-start.6 = (bf16[96,128]{1,0:T(8,128)(2,1)}, bf16[96,128]{1,0:T(8,128)(2,1)S(1)}, u32[]{:S(2)}, u32[]{:S(2)}) collective-permute-start(bf16[96,128]{1,0:T(8,128)(2,1)} %get-tuple-element.24), channel_id=1, source_target_pairs={{1,6},{2,5},{5,2},{6,1},{9,14},{10,13},{13,10},{14,9},{17,22},{18,... | collective-permute-start | bytes 73736 | tf_op jit(solution)/shard_map/ppermute | solution.py:361
  31.7 0.6 %copy-start.5 = (bf16[96,128]{1,0:T(8,128)(2,1)}, bf16[96,128]{1,0:T(8,128)(2,1)S(1)}, u32[]{:S(2)}) copy-start(bf16[96,128]{1,0:T(8,128)(2,1)S(1)} %collective-permute-done.5.refs_4_) | copy-start | bytes 73732
  31.7 0.6 %copy-start.6 = (bf16[96,128]{1,0:T(8,128)(2,1)}, bf16[96,128]{1,0:T(8,128)(2,1)S(1)}, u32[]{:S(2)}) copy-start(bf16[96,128]{1,0:T(8,128)(2,1)S(1)} %collective-permute-done.6.refs_5_) | copy-start | bytes 73732
  31.7 0.7 %copy-start = (bf16[736,128]{1,0:T(8,128)(2,1)}, bf16[736,128]{1,0:T(8,128)(2,1)S(1)}, u32[]{:S(2)}) copy-start(bf16[736,128]{1,0:T(8,128)(2,1)S(1)} %collective-permute-done.2.refs_1_) | copy-start | bytes 565252
  31.7 0.8 %copy-start.1 = (bf16[736,128]{1,0:T(8,128)(2,1)}, bf16[736,128]{1,0:T(8,128)(2,1)S(1)}, u32[]{:S(2)}) copy-start(bf16[736,128]{1,0:T(8,128)(2,1)S(1)} %collective-permute-done.3.refs_2_) | copy-start | bytes 565252
  31.7 0.8 %copy-start.2 = (bf16[736,128]{1,0:T(8,128)(2,1)}, bf16[736,128]{1,0:T(8,128)(2,1)S(1)}, u32[]{:S(2)}) copy-start(bf16[736,128]{1,0:T(8,128)(2,1)S(1)} %collective-permute-done.4.refs_3_) | copy-start | bytes 565252

commit v2 on v1

v2 whole, which is shorter than its diff:
```python
import jax
import jax.numpy as jnp
from jax import lax
from jax.experimental import pallas as pl
from jax.experimental.pallas import tpu as pltpu
from jax.sharding import PartitionSpec as P

SIDE = 16
LPD = 4
SWEEPS = 3
SIGMA = 0.05
CELLS = SIDE * SIDE
ROWS = LPD * SIDE
OUT_ROWS = (LPD + 2) * SIDE
DEPTH = 2 * SWEEPS
REACH = 24
LANES = 128
XPOS = 32
COEFS = 8
RIM = COEFS * (DEPTH - 1) * SIDE + DEPTH * SIDE
CORNER = 96
F32 = jnp.float32
BF16 = jnp.bfloat16


def box_grid(box_count):
    box_rows = max(2, min(8, box_count // 4))
    return box_rows, box_count // box_rows


def split(value):
    high = value.astype(BF16)
    return high, (value - high.astype(F32)).astype(BF16)


def cell_planes(start, count, flag, vol, ap, cond, src, prev, put):
    rows = pl.ds(start, count)
    regular = flag == 1
    covered = flag == 0
    inverse = 1.0 / cond[rows, :].astype(F32)
    fraction = jnp.where(regular, 1.0, vol[rows, :].astype(F32))
    for face in range(6):
        value = ap[face, rows, :].astype(F32)
        put(face, slice(None), jnp.where(regular, 1.0, jnp.where(covered, 0.0, value)))
    put(6, slice(None), jnp.where(covered, 1.0, (SIGMA * fraction) * inverse))
    scale = fraction * inverse
    for half in range(2):
        cells = slice(half * LANES, (half + 1) * LANES)
        picked = pl.ds(2 * start + half, count, stride=2)
        before = prev[picked, :]
        put(7, cells, jnp.where(covered, before, scale[:, cells] * src[picked, :]))
        put(8, cells, before)


def pack_kernel(vol, ap, cond, src, prev, flags, send_a, send_b):
    group = lax.axis_index("grp")
    column = lax.axis_index("box")

    def emit(out, first):
        for layer in range(LPD):
            low, high = max(layer * SIDE, first), min((layer + 1) * SIDE, first + REACH)
            if low >= high:
                continue
            rows = pl.ds(low - first, high - low)

            def put(plane, cells, value, rows=rows):
                if plane < 6:
                    out[plane, rows, cells] = value.astype(BF16)
                else:
                    at = 6 + 2 * (plane - 6)
                    out[at, rows, cells], out[at + 1, rows, cells] = split(value)

            cell_planes(low, high - low, flags[column, group * LPD + layer], vol, ap, cond, src, prev, put)

    for odd in (0, 1):

        @pl.when(group % 2 == odd)
        def _():
            emit(send_a, 0 if odd else ROWS - REACH)
            emit(send_b, ROWS - REACH if odd else 0)


def own_kernel(vol, ap, cond, src, prev, flags, own):
    group = lax.axis_index("grp")
    column = lax.axis_index("box")
    for layer in range(LPD):

        def put(plane, cells, value, rows=pl.ds(layer * SIDE, SIDE)):
            own[plane, rows, cells] = value

        cell_planes(layer * SIDE, SIDE, flags[column, group * LPD + layer], vol, ap, cond, src, prev, put)


def corner_runs():
    runs = []
    row = 0
    for plane in range(COEFS + 1):
        reach = DEPTH - 1 if plane < COEFS else DEPTH
        for dy in range(1, reach):
            runs.append((plane, dy, reach - dy, row))
            row += reach - dy
    return runs


def turn_kernel(box_rows, box_cols, own, from_a, from_b, turned, *refs):
    rims, stage = refs[:-1], refs[-1]
    even_group = lax.axis_index("grp") % 2 == 0
    box_y = lax.axis_index("box") // box_cols
    used = REACH + ROWS + REACH
    stage[pl.ds(used, LANES - used), :] = jnp.zeros((LANES - used, CELLS), F32)
    for plane in range(9):
        if plane < 6:
            a = from_a[plane, :, :].astype(F32)
            b = from_b[plane, :, :].astype(F32)
        else:
            at = 6 + 2 * (plane - 6)
            a = from_a[at, :, :].astype(F32) + from_a[at + 1, :, :].astype(F32)
            b = from_b[at, :, :].astype(F32) + from_b[at + 1, :, :].astype(F32)
        stage[pl.ds(0, REACH), :] = jnp.where(even_group, b, a)
        stage[pl.ds(REACH, ROWS), :] = own[plane, :, :]
        stage[pl.ds(REACH + ROWS, REACH), :] = jnp.where(even_group, a, b)
        for half in range(2):
            turned[plane, pl.ds(half * LANES, LANES), :] = stage[:, pl.ds(half * LANES, LANES)].T

    def rim(out, high):
        for plane in range(COEFS + 1):
            reach = DEPTH - 1 if plane < COEFS else DEPTH
            start = (SIDE - reach) * SIDE if high else 0
            out[pl.ds(plane * (DEPTH - 1) * SIDE, reach * SIDE), :] = turned[
                plane, pl.ds(start, reach * SIDE), :
            ].astype(BF16)

    for odd in (0, 1):

        @pl.when(box_y % 2 == odd)
        def _():
            for kind, out in enumerate(rims):
                rim(out, odd == kind)


def rims_kernel(box_rows, box_cols, turned, *refs):
    rims, corners, stage = refs[:2], refs[2:-1], refs[-1]
    box_x = lax.axis_index("box") % box_cols
    box_y = lax.axis_index("box") // box_cols

    def rim(out, high):
        for plane in range(COEFS + 1):
            reach = DEPTH - 1 if plane < COEFS else DEPTH
            for i in range(reach):
                x = SIDE - reach + i if high else i
                out[pl.ds((plane * (DEPTH - 1) + i) * SIDE, SIDE), :] = turned[
                    plane, pl.ds(x, SIDE, stride=SIDE), :
                ].astype(BF16)

    def corner(out, high_y, high_x):
        for plane, dy, run, row in corner_runs():
            y = SIDE - dy if high_y else dy - 1
            x = SIDE - run if high_x else 0
            stage[pl.ds(row, run), :] = turned[plane, pl.ds(y * SIDE + x, run), :]
        stage[pl.ds(CORNER - 1, 1), :] = jnp.zeros((1, LANES), F32)
        out[...] = stage[...].astype(BF16)

    for odd_x in (0, 1):

        @pl.when(box_x % 2 == odd_x)
        def _():
            rim(rims[0], odd_x == 0)
            rim(rims[1], odd_x == 1)

        for odd_y in (0, 1):

            @pl.when((box_y % 2 == odd_y) & (box_x % 2 == odd_x))
            def _():
                for index, out in enumerate(corners):
                    corner(out, odd_y == index // 2, odd_x == index % 2)


def normal(values):
    total = values[6]
    for face in range(6):
        total = total + values[face]
    inverse = 1.0 / jnp.where(total > 0.0, total, 1.0)
    return [values[face] * inverse for face in range(6)] + [values[7] * inverse]


def rows_of(box_rows):
    return SIDE + DEPTH * (1 if box_rows == 2 else 2)


def prepare_kernel(box_rows, box_cols, turned, planes):
    box_y = lax.axis_index("box") // box_cols
    low_open = jnp.where(box_y > 0, 1.0, 0.0).astype(F32)
    high_open = jnp.where(box_y < box_rows - 1, 1.0, 0.0).astype(F32)
    for y in range(rows_of(box_rows)):
        clear = pl.ds(y * XPOS + SIDE, SIDE) if y < SIDE else pl.ds(y * XPOS, XPOS)
        for plane in range(COEFS):
            planes[plane, clear, :] = jnp.zeros((SIDE if y < SIDE else XPOS, LANES), F32)
        if y >= SIDE:
            continue
        values = [turned[plane, pl.ds(y * SIDE, SIDE), :] for plane in range(COEFS)]
        weights = normal(values)
        if y == 0:
            weights[2] = weights[2] * low_open
        if y == SIDE - 1:
            weights[3] = weights[3] * high_open
        for plane, value in enumerate(weights + [turned[8, pl.ds(y * SIDE, SIDE), :]]):
            planes[plane, pl.ds(y * XPOS, SIDE), :] = value


def smooth_kernel(box_rows, box_cols, kinds, planes_in, *refs):
    pieces = dict(zip(kinds, refs[: len(kinds)], strict=True))
    groups, out, planes, result = refs[len(kinds) :]
    y_count = rows_of(box_rows)
    low_base = y_count - DEPTH
    group = lax.axis_index("grp")
    box_x = lax.axis_index("box") % box_cols
    box_y = lax.axis_index("box") // box_cols

    def place_y(rim, high):
        for i in range(DEPTH - 1):
            values = [
                rim[pl.ds((plane * (DEPTH - 1) + i) * SIDE, SIDE), :].astype(F32) for plane in range(COEFS)
            ]
            rows = pl.ds((SIDE + i if high else low_base + 1 + i) * XPOS, SIDE)
            for plane, value in enumerate(normal(values)):
                planes[plane, rows, :] = value
        for i in range(DEPTH):
            rows = pl.ds((SIDE + i if high else low_base + i) * XPOS, SIDE)
            planes[7, rows, :] = rim[pl.ds((COEFS * (DEPTH - 1) + i) * SIDE, SIDE), :].astype(F32)

    def place_x(rim, high):
        for i in range(DEPTH - 1):
            values = [
                rim[pl.ds((plane * (DEPTH - 1) + i) * SIDE, SIDE), :].astype(F32) for plane in range(COEFS)
            ]
            rows = pl.ds(SIDE + i if high else XPOS - DEPTH + 1 + i, SIDE, stride=XPOS)
            for plane, value in enumerate(normal(values)):
                planes[plane, rows, :] = value
        for i in range(DEPTH):
            rows = pl.ds(SIDE + i if high else XPOS - DEPTH + i, SIDE, stride=XPOS)
            planes[7, rows, :] = rim[pl.ds((COEFS * (DEPTH - 1) + i) * SIDE, SIDE), :].astype(F32)

    def place_corner(piece, high_y, high_x):
        cells = piece[...].astype(F32)
        found = {}
        for plane, dy, run, row in corner_runs():
            found[plane, dy] = cells[row : row + run, :]
        for dy in range(1, DEPTH):
            y = SIDE + dy - 1 if high_y else low_base + DEPTH - dy
            run = DEPTH - 1 - dy
            if run > 0:
                rows = pl.ds(y * XPOS + (SIDE if high_x else XPOS - run), run)
                for plane, value in enumerate(normal([found[plane, dy] for plane in range(COEFS)])):
                    planes[plane, rows, :] = value
            rows = pl.ds(y * XPOS + (SIDE if high_x else XPOS - run - 1), run + 1)
            planes[7, rows, :] = found[COEFS, dy]

    for odd_x in (0, 1):

        @pl.when(box_x % 2 == odd_x)
        def _():
            place_x(pieces[None, 0], odd_x == 0)
            place_x(pieces[None, 1], odd_x == 1)

    for odd_y in (0, 1):

        @pl.when(box_y % 2 == odd_y)
        def _():
            for (kind_y, kind_x), piece in pieces.items():
                if kind_x is None:
                    place_y(piece, odd_y == kind_y)

        for odd_x in (0, 1):

            @pl.when((box_y % 2 == odd_y) & (box_x % 2 == odd_x))
            def _():
                for (kind_y, kind_x), piece in pieces.items():
                    if None not in (kind_y, kind_x):
                        place_corner(piece, odd_y == kind_y, odd_x == kind_x)

    parity = (
        lax.broadcasted_iota(jnp.int32, (XPOS, LANES), 0) + lax.broadcasted_iota(jnp.int32, (XPOS, LANES), 1)
    ) % 2
    for sweep in range(SWEEPS):
        for colour in (0, 1):
            for y in range(y_count):
                rows = pl.ds(y * XPOS, XPOS)
                here = planes[7, rows, :]
                low = planes[7, pl.ds((y - 1) % y_count * XPOS, XPOS), :]
                high = planes[7, pl.ds((y + 1) % y_count * XPOS, XPOS), :]
                gathered = (
                    planes[6, rows, :]
                    + planes[0, rows, :] * pltpu.roll(here, 1, 1)
                    + planes[1, rows, :] * pltpu.roll(here, LANES - 1, 1)
                    + planes[2, rows, :] * low
                    + planes[3, rows, :] * high
                    + planes[4, rows, :] * pltpu.roll(here, 1, 0)
                    + planes[5, rows, :] * pltpu.roll(here, XPOS - 1, 0)
                )
                planes[7, rows, :] = jnp.where(parity == (colour + y) % 2, gathered, here)

    for half in range(2):
        pieces = [planes[7, pl.ds((half * 8 + y) * XPOS, SIDE), :] for y in range(8)]
        result[pl.ds(0, LANES), pl.ds(half * LANES, LANES)] = jnp.concatenate(pieces, axis=0).T
    count = jnp.int32(0)
    first = jnp.int32(0)
    for layer in range(groups.shape[0]):
        owner = groups[layer]
        count = count + jnp.where(owner == group, 1, 0)
        first = first + jnp.where(owner < group, 1, 0)
    start = pl.multiple_of(REACH + (first - group * LPD) * SIDE, 8)
    valid = lax.broadcasted_iota(jnp.int32, (OUT_ROWS, LANES), 0) < count * SIDE
    for half in range(2):
        value = result[pl.ds(start, OUT_ROWS), pl.ds(half * LANES, LANES)]
        out[pl.ds(half, OUT_ROWS, stride=2), :] = jnp.where(valid, value, 0.0)


def swaps(count, kind):
    pairs = []
    for low in range(kind, count - 1, 2):
        pairs += [(low, low + 1), (low + 1, low)]
    return pairs


def lateral_pairs(box_rows, box_cols, kind_y, kind_x):
    move_y = dict(swaps(box_rows, kind_y)) if kind_y is not None else {i: i for i in range(box_rows)}
    move_x = dict(swaps(box_cols, kind_x)) if kind_x is not None else {i: i for i in range(box_cols)}
    return [
        (y * box_cols + x, move_y[y] * box_cols + move_x[x])
        for y in range(box_rows)
        for x in range(box_cols)
        if y in move_y and x in move_x
    ]


def vmem(count):
    return [pl.BlockSpec(memory_space=pltpu.VMEM)] * count


def held(*arrays):
    return [pltpu.with_memory_space_constraint(array, pltpu.VMEM) for array in arrays]


def params():
    return pltpu.CompilerParams(vmem_limit_bytes=16 * 2**20)


def per_device(volume, apertures, conductivity, source, previous, cut_flags, new_group):
    group_count = lax.axis_size("grp")
    box_rows, box_cols = box_grid(lax.axis_size("box"))
    smem = pl.BlockSpec(memory_space=pltpu.SMEM)
    raw = (
        volume.reshape(ROWS, CELLS),
        apertures.reshape(6, ROWS, CELLS),
        conductivity.reshape(ROWS, CELLS),
        source.reshape(2 * ROWS, LANES),
        previous.reshape(2 * ROWS, LANES),
        cut_flags.T,
    )
    send_a, send_b = pl.pallas_call(
        pack_kernel,
        out_shape=[pltpu.VMEM((12, REACH, CELLS), BF16)] * 2,
        in_specs=vmem(5) + [smem],
        out_specs=vmem(2),
        compiler_params=params(),
        name="pack",
    )(*raw)
    from_a = lax.ppermute(send_a, "grp", swaps(group_count, 0))
    from_b = lax.ppermute(send_b, "grp", swaps(group_count, 1))
    own = pl.pallas_call(
        own_kernel,
        out_shape=pltpu.VMEM((9, ROWS, CELLS), F32),
        in_specs=vmem(5) + [smem],
        out_specs=vmem(1)[0],
        compiler_params=params(),
        cost_estimate=pl.CostEstimate(flops=4 * 2**20, bytes_accessed=2**20, transcendentals=0),
        name="own",
    )(*raw)

    kinds_y = [0] if box_rows == 2 else [0, 1]
    kinds = [(kind, None) for kind in kinds_y] + [(None, 0), (None, 1)]
    kinds += [(kind_y, kind_x) for kind_y in kinds_y for kind_x in (0, 1)]
    shapes = [pltpu.VMEM((RIM if None in kind else CORNER, LANES), BF16) for kind in kinds]
    turned, *sends = pl.pallas_call(
        lambda *refs: turn_kernel(box_rows, box_cols, *refs),
        out_shape=[pltpu.VMEM((9, CELLS, LANES), F32)] + shapes[: len(kinds_y)],
        in_specs=vmem(3),
        out_specs=vmem(1 + len(kinds_y)),
        scratch_shapes=[pltpu.VMEM((LANES, CELLS), F32)],
        compiler_params=params(),
        name="turn",
    )(*held(own, from_a, from_b))
    sends += pl.pallas_call(
        lambda *refs: rims_kernel(box_rows, box_cols, *refs),
        out_shape=shapes[len(kinds_y) :],
        in_specs=vmem(1),
        out_specs=vmem(len(shapes) - len(kinds_y)),
        scratch_shapes=[pltpu.VMEM((CORNER, LANES), F32)],
        compiler_params=params(),
        cost_estimate=pl.CostEstimate(flops=2**20, bytes_accessed=2**20, transcendentals=0),
        name="rims",
    )(*held(turned))
    arrived = [
        lax.ppermute(send, "box", lateral_pairs(box_rows, box_cols, *kind))
        for send, kind in zip(sends, kinds, strict=True)
    ]
    planes_shape = (COEFS, rows_of(box_rows) * XPOS, LANES)
    planes = pl.pallas_call(
        lambda *refs: prepare_kernel(box_rows, box_cols, *refs),
        out_shape=pltpu.VMEM(planes_shape, F32),
        in_specs=vmem(1),
        out_specs=vmem(1)[0],
        compiler_params=params(),
        cost_estimate=pl.CostEstimate(flops=8 * 2**20, bytes_accessed=2**20, transcendentals=0),
        name="prepare",
    )(*held(turned))
    smoothed, _ = pl.pallas_call(
        lambda *refs: smooth_kernel(box_rows, box_cols, kinds, *refs),
        out_shape=[
            jax.ShapeDtypeStruct((2 * OUT_ROWS, LANES), F32),
            pltpu.VMEM(planes_shape, F32),
        ],
        in_specs=vmem(1 + len(kinds)) + [smem],
        out_specs=vmem(2),
        scratch_shapes=[pltpu.VMEM((REACH + SIDE + OUT_ROWS, CELLS), F32)],
        input_output_aliases={0: 1},
        compiler_params=params(),
        name="smooth",
    )(*held(planes, *arrived), new_group)
    return smoothed.reshape(OUT_ROWS, 1, CELLS)


def solution(mesh):
    in_specs = (
        P("grp", "box", None),
        P(None, "grp", "box", None),
        P("grp", "box", None),
        P("grp", "box", None),
        P("grp", "box", None),
        P(),
        P(),
    )
    out_specs = P("grp", "box", None)
    return jax.shard_map(
        per_device, mesh=mesh, in_specs=in_specs, out_specs=out_specs, check_vma=False
    )
```

time: 37.4 us -> 33.5 us (0.90)
  the two profiles are of different devices: /device:TPU:2 before, /device:TPU:5 now
where the time goes in v2:
time: 33.5 us; the launch traced here: 32.9 us
  starting transfers between devices  14.1 us (42%)
  waiting for transfers between devices  8.18 us (24%)
  Pallas kernels  5.78 us (17%)
  local copies, waits for them, and re-layouts  4.81 us (14%)
    ppermute x5, starting transfers between devices, per_device(): lax.ppermute(send, 'box', lateral_pairs(box_rows, box_cols, *kind))  10.9 us
    unnamed x14, local copies, waits for them, and re-layouts  4.81 us
    ppermute x1, waiting for transfers between devices, per_device(): from_b = lax.ppermute(send_b, 'grp', swaps(group_count, 1))  3.67 us
    ppermute x5, waiting for transfers between devices, per_device(): lax.ppermute(send, 'box', lateral_pairs(box_rows, box_cols, *kind))  3.62 us
    pallas_call x1, Pallas kernels, per_device(): pl.pallas_call(lambda *refs: smooth_kernel(box_rows, box_cols, kinds, *re...  3.54 us
    ppermute x1, starting transfers between devices, per_device(): from_b = lax.ppermute(send_b, 'grp', swaps(group_count, 1))  1.91 us
    ppermute x1, starting transfers between devices, per_device(): from_a = lax.ppermute(send_a, 'grp', swaps(group_count, 0))  1.27 us
    ppermute x1, waiting for transfers between devices, per_device(): from_a = lax.ppermute(send_a, 'grp', swaps(group_count, 0))  0.89 us
  transfers between devices with their start and end apart: 7, of which 4 were waited for; matrix products, arithmetic and copies ran while one was open for 0% of the time, Pallas kernels for 4%

profile of v2, /device:TPU:5, one launch (start us, length us, event | category | flops | bytes accessed | tf_op | source)
XLA Modules:
  0.0 32.9 jit_solution(4508227010690523058)
XLA Ops:
  0.0 0.0 copy-start
  0.0 0.9 %copy-done = bf16[6,64,1,256]{3,1,2,0:T(8,128)(2,1)S(1)} copy-done((bf16[6,64,1,256]{3,1,2,0:T(8,128)(2,1)S(1)}, bf16[6,64,1,256]{3,1,2,0:T(8,128)(2,1)}, u32[]{:S(2)}) %copy-start) | copy-done | bytes 196632
  0.9 0.0 copy-start.1
  0.9 0.8 %copy-done.1 = f32[64,1,256]{2,1,0:T(1,128)S(1)} copy-done((f32[64,1,256]{2,1,0:T(1,128)S(1)}, f32[64,1,256]{2,1,0:T(1,128)}, u32[]{:S(2)}) %copy-start.1) | copy-done | bytes 65560
  1.8 0.0 copy-start.2
  1.8 0.8 %copy-done.2 = f32[64,1,256]{2,1,0:T(1,128)S(1)} copy-done((f32[64,1,256]{2,1,0:T(1,128)S(1)}, f32[64,1,256]{2,1,0:T(1,128)}, u32[]{:S(2)}) %copy-start.2) | copy-done | bytes 65560
  2.6 0.0 copy-start.3
  2.6 0.8 %copy-done.3 = bf16[64,1,256]{2,0,1:T(8,128)(2,1)S(1)} copy-done((bf16[64,1,256]{2,0,1:T(8,128)(2,1)S(1)}, bf16[64,1,256]{2,0,1:T(8,128)(2,1)}, u32[]{:S(2)}) %copy-start.3) | copy-done | bytes 32792
  3.4 0.0 copy-start.4
  3.4 0.8 %copy-done.4 = bf16[64,1,256]{2,0,1:T(8,128)(2,1)S(1)} copy-done((bf16[64,1,256]{2,0,1:T(8,128)(2,1)S(1)}, bf16[64,1,256]{2,0,1:T(8,128)(2,1)}, u32[]{:S(2)}) %copy-start.4) | copy-done | bytes 32792
  4.1 0.0 copy-start.5
  4.1 0.7 %copy-done.5 = s32[16,8]{0,1:T(8,128)S(1)} copy-done((s32[16,8]{0,1:T(8,128)S(1)}, s32[16,8]{0,1:T(8,128)}, u32[]{:S(2)}) %copy-start.5) | copy-done | bytes 536
  4.8 0.7 %pack.1 = (bf16[12,24,256]{2,1,0:T(8,128)(2,1)S(1)}, bf16[12,24,256]{2,1,0:T(8,128)(2,1)S(1)}) custom-call(bf16[64,256]{1,0:T(8,128)(2,1)S(1)} %bitcast.13, bf16[6,64,256]{2,1,0:T(8,128)(2,1)S(1)} %bitcast.7, bf16[64,256]{1,0:T(8,128)(2,1)S(1)} %bitcast.15, f32[128,128]{1,0:T(8,128)S(1)} %bitcast.9, f32[128,128]{1,0:T(8,128)S(1)} %bitcast.11, ...), custom_call_target="tpu_custom_call" | custom-call | tf_op jit(solution)/shard_map/pack/pallas_call | solution.py:360
  5.5 1.3 %collective-permute-start = (bf16[12,24,256]{2,1,0:T(8,128)(2,1)S(1)}, bf16[12,24,256]{2,1,0:T(8,128)(2,1)S(1)}, u32[]{:S(2)}, u32[]{:S(2)}) collective-permute-start(bf16[12,24,256]{2,1,0:T(8,128)(2,1)S(1)} %get-tuple-element.14), channel_id=1, source_target_pairs={{0,8},{8,0},{16,24},{24,16},{1,9},{9,1},{17,25},{25,17},{2,10},{10... | collective-permute-start | bytes 442376 | tf_op jit(solution)/shard_map/ppermute | solution.py:368
  6.8 1.9 %collective-permute-start.1 = (bf16[12,24,256]{2,1,0:T(8,128)(2,1)S(1)}, bf16[12,24,256]{2,1,0:T(8,128)(2,1)S(1)}, u32[]{:S(2)}, u32[]{:S(2)}) collective-permute-start(bf16[12,24,256]{2,1,0:T(8,128)(2,1)S(1)} %get-tuple-element.15), channel_id=1, source_target_pairs={{8,16},{16,8},{9,17},{17,9},{10,18},{18,10},{11,19},{19,11},{12,20... | collective-permute-start | bytes 442376 | tf_op jit(solution)/shard_map/ppermute | solution.py:369
  8.7 0.7 %own.1.refs_0_ = f32[9,64,256]{2,1,0:T(8,128)S(1)} custom-call(bf16[64,256]{1,0:T(8,128)(2,1)S(1)} %bitcast.14, bf16[6,64,256]{2,1,0:T(8,128)(2,1)S(1)} %bitcast.8, bf16[64,256]{1,0:T(8,128)(2,1)S(1)} %bitcast.16, f32[128,128]{1,0:T(8,128)S(1)} %bitcast.10, f32[128,128]{1,0:T(8,128)S(1)} %bitcast.12, s32[8,16]{1,0:T(8,128)S(1)} %bitcast.18), custom_call_target="tpu_custom_call" | custom-call | flops 4194304 | bytes 1048576 | tf_op jit(solution)/shard_map/own/pallas_call | solution.py:370
  9.4 0.0 copy-start.6
  9.4 0.9 %collective-permute-done.refs_1_ = bf16[12,24,256]{2,1,0:T(8,128)(2,1)S(1)} collective-permute-done((bf16[12,24,256]{2,1,0:T(8,128)(2,1)S(1)}, bf16[12,24,256]{2,1,0:T(8,128)(2,1)S(1)}, u32[]{:S(2)}, u32[]{:S(2)}) %collective-permute-start) | collective-permute-done | bytes 147488 | tf_op jit(solution)/shard_map/ppermute | solution.py:368
  10.3 3.7 %collective-permute-done.1.refs_2_ = bf16[12,24,256]{2,1,0:T(8,128)(2,1)S(1)} collective-permute-done((bf16[12,24,256]{2,1,0:T(8,128)(2,1)S(1)}, bf16[12,24,256]{2,1,0:T(8,128)(2,1)S(1)}, u32[]{:S(2)}, u32[]{:S(2)}) %collective-permute-start.1) | collective-permute-done | bytes 147488 | tf_op jit(solution)/shard_map/ppermute | solution.py:369
  14.0 0.4 %turn.1 = (f32[9,256,128]{2,1,0:T(8,128)S(1)}, bf16[736,128]{1,0:T(8,128)(2,1)S(1)}) custom-call(f32[9,64,256]{2,1,0:T(8,128)S(1)} %own.1.refs_0_, bf16[12,24,256]{2,1,0:T(8,128)(2,1)S(1)} %collective-permute-done.refs_1_, bf16[12,24,256]{2,1,0:T(8,128)(2,1)S(1)} %collective-permute-done.1.refs_2_), custom_call_target="tpu_custom_call" | custom-call | tf_op jit(solution)/shard_map/turn/pallas_call | solution.py:384
  14.4 2.4 %collective-permute-start.2 = (bf16[736,128]{1,0:T(8,128)(2,1)S(1)}, bf16[736,128]{1,0:T(8,128)(2,1)S(1)}, u32[]{:S(2)}, u32[]{:S(2)}) collective-permute-start(bf16[736,128]{1,0:T(8,128)(2,1)S(1)} %get-tuple-element.17), channel_id=1, source_target_pairs={{0,4},{1,5},{2,6},{3,7},{4,0},{5,1},{6,2},{7,3},{8,12},{9,13},{10,... | collective-permute-start | bytes 565256 | tf_op jit(solution)/shard_map/ppermute | solution.py:404
  16.8 0.3 rims.1
  17.0 2.2 %collective-permute-start.3 = (bf16[736,128]{1,0:T(8,128)(2,1)S(1)}, bf16[736,128]{1,0:T(8,128)(2,1)S(1)}, u32[]{:S(2)}, u32[]{:S(2)}) collective-permute-start(bf16[736,128]{1,0:T(8,128)(2,1)S(1)} %get-tuple-element.18), channel_id=1, source_target_pairs={{0,1},{1,0},{2,3},{3,2},{4,5},{5,4},{6,7},{7,6},{8,9},{9,8},{10,11... | collective-permute-start | bytes 565256 | tf_op jit(solution)/shard_map/ppermute | solution.py:404
  19.2 3.1 %collective-permute-start.4 = (bf16[736,128]{1,0:T(8,128)(2,1)S(1)}, bf16[736,128]{1,0:T(8,128)(2,1)S(1)}, u32[]{:S(2)}, u32[]{:S(2)}) collective-permute-start(bf16[736,128]{1,0:T(8,128)(2,1)S(1)} %get-tuple-element.19), channel_id=1, source_target_pairs={{1,2},{2,1},{5,6},{6,5},{9,10},{10,9},{13,14},{14,13},{17,18},{18,... | collective-permute-start | bytes 565256 | tf_op jit(solution)/shard_map/ppermute | solution.py:404
  22.4 0.1 collective-permute-start.5
  22.4 3.1 %collective-permute-start.6 = (bf16[96,128]{1,0:T(8,128)(2,1)S(1)}, bf16[96,128]{1,0:T(8,128)(2,1)S(1)}, u32[]{:S(2)}, u32[]{:S(2)}) collective-permute-start(bf16[96,128]{1,0:T(8,128)(2,1)S(1)} %get-tuple-element.21), channel_id=1, source_target_pairs={{1,6},{2,5},{5,2},{6,1},{9,14},{10,13},{13,10},{14,9},{17,22},{18,... | collective-permute-start | bytes 73736 | tf_op jit(solution)/shard_map/ppermute | solution.py:404
  25.5 0.2 prepare.1.refs_0_
  25.8 1.2 %collective-permute-done.5.refs_4_ = bf16[96,128]{1,0:T(8,128)(2,1)S(1)} collective-permute-done((bf16[96,128]{1,0:T(8,128)(2,1)S(1)}, bf16[96,128]{1,0:T(8,128)(2,1)S(1)}, u32[]{:S(2)}, u32[]{:S(2)}) %collective-permute-start.5) | collective-permute-done | bytes 24608 | tf_op jit(solution)/shard_map/ppermute | solution.py:404
  27.0 2.4 %collective-permute-done.6.refs_5_ = bf16[96,128]{1,0:T(8,128)(2,1)S(1)} collective-permute-done((bf16[96,128]{1,0:T(8,128)(2,1)S(1)}, bf16[96,128]{1,0:T(8,128)(2,1)S(1)}, u32[]{:S(2)}, u32[]{:S(2)}) %collective-permute-start.6) | collective-permute-done | bytes 24608 | tf_op jit(solution)/shard_map/ppermute | solution.py:404
  29.4 0.0 collective-permute-done.2.refs_1_
  29.4 0.0 collective-permute-done.3.refs_2_
  29.4 0.0 collective-permute-done.4.refs_3_
  29.4 0.0 copy-done.6
  29.4 3.5 %smooth.1 = (f32[192,128]{1,0:T(8,128)}, f32[8,704,128]{2,1,0:T(8,128)S(1)}) custom-call(f32[8,704,128]{2,1,0:T(8,128)S(1)} %prepare.1.refs_0_, bf16[736,128]{1,0:T(8,128)(2,1)S(1)} %collective-permute-done.2.refs_1_, bf16[736,128]{1,0:T(8,128)(2,1)S(1)} %collective-permute-done.3.refs_2_, ...), custom_call_target="tpu_custom_call", output_to_operand_aliasing={{1}: (0, {})} | custom-call | tf_op jit(solution)/shard_map/smooth/pallas_call | solution.py:417
Async XLA Ops:
  0.0 0.9 %copy-start = (bf16[6,64,1,256]{3,1,2,0:T(8,128)(2,1)S(1)}, bf16[6,64,1,256]{3,1,2,0:T(8,128)(2,1)}, u32[]{:S(2)}) copy-start(bf16[6,64,1,256]{3,1,2,0:T(8,128)(2,1)} %param.8) | copy-start | bytes 589828
  0.9 0.8 %copy-start.1 = (f32[64,1,256]{2,1,0:T(1,128)S(1)}, f32[64,1,256]{2,1,0:T(1,128)}, u32[]{:S(2)}) copy-start(f32[64,1,256]{2,1,0:T(1,128)} %param.10) | copy-start | bytes 196612
  1.8 0.8 %copy-start.2 = (f32[64,1,256]{2,1,0:T(1,128)S(1)}, f32[64,1,256]{2,1,0:T(1,128)}, u32[]{:S(2)}) copy-start(f32[64,1,256]{2,1,0:T(1,128)} %param.11) | copy-start | bytes 196612
  2.6 0.8 %copy-start.3 = (bf16[64,1,256]{2,0,1:T(8,128)(2,1)S(1)}, bf16[64,1,256]{2,0,1:T(8,128)(2,1)}, u32[]{:S(2)}) copy-start(bf16[64,1,256]{2,0,1:T(8,128)(2,1)} %param.7) | copy-start | bytes 98308
  3.4 0.8 %copy-start.4 = (bf16[64,1,256]{2,0,1:T(8,128)(2,1)S(1)}, bf16[64,1,256]{2,0,1:T(8,128)(2,1)}, u32[]{:S(2)}) copy-start(bf16[64,1,256]{2,0,1:T(8,128)(2,1)} %param.9) | copy-start | bytes 98308
  4.1 0.7 %copy-start.5 = (s32[16,8]{0,1:T(8,128)S(1)}, s32[16,8]{0,1:T(8,128)}, u32[]{:S(2)}) copy-start(s32[16,8]{0,1:T(8,128)} %param.12) | copy-start | bytes 1540
  5.5 4.8 %collective-permute-start = (bf16[12,24,256]{2,1,0:T(8,128)(2,1)S(1)}, bf16[12,24,256]{2,1,0:T(8,128)(2,1)S(1)}, u32[]{:S(2)}, u32[]{:S(2)}) collective-permute-start(bf16[12,24,256]{2,1,0:T(8,128)(2,1)S(1)} %get-tuple-element.14), channel_id=1, source_target_pairs={{0,8},{8,0},{16,24},{24,16},{1,9},{9,1},{17,25},{25,17},{2,10},{10... | collective-permute-start | bytes 442376 | tf_op jit(solution)/shard_map/ppermute | solution.py:368
  6.8 7.2 %collective-permute-start.1 = (bf16[12,24,256]{2,1,0:T(8,128)(2,1)S(1)}, bf16[12,24,256]{2,1,0:T(8,128)(2,1)S(1)}, u32[]{:S(2)}, u32[]{:S(2)}) collective-permute-start(bf16[12,24,256]{2,1,0:T(8,128)(2,1)S(1)} %get-tuple-element.15), channel_id=1, source_target_pairs={{8,16},{16,8},{9,17},{17,9},{10,18},{18,10},{11,19},{19,11},{12,20... | collective-permute-start | bytes 442376 | tf_op jit(solution)/shard_map/ppermute | solution.py:369
  9.4 20.0 %copy-start.6 = (s32[16]{0:T(128)S(1)}, s32[16]{0:T(128)}, u32[]{:S(2)}) copy-start(s32[16]{0:T(128)} %refs_6_.1) | copy-start | bytes 196
  14.4 15.0 %collective-permute-start.2 = (bf16[736,128]{1,0:T(8,128)(2,1)S(1)}, bf16[736,128]{1,0:T(8,128)(2,1)S(1)}, u32[]{:S(2)}, u32[]{:S(2)}) collective-permute-start(bf16[736,128]{1,0:T(8,128)(2,1)S(1)} %get-tuple-element.17), channel_id=1, source_target_pairs={{0,4},{1,5},{2,6},{3,7},{4,0},{5,1},{6,2},{7,3},{8,12},{9,13},{10,... | collective-permute-start | bytes 565256 | tf_op jit(solution)/shard_map/ppermute | solution.py:404
  17.0 12.4 %collective-permute-start.3 = (bf16[736,128]{1,0:T(8,128)(2,1)S(1)}, bf16[736,128]{1,0:T(8,128)(2,1)S(1)}, u32[]{:S(2)}, u32[]{:S(2)}) collective-permute-start(bf16[736,128]{1,0:T(8,128)(2,1)S(1)} %get-tuple-element.18), channel_id=1, source_target_pairs={{0,1},{1,0},{2,3},{3,2},{4,5},{5,4},{6,7},{7,6},{8,9},{9,8},{10,11... | collective-permute-start | bytes 565256 | tf_op jit(solution)/shard_map/ppermute | solution.py:404
  19.2 10.1 %collective-permute-start.4 = (bf16[736,128]{1,0:T(8,128)(2,1)S(1)}, bf16[736,128]{1,0:T(8,128)(2,1)S(1)}, u32[]{:S(2)}, u32[]{:S(2)}) collective-permute-start(bf16[736,128]{1,0:T(8,128)(2,1)S(1)} %get-tuple-element.19), channel_id=1, source_target_pairs={{1,2},{2,1},{5,6},{6,5},{9,10},{10,9},{13,14},{14,13},{17,18},{18,... | collective-permute-start | bytes 565256 | tf_op jit(solution)/shard_map/ppermute | solution.py:404
  22.4 4.6 %collective-permute-start.5 = (bf16[96,128]{1,0:T(8,128)(2,1)S(1)}, bf16[96,128]{1,0:T(8,128)(2,1)S(1)}, u32[]{:S(2)}, u32[]{:S(2)}) collective-permute-start(bf16[96,128]{1,0:T(8,128)(2,1)S(1)} %get-tuple-element.20), channel_id=1, source_target_pairs={{0,5},{1,4},{2,7},{3,6},{4,1},{5,0},{6,3},{7,2},{8,13},{9,12},{10,... | collective-permute-start | bytes 73736 | tf_op jit(solution)/shard_map/ppermute | solution.py:404
  22.4 6.9 %collective-permute-start.6 = (bf16[96,128]{1,0:T(8,128)(2,1)S(1)}, bf16[96,128]{1,0:T(8,128)(2,1)S(1)}, u32[]{:S(2)}, u32[]{:S(2)}) collective-permute-start(bf16[96,128]{1,0:T(8,128)(2,1)S(1)} %get-tuple-element.21), channel_id=1, source_target_pairs={{1,6},{2,5},{5,2},{6,1},{9,14},{10,13},{13,10},{14,9},{17,22},{18,... | collective-permute-start | bytes 73736 | tf_op jit(solution)/shard_map/ppermute | solution.py:404

commit v3 on v2

--- a/solution.py
+++ b/solution.py
@@ -52,9 +52,19 @@
         put(8, cells, before)
 
 
-def pack_kernel(vol, ap, cond, src, prev, flags, send_a, send_b):
+def pack_kernel(*refs):
+    sources, (send_a, send_b), copies, semaphores = refs[:6], refs[6:8], refs[8:14], refs[14]
+    moves = [
+        pltpu.make_async_copy(source, copy, semaphores.at[index])
+        for index, (source, copy) in enumerate(zip(sources, copies, strict=True))
+    ]
+    for move in moves:
+        move.start()
+    vol, ap, cond, src, prev, flags = copies
     group = lax.axis_index("grp")
     column = lax.axis_index("box")
+    for move in moves:
+        move.wait()
 
     def emit(out, first):
         for layer in range(LPD):
@@ -357,14 +367,17 @@
         previous.reshape(2 * ROWS, LANES),
         cut_flags.T,
     )
-    send_a, send_b = pl.pallas_call(
+    send_a, send_b, *local = pl.pallas_call(
         pack_kernel,
-        out_shape=[pltpu.VMEM((12, REACH, CELLS), BF16)] * 2,
-        in_specs=vmem(5) + [smem],
-        out_specs=vmem(2),
+        out_shape=[pltpu.VMEM((12, REACH, CELLS), BF16)] * 2
+        + [pltpu.VMEM(array.shape, array.dtype) for array in raw[:-1]]
+        + [pltpu.SMEM(raw[-1].shape, raw[-1].dtype)],
+        in_specs=[pl.BlockSpec(memory_space=pltpu.HBM)] * 6,
+        out_specs=vmem(7) + [smem],
+        scratch_shapes=[pltpu.SemaphoreType.DMA((6,))],
         compiler_params=params(),
         name="pack",
-    )(*raw)
+    )(*[pltpu.with_memory_space_constraint(array, pltpu.HBM) for array in raw])
     from_a = lax.ppermute(send_a, "grp", swaps(group_count, 0))
     from_b = lax.ppermute(send_b, "grp", swaps(group_count, 1))
     own = pl.pallas_call(
@@ -375,7 +388,7 @@
         compiler_params=params(),
         cost_estimate=pl.CostEstimate(flops=4 * 2**20, bytes_accessed=2**20, transcendentals=0),
         name="own",
-    )(*raw)
+    )(*held(*local[:-1]), local[-1])
 
     kinds_y = [0] if box_rows == 2 else [0, 1]
     kinds = [(kind, None) for kind in kinds_y] + [(None, 0), (None, 1)]

time: 33.5 us -> 28.9 us (0.86)
  local copies, waits for them, and re-layouts: 4.81 us -> 0.01 us
  waiting for transfers between devices: 8.18 us -> 8.78 us
    unnamed x14 -> x2, local copies, waits for them, and re-layouts: 4.81 us -> 0.01 us
    pallas_call x1, Pallas kernels: 0.68 us -> 0.08 us  [per_device(): pl.pallas_call(own_kernel, out_shape=pltpu.VMEM((9, ROWS, CELLS), F32), i...]
    ppermute x1, waiting for transfers between devices: 0.89 us -> 1.49 us  [per_device(): from_a = lax.ppermute(send_a, 'grp', swaps(group_count, 0))]
    pallas_call x1, Pallas kernels: 0.7 us -> 1.15 us  [per_device(): pl.pallas_call(pack_kernel, out_shape=[pltpu.VMEM((12, REACH, CELLS), BF1...]
  transfers between devices with their start and end apart: 7 -> 7, of which waited for: 4 -> 4; matrix products, arithmetic and copies ran while one was open for 0% -> 0% of each run, Pallas kernels for 4% -> 2%
where the time goes in v3:
time: 28.9 us; the launch traced here: 28.6 us
  starting transfers between devices  14.1 us (49%)
  waiting for transfers between devices  8.78 us (30%)
  Pallas kernels  5.64 us (20%)
    ppermute x5, starting transfers between devices, per_device(): lax.ppermute(send, 'box', lateral_pairs(box_rows, box_cols, *kind))  10.9 us
    ppermute x1, waiting for transfers between devices, per_device(): from_b = lax.ppermute(send_b, 'grp', swaps(group_count, 1))  3.67 us
    ppermute x5, waiting for transfers between devices, per_device(): lax.ppermute(send, 'box', lateral_pairs(box_rows, box_cols, *kind))  3.62 us
    pallas_call x1, Pallas kernels, per_device(): pl.pallas_call(lambda *refs: smooth_kernel(box_rows, box_cols, kinds, *re...  3.54 us
    ppermute x1, starting transfers between devices, per_device(): from_b = lax.ppermute(send_b, 'grp', swaps(group_count, 1))  1.91 us
    ppermute x1, waiting for transfers between devices, per_device(): from_a = lax.ppermute(send_a, 'grp', swaps(group_count, 0))  1.49 us
    ppermute x1, starting transfers between devices, per_device(): from_a = lax.ppermute(send_a, 'grp', swaps(group_count, 0))  1.27 us
    pallas_call x1, Pallas kernels, per_device(): pl.pallas_call(pack_kernel, out_shape=[pltpu.VMEM((12, REACH, CELLS), BF1...  1.15 us
  transfers between devices with their start and end apart: 7, of which 4 were waited for; matrix products, arithmetic and copies ran while one was open for 0% of the time, Pallas kernels for 2%

profile of v3, /device:TPU:5, one launch (start us, length us, event | category | flops | bytes accessed | tf_op | source)
XLA Modules:
  0.0 28.6 jit_solution(7763987169012258222)
XLA Ops:
  0.0 1.2 %pack.1 = (bf16[12,24,256]{2,1,0:T(8,128)(2,1)S(1)}, bf16[12,24,256]{2,1,0:T(8,128)(2,1)S(1)}, bf16[64,256]{1,0:T(8,128)(2,1)S(1)}, bf16[6,64,256]{2,1,0:T(8,128...) custom-call(bf16[64,256]{1,0:T(8,128)(2,1)} %bitcast.10, ...), custom_call_target="tpu_custom_call" | custom-call | tf_op jit(solution)/shard_map/pack/pallas_call | solution.py:370
  1.2 1.3 %collective-permute-start = (bf16[12,24,256]{2,1,0:T(8,128)(2,1)S(1)}, bf16[12,24,256]{2,1,0:T(8,128)(2,1)S(1)}, u32[]{:S(2)}, u32[]{:S(2)}) collective-permute-start(bf16[12,24,256]{2,1,0:T(8,128)(2,1)S(1)} %get-tuple-element.26), channel_id=1, source_target_pairs={{0,8},{8,0},{16,24},{24,16},{1,9},{9,1},{17,25},{25,17},{2,10},{10... | collective-permute-start | bytes 442376 | tf_op jit(solution)/shard_map/ppermute | solution.py:381
  2.4 1.9 %collective-permute-start.1 = (bf16[12,24,256]{2,1,0:T(8,128)(2,1)S(1)}, bf16[12,24,256]{2,1,0:T(8,128)(2,1)S(1)}, u32[]{:S(2)}, u32[]{:S(2)}) collective-permute-start(bf16[12,24,256]{2,1,0:T(8,128)(2,1)S(1)} %get-tuple-element.27), channel_id=1, source_target_pairs={{8,16},{16,8},{9,17},{17,9},{10,18},{18,10},{11,19},{19,11},{12,20... | collective-permute-start | bytes 442376 | tf_op jit(solution)/shard_map/ppermute | solution.py:382
  4.3 0.1 own.1.refs_0_
  4.4 0.0 copy-start
  4.5 1.5 %collective-permute-done.refs_1_ = bf16[12,24,256]{2,1,0:T(8,128)(2,1)S(1)} collective-permute-done((bf16[12,24,256]{2,1,0:T(8,128)(2,1)S(1)}, bf16[12,24,256]{2,1,0:T(8,128)(2,1)S(1)}, u32[]{:S(2)}, u32[]{:S(2)}) %collective-permute-start) | collective-permute-done | bytes 147488 | tf_op jit(solution)/shard_map/ppermute | solution.py:381
  5.9 3.7 %collective-permute-done.1.refs_2_ = bf16[12,24,256]{2,1,0:T(8,128)(2,1)S(1)} collective-permute-done((bf16[12,24,256]{2,1,0:T(8,128)(2,1)S(1)}, bf16[12,24,256]{2,1,0:T(8,128)(2,1)S(1)}, u32[]{:S(2)}, u32[]{:S(2)}) %collective-permute-start.1) | collective-permute-done | bytes 147488 | tf_op jit(solution)/shard_map/ppermute | solution.py:382
  9.6 0.4 %turn.1 = (f32[9,256,128]{2,1,0:T(8,128)S(1)}, bf16[736,128]{1,0:T(8,128)(2,1)S(1)}) custom-call(f32[9,64,256]{2,1,0:T(8,128)S(1)} %own.1.refs_0_, bf16[12,24,256]{2,1,0:T(8,128)(2,1)S(1)} %collective-permute-done.refs_1_, bf16[12,24,256]{2,1,0:T(8,128)(2,1)S(1)} %collective-permute-done.1.refs_2_), custom_call_target="tpu_custom_call" | custom-call | tf_op jit(solution)/shard_map/turn/pallas_call | solution.py:397
  10.0 2.4 %collective-permute-start.2 = (bf16[736,128]{1,0:T(8,128)(2,1)S(1)}, bf16[736,128]{1,0:T(8,128)(2,1)S(1)}, u32[]{:S(2)}, u32[]{:S(2)}) collective-permute-start(bf16[736,128]{1,0:T(8,128)(2,1)S(1)} %get-tuple-element.29), channel_id=1, source_target_pairs={{0,4},{1,5},{2,6},{3,7},{4,0},{5,1},{6,2},{7,3},{8,12},{9,13},{10,... | collective-permute-start | bytes 565256 | tf_op jit(solution)/shard_map/ppermute | solution.py:417
  12.4 0.3 rims.1
  12.7 2.2 %collective-permute-start.3 = (bf16[736,128]{1,0:T(8,128)(2,1)S(1)}, bf16[736,128]{1,0:T(8,128)(2,1)S(1)}, u32[]{:S(2)}, u32[]{:S(2)}) collective-permute-start(bf16[736,128]{1,0:T(8,128)(2,1)S(1)} %get-tuple-element.30), channel_id=1, source_target_pairs={{0,1},{1,0},{2,3},{3,2},{4,5},{5,4},{6,7},{7,6},{8,9},{9,8},{10,11... | collective-permute-start | bytes 565256 | tf_op jit(solution)/shard_map/ppermute | solution.py:417
  14.9 3.1 %collective-permute-start.4 = (bf16[736,128]{1,0:T(8,128)(2,1)S(1)}, bf16[736,128]{1,0:T(8,128)(2,1)S(1)}, u32[]{:S(2)}, u32[]{:S(2)}) collective-permute-start(bf16[736,128]{1,0:T(8,128)(2,1)S(1)} %get-tuple-element.31), channel_id=1, source_target_pairs={{1,2},{2,1},{5,6},{6,5},{9,10},{10,9},{13,14},{14,13},{17,18},{18,... | collective-permute-start | bytes 565256 | tf_op jit(solution)/shard_map/ppermute | solution.py:417
  18.0 0.1 collective-permute-start.5
  18.1 3.1 %collective-permute-start.6 = (bf16[96,128]{1,0:T(8,128)(2,1)S(1)}, bf16[96,128]{1,0:T(8,128)(2,1)S(1)}, u32[]{:S(2)}, u32[]{:S(2)}) collective-permute-start(bf16[96,128]{1,0:T(8,128)(2,1)S(1)} %get-tuple-element.33), channel_id=1, source_target_pairs={{1,6},{2,5},{5,2},{6,1},{9,14},{10,13},{13,10},{14,9},{17,22},{18,... | collective-permute-start | bytes 73736 | tf_op jit(solution)/shard_map/ppermute | solution.py:417
  21.2 0.2 prepare.1.refs_0_
  21.4 1.2 %collective-permute-done.5.refs_4_ = bf16[96,128]{1,0:T(8,128)(2,1)S(1)} collective-permute-done((bf16[96,128]{1,0:T(8,128)(2,1)S(1)}, bf16[96,128]{1,0:T(8,128)(2,1)S(1)}, u32[]{:S(2)}, u32[]{:S(2)}) %collective-permute-start.5) | collective-permute-done | bytes 24608 | tf_op jit(solution)/shard_map/ppermute | solution.py:417
  22.6 2.4 %collective-permute-done.6.refs_5_ = bf16[96,128]{1,0:T(8,128)(2,1)S(1)} collective-permute-done((bf16[96,128]{1,0:T(8,128)(2,1)S(1)}, bf16[96,128]{1,0:T(8,128)(2,1)S(1)}, u32[]{:S(2)}, u32[]{:S(2)}) %collective-permute-start.6) | collective-permute-done | bytes 24608 | tf_op jit(solution)/shard_map/ppermute | solution.py:417
  25.0 0.0 collective-permute-done.2.refs_1_
  25.0 0.0 collective-permute-done.3.refs_2_
  25.0 0.0 collective-permute-done.4.refs_3_
  25.0 0.0 copy-done
  25.0 3.5 %smooth.1 = (f32[192,128]{1,0:T(8,128)}, f32[8,704,128]{2,1,0:T(8,128)S(1)}) custom-call(f32[8,704,128]{2,1,0:T(8,128)S(1)} %prepare.1.refs_0_, bf16[736,128]{1,0:T(8,128)(2,1)S(1)} %collective-permute-done.2.refs_1_, bf16[736,128]{1,0:T(8,128)(2,1)S(1)} %collective-permute-done.3.refs_2_, ...), custom_call_target="tpu_custom_call", output_to_operand_aliasing={{1}: (0, {})} | custom-call | tf_op jit(solution)/shard_map/smooth/pallas_call | solution.py:430
Async XLA Ops:
  1.2 4.8 %collective-permute-start = (bf16[12,24,256]{2,1,0:T(8,128)(2,1)S(1)}, bf16[12,24,256]{2,1,0:T(8,128)(2,1)S(1)}, u32[]{:S(2)}, u32[]{:S(2)}) collective-permute-start(bf16[12,24,256]{2,1,0:T(8,128)(2,1)S(1)} %get-tuple-element.26), channel_id=1, source_target_pairs={{0,8},{8,0},{16,24},{24,16},{1,9},{9,1},{17,25},{25,17},{2,10},{10... | collective-permute-start | bytes 442376 | tf_op jit(solution)/shard_map/ppermute | solution.py:381
  2.4 7.2 %collective-permute-start.1 = (bf16[12,24,256]{2,1,0:T(8,128)(2,1)S(1)}, bf16[12,24,256]{2,1,0:T(8,128)(2,1)S(1)}, u32[]{:S(2)}, u32[]{:S(2)}) collective-permute-start(bf16[12,24,256]{2,1,0:T(8,128)(2,1)S(1)} %get-tuple-element.27), channel_id=1, source_target_pairs={{8,16},{16,8},{9,17},{17,9},{10,18},{18,10},{11,19},{19,11},{12,20... | collective-permute-start | bytes 442376 | tf_op jit(solution)/shard_map/ppermute | solution.py:382
  4.4 20.6 %copy-start = (s32[16]{0:T(128)S(1)}, s32[16]{0:T(128)}, u32[]{:S(2)}) copy-start(s32[16]{0:T(128)} %refs_6_.1) | copy-start | bytes 196
  10.0 15.0 %collective-permute-start.2 = (bf16[736,128]{1,0:T(8,128)(2,1)S(1)}, bf16[736,128]{1,0:T(8,128)(2,1)S(1)}, u32[]{:S(2)}, u32[]{:S(2)}) collective-permute-start(bf16[736,128]{1,0:T(8,128)(2,1)S(1)} %get-tuple-element.29), channel_id=1, source_target_pairs={{0,4},{1,5},{2,6},{3,7},{4,0},{5,1},{6,2},{7,3},{8,12},{9,13},{10,... | collective-permute-start | bytes 565256 | tf_op jit(solution)/shard_map/ppermute | solution.py:417
  12.7 12.4 %collective-permute-start.3 = (bf16[736,128]{1,0:T(8,128)(2,1)S(1)}, bf16[736,128]{1,0:T(8,128)(2,1)S(1)}, u32[]{:S(2)}, u32[]{:S(2)}) collective-permute-start(bf16[736,128]{1,0:T(8,128)(2,1)S(1)} %get-tuple-element.30), channel_id=1, source_target_pairs={{0,1},{1,0},{2,3},{3,2},{4,5},{5,4},{6,7},{7,6},{8,9},{9,8},{10,11... | collective-permute-start | bytes 565256 | tf_op jit(solution)/shard_map/ppermute | solution.py:417
  14.9 10.1 %collective-permute-start.4 = (bf16[736,128]{1,0:T(8,128)(2,1)S(1)}, bf16[736,128]{1,0:T(8,128)(2,1)S(1)}, u32[]{:S(2)}, u32[]{:S(2)}) collective-permute-start(bf16[736,128]{1,0:T(8,128)(2,1)S(1)} %get-tuple-element.31), channel_id=1, source_target_pairs={{1,2},{2,1},{5,6},{6,5},{9,10},{10,9},{13,14},{14,13},{17,18},{18,... | collective-permute-start | bytes 565256 | tf_op jit(solution)/shard_map/ppermute | solution.py:417
  18.0 4.6 %collective-permute-start.5 = (bf16[96,128]{1,0:T(8,128)(2,1)S(1)}, bf16[96,128]{1,0:T(8,128)(2,1)S(1)}, u32[]{:S(2)}, u32[]{:S(2)}) collective-permute-start(bf16[96,128]{1,0:T(8,128)(2,1)S(1)} %get-tuple-element.32), channel_id=1, source_target_pairs={{0,5},{1,4},{2,7},{3,6},{4,1},{5,0},{6,3},{7,2},{8,13},{9,12},{10,... | collective-permute-start | bytes 73736 | tf_op jit(solution)/shard_map/ppermute | solution.py:417
  18.1 6.9 %collective-permute-start.6 = (bf16[96,128]{1,0:T(8,128)(2,1)S(1)}, bf16[96,128]{1,0:T(8,128)(2,1)S(1)}, u32[]{:S(2)}, u32[]{:S(2)}) collective-permute-start(bf16[96,128]{1,0:T(8,128)(2,1)S(1)} %get-tuple-element.33), channel_id=1, source_target_pairs={{1,6},{2,5},{5,2},{6,1},{9,14},{10,13},{13,10},{14,9},{17,22},{18,... | collective-permute-start | bytes 73736 | tf_op jit(solution)/shard_map/ppermute | solution.py:417

commit v4 on v3

--- a/solution.py
+++ b/solution.py
@@ -18,7 +18,7 @@
 XPOS = 32
 COEFS = 8
 RIM = COEFS * (DEPTH - 1) * SIDE + DEPTH * SIDE
-CORNER = 96
+CORNER = 120
 F32 = jnp.float32
 BF16 = jnp.bfloat16
 
@@ -74,11 +74,10 @@
             rows = pl.ds(low - first, high - low)
 
             def put(plane, cells, value, rows=rows):
-                if plane < 6:
+                if plane == 7:
+                    out[7, rows, cells], out[9, rows, cells] = split(value)
+                else:
                     out[plane, rows, cells] = value.astype(BF16)
-                else:
-                    at = 6 + 2 * (plane - 6)
-                    out[at, rows, cells], out[at + 1, rows, cells] = split(value)
 
             cell_planes(low, high - low, flags[column, group * LPD + layer], vol, ap, cond, src, prev, put)
 
@@ -106,9 +105,11 @@
     row = 0
     for plane in range(COEFS + 1):
         reach = DEPTH - 1 if plane < COEFS else DEPTH
-        for dy in range(1, reach):
-            runs.append((plane, dy, reach - dy, row))
-            row += reach - dy
+        for dy in range(1, DEPTH):
+            run = reach - (dy + 1) // 2 * 2 + 1
+            if run > 0:
+                runs.append((plane, dy, run, row))
+                row += run
     return runs
 
 
@@ -119,13 +120,11 @@
     used = REACH + ROWS + REACH
     stage[pl.ds(used, LANES - used), :] = jnp.zeros((LANES - used, CELLS), F32)
     for plane in range(9):
-        if plane < 6:
-            a = from_a[plane, :, :].astype(F32)
-            b = from_b[plane, :, :].astype(F32)
-        else:
-            at = 6 + 2 * (plane - 6)
-            a = from_a[at, :, :].astype(F32) + from_a[at + 1, :, :].astype(F32)
-            b = from_b[at, :, :].astype(F32) + from_b[at + 1, :, :].astype(F32)
+        a = from_a[plane, :, :].astype(F32)
+        b = from_b[plane, :, :].astype(F32)
+        if plane == 7:
+            a = a + from_a[9, :, :].astype(F32)
+            b = b + from_b[9, :, :].astype(F32)
         stage[pl.ds(0, REACH), :] = jnp.where(even_group, b, a)
         stage[pl.ds(REACH, ROWS), :] = own[plane, :, :]
         stage[pl.ds(REACH + ROWS, REACH), :] = jnp.where(even_group, a, b)
@@ -158,16 +157,16 @@
             reach = DEPTH - 1 if plane < COEFS else DEPTH
             for i in range(reach):
                 x = SIDE - reach + i if high else i
-                out[pl.ds((plane * (DEPTH - 1) + i) * SIDE, SIDE), :] = turned[
-                    plane, pl.ds(x, SIDE, stride=SIDE), :
-                ].astype(BF16)
+                pair = [turned[plane, pl.ds(x + odd * SIDE, SIDE // 2, stride=2 * SIDE), :] for odd in (0, 1)]
+                out[pl.ds((plane * (DEPTH - 1) + i) * SIDE, SIDE), :] = jnp.concatenate(pair, axis=0).astype(BF16)
 
     def corner(out, high_y, high_x):
         for plane, dy, run, row in corner_runs():
             y = SIDE - dy if high_y else dy - 1
             x = SIDE - run if high_x else 0
             stage[pl.ds(row, run), :] = turned[plane, pl.ds(y * SIDE + x, run), :]
-        stage[pl.ds(CORNER - 1, 1), :] = jnp.zeros((1, LANES), F32)
+        used = corner_runs()[-1][2] + corner_runs()[-1][3]
+        stage[pl.ds(used, CORNER - used), :] = jnp.zeros((CORNER - used, LANES), F32)
         out[...] = stage[...].astype(BF16)
 
     for odd_x in (0, 1):
@@ -197,73 +196,109 @@
     return SIDE + DEPTH * (1 if box_rows == 2 else 2)
 
 
+def pairs_of(box_rows):
+    return rows_of(box_rows) // 2
+
+
+def odd_cells(count, first_x):
+    shape = (count, LANES)
+    cells = lax.broadcasted_iota(jnp.int32, shape, 0) + lax.broadcasted_iota(jnp.int32, shape, 1)
+    return (cells + first_x) % 2 == 1
+
+
+def odd_lanes(count, x):
+    return (lax.broadcasted_iota(jnp.int32, (count, LANES), 1) + x) % 2 == 1
+
+
+def put_pair(planes, plane, rows, odd, low, high):
+    planes[0, plane, rows, :] = jnp.where(odd, high, low)
+    planes[1, plane, rows, :] = jnp.where(odd, low, high)
+
+
 def prepare_kernel(box_rows, box_cols, turned, planes):
     box_y = lax.axis_index("box") // box_cols
     low_open = jnp.where(box_y > 0, 1.0, 0.0).astype(F32)
     high_open = jnp.where(box_y < box_rows - 1, 1.0, 0.0).astype(F32)
-    for y in range(rows_of(box_rows)):
-        clear = pl.ds(y * XPOS + SIDE, SIDE) if y < SIDE else pl.ds(y * XPOS, XPOS)
-        for plane in range(COEFS):
-            planes[plane, clear, :] = jnp.zeros((SIDE if y < SIDE else XPOS, LANES), F32)
-        if y >= SIDE:
-            continue
-        values = [turned[plane, pl.ds(y * SIDE, SIDE), :] for plane in range(COEFS)]
-        weights = normal(values)
+    odd = odd_cells(SIDE, 0)
+
+    def weights_at(y):
+        weights = normal([turned[plane, pl.ds(y * SIDE, SIDE), :] for plane in range(COEFS)])
         if y == 0:
             weights[2] = weights[2] * low_open
         if y == SIDE - 1:
             weights[3] = weights[3] * high_open
-        for plane, value in enumerate(weights + [turned[8, pl.ds(y * SIDE, SIDE), :]]):
-            planes[plane, pl.ds(y * XPOS, SIDE), :] = value
+        return weights + [turned[8, pl.ds(y * SIDE, SIDE), :]]
+
+    for k in range(pairs_of(box_rows)):
+        own = 2 * k < SIDE
+        clear = pl.ds(k * XPOS + SIDE, SIDE) if own else pl.ds(k * XPOS, XPOS)
+        for colour in (0, 1):
+            for plane in range(COEFS):
+                planes[colour, plane, clear, :] = jnp.zeros((SIDE if own else XPOS, LANES), F32)
+        if own:
+            for plane, (low, high) in enumerate(zip(weights_at(2 * k), weights_at(2 * k + 1), strict=True)):
+                put_pair(planes, plane, pl.ds(k * XPOS, SIDE), odd, low, high)
 
 
 def smooth_kernel(box_rows, box_cols, kinds, planes_in, *refs):
     pieces = dict(zip(kinds, refs[: len(kinds)], strict=True))
     groups, out, planes, result = refs[len(kinds) :]
-    y_count = rows_of(box_rows)
-    low_base = y_count - DEPTH
+    pair_count = pairs_of(box_rows)
+    low_pair = pair_count - DEPTH // 2
+    high_pair = SIDE // 2
     group = lax.axis_index("grp")
     box_x = lax.axis_index("box") % box_cols
     box_y = lax.axis_index("box") // box_cols
 
+    def slab(rim, index):
+        return rim[pl.ds(index * SIDE, SIDE), :].astype(F32)
+
     def place_y(rim, high):
-        for i in range(DEPTH - 1):
-            values = [
-                rim[pl.ds((plane * (DEPTH - 1) + i) * SIDE, SIDE), :].astype(F32) for plane in range(COEFS)
-            ]
-            rows = pl.ds((SIDE + i if high else low_base + 1 + i) * XPOS, SIDE)
-            for plane, value in enumerate(normal(values)):
-                planes[plane, rows, :] = value
+        odd = odd_cells(SIDE, 0)
+        empty = jnp.zeros((SIDE, LANES), F32)
+
+        def weights_at(i):
+            i = i if high else i - 1
+            if not 0 <= i < DEPTH - 1:
+                return [empty] * (COEFS - 1)
+            return normal([slab(rim, plane * (DEPTH - 1) + i) for plane in range(COEFS)])
+
+        for j in range(DEPTH // 2):
+            rows = pl.ds(((high_pair if high else low_pair) + j) * XPOS, SIDE)
+            two = [weights_at(2 * j + i) + [slab(rim, COEFS * (DEPTH - 1) + 2 * j + i)] for i in (0, 1)]
+            for plane, (low_value, high_value) in enumerate(zip(*two, strict=True)):
+                put_pair(planes, plane, rows, odd, low_value, high_value)
+
+    def place_x(rim, high):
+        half = SIDE // 2
         for i in range(DEPTH):
-            rows = pl.ds((SIDE + i if high else low_base + i) * XPOS, SIDE)
-            planes[7, rows, :] = rim[pl.ds((COEFS * (DEPTH - 1) + i) * SIDE, SIDE), :].astype(F32)
-
-    def place_x(rim, high):
-        for i in range(DEPTH - 1):
-            values = [
-                rim[pl.ds((plane * (DEPTH - 1) + i) * SIDE, SIDE), :].astype(F32) for plane in range(COEFS)
-            ]
-            rows = pl.ds(SIDE + i if high else XPOS - DEPTH + 1 + i, SIDE, stride=XPOS)
-            for plane, value in enumerate(normal(values)):
-                planes[plane, rows, :] = value
-        for i in range(DEPTH):
-            rows = pl.ds(SIDE + i if high else XPOS - DEPTH + i, SIDE, stride=XPOS)
-            planes[7, rows, :] = rim[pl.ds((COEFS * (DEPTH - 1) + i) * SIDE, SIDE), :].astype(F32)
+            x = SIDE + i if high else XPOS - DEPTH + i
+            at = i if high else i - 1
+            rows = pl.ds(x, half, stride=XPOS)
+            odd = odd_lanes(half, x)
+            if 0 <= at < DEPTH - 1:
+                for plane, value in enumerate(normal([slab(rim, plane * (DEPTH - 1) + at) for plane in range(COEFS)])):
+                    put_pair(planes, plane, rows, odd, value[:half], value[half:])
+            value = slab(rim, COEFS * (DEPTH - 1) + i)
+            put_pair(planes, 7, rows, odd, value[:half], value[half:])
 
     def place_corner(piece, high_y, high_x):
         cells = piece[...].astype(F32)
-        found = {}
-        for plane, dy, run, row in corner_runs():
-            found[plane, dy] = cells[row : row + run, :]
-        for dy in range(1, DEPTH):
-            y = SIDE + dy - 1 if high_y else low_base + DEPTH - dy
-            run = DEPTH - 1 - dy
-            if run > 0:
-                rows = pl.ds(y * XPOS + (SIDE if high_x else XPOS - run), run)
-                for plane, value in enumerate(normal([found[plane, dy] for plane in range(COEFS)])):
-                    planes[plane, rows, :] = value
-            rows = pl.ds(y * XPOS + (SIDE if high_x else XPOS - run - 1), run + 1)
-            planes[7, rows, :] = found[COEFS, dy]
+        found = {(plane, dy): cells[row : row + run, :] for plane, dy, run, row in corner_runs()}
+        for j in range(DEPTH // 2):
+            k = (high_pair + j if high_y else low_pair + DEPTH // 2 - 1 - j) * XPOS
+            near = [2 * j + 1, 2 * j + 2] if high_y else [2 * j + 2, 2 * j + 1]
+            groups_of = []
+            if (0, near[0]) in found:
+                two = [normal([found[plane, dy] for plane in range(COEFS)]) for dy in near]
+                groups_of += [(plane, low, high) for plane, (low, high) in enumerate(zip(*two, strict=True))]
+            if (COEFS, 2 * j + 1) in found:
+                pair = [found.get((COEFS, dy), jnp.zeros_like(found[COEFS, 2 * j + 1])) for dy in near]
+                groups_of.append((7, *pair))
+            for plane, low, high in groups_of:
+                run = low.shape[0]
+                x = SIDE if high_x else XPOS - run
+                put_pair(planes, plane, pl.ds(k + x, run), odd_cells(run, x), low, high)
 
     for odd_x in (0, 1):
 
@@ -288,30 +323,54 @@
                     if None not in (kind_y, kind_x):
                         place_corner(piece, odd_y == kind_y, odd_x == kind_x)
 
-    parity = (
-        lax.broadcasted_iota(jnp.int32, (XPOS, LANES), 0) + lax.broadcasted_iota(jnp.int32, (XPOS, LANES), 1)
-    ) % 2
-    for sweep in range(SWEEPS):
-        for colour in (0, 1):
-            for y in range(y_count):
-                rows = pl.ds(y * XPOS, XPOS)
-                here = planes[7, rows, :]
-                low = planes[7, pl.ds((y - 1) % y_count * XPOS, XPOS), :]
-                high = planes[7, pl.ds((y + 1) % y_count * XPOS, XPOS), :]
-                gathered = (
-                    planes[6, rows, :]
-                    + planes[0, rows, :] * pltpu.roll(here, 1, 1)
-                    + planes[1, rows, :] * pltpu.roll(here, LANES - 1, 1)
-                    + planes[2, rows, :] * low
-                    + planes[3, rows, :] * high
-                    + planes[4, rows, :] * pltpu.roll(here, 1, 0)
-                    + planes[5, rows, :] * pltpu.roll(here, XPOS - 1, 0)
-                )
-                planes[7, rows, :] = jnp.where(parity == (colour + y) % 2, gathered, here)
-
+    odd = odd_cells(XPOS, 0)
+
+    def update(colour, k):
+        def at(offset):
+            if isinstance(k, int):
+                return pl.ds((k + offset) % pair_count * XPOS, XPOS)
+            return pl.ds(pl.multiple_of(lax.rem(k + (offset + pair_count), pair_count) * XPOS, XPOS), XPOS)
+
+        here = planes[1 - colour, 7, at(0), :]
+        below = planes[1 - colour, 7, at(-1), :]
+        above = planes[1 - colour, 7, at(1), :]
+        if colour == 0:
+            low, high = jnp.where(odd, here, below), jnp.where(odd, above, here)
+        else:
+            low, high = jnp.where(odd, below, here), jnp.where(odd, here, above)
+        adjacent = (
+            pltpu.roll(here, 1, 1),
+            pltpu.roll(here, LANES - 1, 1),
+            low,
+            high,
+            pltpu.roll(here, 1, 0),
+            pltpu.roll(here, XPOS - 1, 0),
+        )
+        gathered = planes[colour, 6, at(0), :]
+        for face in range(6):
+            gathered = gathered + planes[colour, face, at(0), :] * adjacent[face]
+        planes[colour, 7, at(0), :] = gathered
+
+    even_row = box_y % 2 == 0
+    for half_sweep in range(2 * SWEEPS):
+        colour = half_sweep % 2
+        for k in range(high_pair):
+            update(colour, k)
+        for j in range((DEPTH - half_sweep) // 2):
+            if box_rows == 2:
+                update(colour, jnp.where(even_row, high_pair + j, pair_count - 1 - j))
+            else:
+                update(colour, high_pair + j)
+                update(colour, pair_count - 1 - j)
+
+    odd = odd_cells(SIDE, 0)
     for half in range(2):
-        pieces = [planes[7, pl.ds((half * 8 + y) * XPOS, SIDE), :] for y in range(8)]
-        result[pl.ds(0, LANES), pl.ds(half * LANES, LANES)] = jnp.concatenate(pieces, axis=0).T
+        cells = []
+        for k in range(half * 4, half * 4 + 4):
+            red = planes[0, 7, pl.ds(k * XPOS, SIDE), :]
+            black = planes[1, 7, pl.ds(k * XPOS, SIDE), :]
+            cells += [jnp.where(odd, black, red), jnp.where(odd, red, black)]
+        result[pl.ds(0, LANES), pl.ds(half * LANES, LANES)] = jnp.concatenate(cells, axis=0).T
     count = jnp.int32(0)
     first = jnp.int32(0)
     for layer in range(groups.shape[0]):
@@ -369,7 +428,7 @@
     )
     send_a, send_b, *local = pl.pallas_call(
         pack_kernel,
-        out_shape=[pltpu.VMEM((12, REACH, CELLS), BF16)] * 2
+        out_shape=[pltpu.VMEM((10, REACH, CELLS), BF16)] * 2
         + [pltpu.VMEM(array.shape, array.dtype) for array in raw[:-1]]
         + [pltpu.SMEM(raw[-1].shape, raw[-1].dtype)],
         in_specs=[pl.BlockSpec(memory_space=pltpu.HBM)] * 6,
@@ -417,7 +476,7 @@
         lax.ppermute(send, "box", lateral_pairs(box_rows, box_cols, *kind))
         for send, kind in zip(sends, kinds, strict=True)
     ]
-    planes_shape = (COEFS, rows_of(box_rows) * XPOS, LANES)
+    planes_shape = (2, COEFS, pairs_of(box_rows) * XPOS, LANES)
     planes = pl.pallas_call(
         lambda *refs: prepare_kernel(box_rows, box_cols, *refs),
         out_shape=pltpu.VMEM(planes_shape, F32),

time: 28.9 us -> 28.8 us (level)
  waiting for transfers between devices: 8.78 us -> 8.15 us
  Pallas kernels: 5.64 us -> 6.11 us
    ppermute x1, waiting for transfers between devices: 1.49 us -> 0.96 us  [per_device(): from_a = lax.ppermute(send_a, 'grp', swaps(group_count, 0))]
  transfers between devices with their start and end apart: 7 -> 7, of which waited for: 4 -> 4; matrix products, arithmetic and copies ran while one was open for 0% -> 0% of each run, Pallas kernels for 2% -> 3%
where the time goes in v4:
time: 28.8 us; the launch traced here: 28.7 us
  starting transfers between devices  14.3 us (50%)
  waiting for transfers between devices  8.15 us (28%)
  Pallas kernels  6.11 us (21%)
    ppermute x5, starting transfers between devices, per_device(): lax.ppermute(send, 'box', lateral_pairs(box_rows, box_cols, *kind))  11.1 us
    pallas_call x1, Pallas kernels, per_device(): pl.pallas_call(lambda *refs: smooth_kernel(box_rows, box_cols, kinds, *re...  3.8 us
    ppermute x5, waiting for transfers between devices, per_device(): lax.ppermute(send, 'box', lateral_pairs(box_rows, box_cols, *kind))  3.65 us
    ppermute x1, waiting for transfers between devices, per_device(): from_b = lax.ppermute(send_b, 'grp', swaps(group_count, 1))  3.53 us
    ppermute x1, starting transfers between devices, per_device(): from_b = lax.ppermute(send_b, 'grp', swaps(group_count, 1))  1.91 us
    ppermute x1, starting transfers between devices, per_device(): from_a = lax.ppermute(send_a, 'grp', swaps(group_count, 0))  1.27 us
    pallas_call x1, Pallas kernels, per_device(): pl.pallas_call(pack_kernel, out_shape=[pltpu.VMEM((10, REACH, CELLS), BF1...  1.14 us
    ppermute x1, waiting for transfers between devices, per_device(): from_a = lax.ppermute(send_a, 'grp', swaps(group_count, 0))  0.96 us
  transfers between devices with their start and end apart: 7, of which 4 were waited for; matrix products, arithmetic and copies ran while one was open for 0% of the time, Pallas kernels for 3%

profile of v4, /device:TPU:5, one launch (start us, length us, event | category | flops | bytes accessed | tf_op | source)
XLA Modules:
  0.0 28.7 jit_solution(7826601632668467749)
XLA Ops:
  0.0 1.1 %pack.1 = (bf16[10,24,256]{2,1,0:T(8,128)(2,1)S(1)}, bf16[10,24,256]{2,1,0:T(8,128)(2,1)S(1)}, bf16[64,256]{1,0:T(8,128)(2,1)S(1)}, bf16[6,64,256]{2,1,0:T(8,128...) custom-call(bf16[64,256]{1,0:T(8,128)(2,1)} %bitcast.10, ...), custom_call_target="tpu_custom_call" | custom-call | tf_op jit(solution)/shard_map/pack/pallas_call | solution.py:429
  1.1 1.3 %collective-permute-start = (bf16[10,24,256]{2,1,0:T(8,128)(2,1)S(1)}, bf16[10,24,256]{2,1,0:T(8,128)(2,1)S(1)}, u32[]{:S(2)}, u32[]{:S(2)}) collective-permute-start(bf16[10,24,256]{2,1,0:T(8,128)(2,1)S(1)} %get-tuple-element.26), channel_id=1, source_target_pairs={{0,8},{8,0},{16,24},{24,16},{1,9},{9,1},{17,25},{25,17},{2,10},{10... | collective-permute-start | bytes 368648 | tf_op jit(solution)/shard_map/ppermute | solution.py:440
  2.4 1.9 %collective-permute-start.1 = (bf16[10,24,256]{2,1,0:T(8,128)(2,1)S(1)}, bf16[10,24,256]{2,1,0:T(8,128)(2,1)S(1)}, u32[]{:S(2)}, u32[]{:S(2)}) collective-permute-start(bf16[10,24,256]{2,1,0:T(8,128)(2,1)S(1)} %get-tuple-element.27), channel_id=1, source_target_pairs={{8,16},{16,8},{9,17},{17,9},{10,18},{18,10},{11,19},{19,11},{12,20... | collective-permute-start | bytes 368648 | tf_op jit(solution)/shard_map/ppermute | solution.py:441
  4.3 0.1 own.1.refs_0_
  4.4 0.0 copy-start
  4.4 1.0 %collective-permute-done.refs_1_ = bf16[10,24,256]{2,1,0:T(8,128)(2,1)S(1)} collective-permute-done((bf16[10,24,256]{2,1,0:T(8,128)(2,1)S(1)}, bf16[10,24,256]{2,1,0:T(8,128)(2,1)S(1)}, u32[]{:S(2)}, u32[]{:S(2)}) %collective-permute-start) | collective-permute-done | bytes 122912 | tf_op jit(solution)/shard_map/ppermute | solution.py:440
  5.4 3.5 %collective-permute-done.1.refs_2_ = bf16[10,24,256]{2,1,0:T(8,128)(2,1)S(1)} collective-permute-done((bf16[10,24,256]{2,1,0:T(8,128)(2,1)S(1)}, bf16[10,24,256]{2,1,0:T(8,128)(2,1)S(1)}, u32[]{:S(2)}, u32[]{:S(2)}) %collective-permute-start.1) | collective-permute-done | bytes 122912 | tf_op jit(solution)/shard_map/ppermute | solution.py:441
  8.9 0.4 %turn.1 = (f32[9,256,128]{2,1,0:T(8,128)S(1)}, bf16[736,128]{1,0:T(8,128)(2,1)S(1)}) custom-call(f32[9,64,256]{2,1,0:T(8,128)S(1)} %own.1.refs_0_, bf16[10,24,256]{2,1,0:T(8,128)(2,1)S(1)} %collective-permute-done.refs_1_, bf16[10,24,256]{2,1,0:T(8,128)(2,1)S(1)} %collective-permute-done.1.refs_2_), custom_call_target="tpu_custom_call" | custom-call | tf_op jit(solution)/shard_map/turn/pallas_call | solution.py:456
  9.3 2.4 %collective-permute-start.2 = (bf16[736,128]{1,0:T(8,128)(2,1)S(1)}, bf16[736,128]{1,0:T(8,128)(2,1)S(1)}, u32[]{:S(2)}, u32[]{:S(2)}) collective-permute-start(bf16[736,128]{1,0:T(8,128)(2,1)S(1)} %get-tuple-element.29), channel_id=1, source_target_pairs={{0,4},{1,5},{2,6},{3,7},{4,0},{5,1},{6,2},{7,3},{8,12},{9,13},{10,... | collective-permute-start | bytes 565256 | tf_op jit(solution)/shard_map/ppermute | solution.py:476
  11.7 0.5 %rims.1 = (bf16[736,128]{1,0:T(8,128)(2,1)S(1)}, bf16[736,128]{1,0:T(8,128)(2,1)S(1)}, bf16[120,128]{1,0:T(8,128)(2,1)S(1)}, bf16[120,128]{1,0:T(8,128)(2,1)S(1)}) custom-call(f32[9,256,128]{2,1,0:T(8,128)S(1)} %get-tuple-element.28.refs_0_), custom_call_target="tpu_custom_call" | custom-call | flops 1048576 | bytes 1048576 | tf_op jit(solution)/shard_map/rims/pallas_call | solution.py:465
  12.2 2.5 %collective-permute-start.3 = (bf16[736,128]{1,0:T(8,128)(2,1)S(1)}, bf16[736,128]{1,0:T(8,128)(2,1)S(1)}, u32[]{:S(2)}, u32[]{:S(2)}) collective-permute-start(bf16[736,128]{1,0:T(8,128)(2,1)S(1)} %get-tuple-element.30), channel_id=1, source_target_pairs={{0,1},{1,0},{2,3},{3,2},{4,5},{5,4},{6,7},{7,6},{8,9},{9,8},{10,11... | collective-permute-start | bytes 565256 | tf_op jit(solution)/shard_map/ppermute | solution.py:476
  14.6 3.1 %collective-permute-start.4 = (bf16[736,128]{1,0:T(8,128)(2,1)S(1)}, bf16[736,128]{1,0:T(8,128)(2,1)S(1)}, u32[]{:S(2)}, u32[]{:S(2)}) collective-permute-start(bf16[736,128]{1,0:T(8,128)(2,1)S(1)} %get-tuple-element.31), channel_id=1, source_target_pairs={{1,2},{2,1},{5,6},{6,5},{9,10},{10,9},{13,14},{14,13},{17,18},{18,... | collective-permute-start | bytes 565256 | tf_op jit(solution)/shard_map/ppermute | solution.py:476
  17.8 0.1 collective-permute-start.5
  17.8 3.1 %collective-permute-start.6 = (bf16[120,128]{1,0:T(8,128)(2,1)S(1)}, bf16[120,128]{1,0:T(8,128)(2,1)S(1)}, u32[]{:S(2)}, u32[]{:S(2)}) collective-permute-start(bf16[120,128]{1,0:T(8,128)(2,1)S(1)} %get-tuple-element.33), channel_id=1, source_target_pairs={{1,6},{2,5},{5,2},{6,1},{9,14},{10,13},{13,10},{14,9},{17,22},{18,... | collective-permute-start | bytes 92168 | tf_op jit(solution)/shard_map/ppermute | solution.py:476
  20.9 0.2 prepare.1.refs_0_
  21.2 1.2 %collective-permute-done.5.refs_4_ = bf16[120,128]{1,0:T(8,128)(2,1)S(1)} collective-permute-done((bf16[120,128]{1,0:T(8,128)(2,1)S(1)}, bf16[120,128]{1,0:T(8,128)(2,1)S(1)}, u32[]{:S(2)}, u32[]{:S(2)}) %collective-permute-start.5) | collective-permute-done | bytes 30752 | tf_op jit(solution)/shard_map/ppermute | solution.py:476
  22.4 2.5 %collective-permute-done.6.refs_5_ = bf16[120,128]{1,0:T(8,128)(2,1)S(1)} collective-permute-done((bf16[120,128]{1,0:T(8,128)(2,1)S(1)}, bf16[120,128]{1,0:T(8,128)(2,1)S(1)}, u32[]{:S(2)}, u32[]{:S(2)}) %collective-permute-start.6) | collective-permute-done | bytes 30752 | tf_op jit(solution)/shard_map/ppermute | solution.py:476
  24.8 0.0 collective-permute-done.2.refs_1_
  24.9 0.0 collective-permute-done.3.refs_2_
  24.9 0.0 collective-permute-done.4.refs_3_
  24.9 0.0 copy-done
  24.9 3.8 %smooth.1 = (f32[192,128]{1,0:T(8,128)}, f32[2,8,352,128]{3,2,1,0:T(8,128)S(1)}) custom-call(f32[2,8,352,128]{3,2,1,0:T(8,128)S(1)} %prepare.1.refs_0_, bf16[736,128]{1,0:T(8,128)(2,1)S(1)} %collective-permute-done.2.refs_1_, bf16[736,128]{1,0:T(8,128)(2,1)S(1)} %collective-permute-done.3.refs_2_, ...), custom_call_target="tpu_custom_call", output_to_operand_aliasing={{1}: (0, {})} | custom-call | tf_op jit(solution)/shard_map/smooth/pallas_call | solution.py:489
Async XLA Ops:
  1.1 4.3 %collective-permute-start = (bf16[10,24,256]{2,1,0:T(8,128)(2,1)S(1)}, bf16[10,24,256]{2,1,0:T(8,128)(2,1)S(1)}, u32[]{:S(2)}, u32[]{:S(2)}) collective-permute-start(bf16[10,24,256]{2,1,0:T(8,128)(2,1)S(1)} %get-tuple-element.26), channel_id=1, source_target_pairs={{0,8},{8,0},{16,24},{24,16},{1,9},{9,1},{17,25},{25,17},{2,10},{10... | collective-permute-start | bytes 368648 | tf_op jit(solution)/shard_map/ppermute | solution.py:440
  2.4 6.5 %collective-permute-start.1 = (bf16[10,24,256]{2,1,0:T(8,128)(2,1)S(1)}, bf16[10,24,256]{2,1,0:T(8,128)(2,1)S(1)}, u32[]{:S(2)}, u32[]{:S(2)}) collective-permute-start(bf16[10,24,256]{2,1,0:T(8,128)(2,1)S(1)} %get-tuple-element.27), channel_id=1, source_target_pairs={{8,16},{16,8},{9,17},{17,9},{10,18},{18,10},{11,19},{19,11},{12,20... | collective-permute-start | bytes 368648 | tf_op jit(solution)/shard_map/ppermute | solution.py:441
  4.4 20.4 %copy-start = (s32[16]{0:T(128)S(1)}, s32[16]{0:T(128)}, u32[]{:S(2)}) copy-start(s32[16]{0:T(128)} %refs_6_.1) | copy-start | bytes 196
  9.3 15.5 %collective-permute-start.2 = (bf16[736,128]{1,0:T(8,128)(2,1)S(1)}, bf16[736,128]{1,0:T(8,128)(2,1)S(1)}, u32[]{:S(2)}, u32[]{:S(2)}) collective-permute-start(bf16[736,128]{1,0:T(8,128)(2,1)S(1)} %get-tuple-element.29), channel_id=1, source_target_pairs={{0,4},{1,5},{2,6},{3,7},{4,0},{5,1},{6,2},{7,3},{8,12},{9,13},{10,... | collective-permute-start | bytes 565256 | tf_op jit(solution)/shard_map/ppermute | solution.py:476
  12.2 12.7 %collective-permute-start.3 = (bf16[736,128]{1,0:T(8,128)(2,1)S(1)}, bf16[736,128]{1,0:T(8,128)(2,1)S(1)}, u32[]{:S(2)}, u32[]{:S(2)}) collective-permute-start(bf16[736,128]{1,0:T(8,128)(2,1)S(1)} %get-tuple-element.30), channel_id=1, source_target_pairs={{0,1},{1,0},{2,3},{3,2},{4,5},{5,4},{6,7},{7,6},{8,9},{9,8},{10,11... | collective-permute-start | bytes 565256 | tf_op jit(solution)/shard_map/ppermute | solution.py:476
  14.6 10.2 %collective-permute-start.4 = (bf16[736,128]{1,0:T(8,128)(2,1)S(1)}, bf16[736,128]{1,0:T(8,128)(2,1)S(1)}, u32[]{:S(2)}, u32[]{:S(2)}) collective-permute-start(bf16[736,128]{1,0:T(8,128)(2,1)S(1)} %get-tuple-element.31), channel_id=1, source_target_pairs={{1,2},{2,1},{5,6},{6,5},{9,10},{10,9},{13,14},{14,13},{17,18},{18,... | collective-permute-start | bytes 565256 | tf_op jit(solution)/shard_map/ppermute | solution.py:476
  17.8 4.6 %collective-permute-start.5 = (bf16[120,128]{1,0:T(8,128)(2,1)S(1)}, bf16[120,128]{1,0:T(8,128)(2,1)S(1)}, u32[]{:S(2)}, u32[]{:S(2)}) collective-permute-start(bf16[120,128]{1,0:T(8,128)(2,1)S(1)} %get-tuple-element.32), channel_id=1, source_target_pairs={{0,5},{1,4},{2,7},{3,6},{4,1},{5,0},{6,3},{7,2},{8,13},{9,12},{10,... | collective-permute-start | bytes 92168 | tf_op jit(solution)/shard_map/ppermute | solution.py:476
  17.8 7.0 %collective-permute-start.6 = (bf16[120,128]{1,0:T(8,128)(2,1)S(1)}, bf16[120,128]{1,0:T(8,128)(2,1)S(1)}, u32[]{:S(2)}, u32[]{:S(2)}) collective-permute-start(bf16[120,128]{1,0:T(8,128)(2,1)S(1)} %get-tuple-element.33), channel_id=1, source_target_pairs={{1,6},{2,5},{5,2},{6,1},{9,14},{10,13},{13,10},{14,9},{17,22},{18,... | collective-permute-start | bytes 92168 | tf_op jit(solution)/shard_map/ppermute | solution.py:476

commit v5 on v4

--- a/solution.py
+++ b/solution.py
@@ -53,14 +53,14 @@
 
 
 def pack_kernel(*refs):
-    sources, (send_a, send_b), copies, semaphores = refs[:6], refs[6:8], refs[8:14], refs[14]
+    sources, (send_a, send_b), copies, semaphores = refs[:7], refs[7:9], refs[9:16], refs[16]
     moves = [
         pltpu.make_async_copy(source, copy, semaphores.at[index])
         for index, (source, copy) in enumerate(zip(sources, copies, strict=True))
     ]
     for move in moves:
         move.start()
-    vol, ap, cond, src, prev, flags = copies
+    vol, ap, cond, src, prev, flags, _ = copies
     group = lax.axis_index("grp")
     column = lax.axis_index("box")
     for move in moves:
@@ -210,12 +210,22 @@
     return (lax.broadcasted_iota(jnp.int32, (count, LANES), 1) + x) % 2 == 1
 
 
-def put_pair(planes, plane, rows, odd, low, high):
-    planes[0, plane, rows, :] = jnp.where(odd, high, low)
-    planes[1, plane, rows, :] = jnp.where(odd, low, high)
-
-
-def prepare_kernel(box_rows, box_cols, turned, planes):
+def put_pair(grid, plane, rows, odd, low, high):
+    planes, *states = grid
+    red, black = jnp.where(odd, high, low), jnp.where(odd, low, high)
+    if plane == COEFS - 1:
+        states[0][rows, :] = red
+        states[1][rows, :] = black
+    else:
+        planes[0, plane, rows, :] = red
+        planes[1, plane, rows, :] = black
+
+
+def slab(rim, index):
+    return rim[pl.ds(index * SIDE, SIDE), :].astype(F32)
+
+
+def prepare_kernel(box_rows, box_cols, turned, *grid):
     box_y = lax.axis_index("box") // box_cols
     low_open = jnp.where(box_y > 0, 1.0, 0.0).astype(F32)
     high_open = jnp.where(box_y < box_rows - 1, 1.0, 0.0).astype(F32)
@@ -232,26 +242,20 @@
     for k in range(pairs_of(box_rows)):
         own = 2 * k < SIDE
         clear = pl.ds(k * XPOS + SIDE, SIDE) if own else pl.ds(k * XPOS, XPOS)
-        for colour in (0, 1):
-            for plane in range(COEFS):
-                planes[colour, plane, clear, :] = jnp.zeros((SIDE if own else XPOS, LANES), F32)
+        empty = jnp.zeros((SIDE if own else XPOS, LANES), F32)
+        for plane in range(COEFS):
+            put_pair(grid, plane, clear, empty > 0.0, empty, empty)
         if own:
             for plane, (low, high) in enumerate(zip(weights_at(2 * k), weights_at(2 * k + 1), strict=True)):
-                put_pair(planes, plane, pl.ds(k * XPOS, SIDE), odd, low, high)
-
-
-def smooth_kernel(box_rows, box_cols, kinds, planes_in, *refs):
-    pieces = dict(zip(kinds, refs[: len(kinds)], strict=True))
-    groups, out, planes, result = refs[len(kinds) :]
-    pair_count = pairs_of(box_rows)
-    low_pair = pair_count - DEPTH // 2
-    high_pair = SIDE // 2
-    group = lax.axis_index("grp")
+                put_pair(grid, plane, pl.ds(k * XPOS, SIDE), odd, low, high)
+
+
+def sides_kernel(box_rows, box_cols, *refs):
+    rims, grid = refs[3:-3], refs[-3:]
     box_x = lax.axis_index("box") % box_cols
     box_y = lax.axis_index("box") // box_cols
-
-    def slab(rim, index):
-        return rim[pl.ds(index * SIDE, SIDE), :].astype(F32)
+    low_pair = pairs_of(box_rows) - DEPTH // 2
+    high_pair = SIDE // 2
 
     def place_y(rim, high):
         odd = odd_cells(SIDE, 0)
@@ -267,7 +271,7 @@
             rows = pl.ds(((high_pair if high else low_pair) + j) * XPOS, SIDE)
             two = [weights_at(2 * j + i) + [slab(rim, COEFS * (DEPTH - 1) + 2 * j + i)] for i in (0, 1)]
             for plane, (low_value, high_value) in enumerate(zip(*two, strict=True)):
-                put_pair(planes, plane, rows, odd, low_value, high_value)
+                put_pair(grid, plane, rows, odd, low_value, high_value)
 
     def place_x(rim, high):
         half = SIDE // 2
@@ -278,9 +282,36 @@
             odd = odd_lanes(half, x)
             if 0 <= at < DEPTH - 1:
                 for plane, value in enumerate(normal([slab(rim, plane * (DEPTH - 1) + at) for plane in range(COEFS)])):
-                    put_pair(planes, plane, rows, odd, value[:half], value[half:])
+                    put_pair(grid, plane, rows, odd, value[:half], value[half:])
             value = slab(rim, COEFS * (DEPTH - 1) + i)
-            put_pair(planes, 7, rows, odd, value[:half], value[half:])
+            put_pair(grid, 7, rows, odd, value[:half], value[half:])
+
+    for odd_x in (0, 1):
+
+        @pl.when(box_x % 2 == odd_x)
+        def _():
+            place_x(rims[-2], odd_x == 0)
+            place_x(rims[-1], odd_x == 1)
+
+    for odd_y in (0, 1):
+
+        @pl.when(box_y % 2 == odd_y)
+        def _():
+            for kind, rim in enumerate(rims[:-2]):
+                place_y(rim, odd_y == kind)
+
+
+def smooth_kernel(box_rows, box_cols, kinds, *refs):
+    refs = refs[3:]
+    pieces = dict(zip(kinds, refs[: len(kinds)], strict=True))
+    groups, out, planes, *states, result = refs[len(kinds) :]
+    grid = (planes, *states)
+    pair_count = pairs_of(box_rows)
+    low_pair = pair_count - DEPTH // 2
+    high_pair = SIDE // 2
+    group = lax.axis_index("grp")
+    box_x = lax.axis_index("box") % box_cols
+    box_y = lax.axis_index("box") // box_cols
 
     def place_corner(piece, high_y, high_x):
         cells = piece[...].astype(F32)
@@ -298,23 +329,9 @@
             for plane, low, high in groups_of:
                 run = low.shape[0]
                 x = SIDE if high_x else XPOS - run
-                put_pair(planes, plane, pl.ds(k + x, run), odd_cells(run, x), low, high)
-
-    for odd_x in (0, 1):
-
-        @pl.when(box_x % 2 == odd_x)
-        def _():
-            place_x(pieces[None, 0], odd_x == 0)
-            place_x(pieces[None, 1], odd_x == 1)
+                put_pair(grid, plane, pl.ds(k + x, run), odd_cells(run, x), low, high)
 
     for odd_y in (0, 1):
-
-        @pl.when(box_y % 2 == odd_y)
-        def _():
-            for (kind_y, kind_x), piece in pieces.items():
-                if kind_x is None:
-                    place_y(piece, odd_y == kind_y)
-
         for odd_x in (0, 1):
 
             @pl.when((box_y % 2 == odd_y) & (box_x % 2 == odd_x))
@@ -331,9 +348,9 @@
                 return pl.ds((k + offset) % pair_count * XPOS, XPOS)
             return pl.ds(pl.multiple_of(lax.rem(k + (offset + pair_count), pair_count) * XPOS, XPOS), XPOS)
 
-        here = planes[1 - colour, 7, at(0), :]
-        below = planes[1 - colour, 7, at(-1), :]
-        above = planes[1 - colour, 7, at(1), :]
+        here = states[1 - colour][at(0), :]
+        below = states[1 - colour][at(-1), :]
+        above = states[1 - colour][at(1), :]
         if colour == 0:
             low, high = jnp.where(odd, here, below), jnp.where(odd, above, here)
         else:
@@ -349,7 +366,7 @@
         gathered = planes[colour, 6, at(0), :]
         for face in range(6):
             gathered = gathered + planes[colour, face, at(0), :] * adjacent[face]
-        planes[colour, 7, at(0), :] = gathered
+        states[colour][at(0), :] = gathered
 
     even_row = box_y % 2 == 0
     for half_sweep in range(2 * SWEEPS):
@@ -367,8 +384,8 @@
     for half in range(2):
         cells = []
         for k in range(half * 4, half * 4 + 4):
-            red = planes[0, 7, pl.ds(k * XPOS, SIDE), :]
-            black = planes[1, 7, pl.ds(k * XPOS, SIDE), :]
+            red = states[0][pl.ds(k * XPOS, SIDE), :]
+            black = states[1][pl.ds(k * XPOS, SIDE), :]
             cells += [jnp.where(odd, black, red), jnp.where(odd, red, black)]
         result[pl.ds(0, LANES), pl.ds(half * LANES, LANES)] = jnp.concatenate(cells, axis=0).T
     count = jnp.int32(0)
@@ -425,15 +442,16 @@
         source.reshape(2 * ROWS, LANES),
         previous.reshape(2 * ROWS, LANES),
         cut_flags.T,
+        new_group,
     )
     send_a, send_b, *local = pl.pallas_call(
         pack_kernel,
         out_shape=[pltpu.VMEM((10, REACH, CELLS), BF16)] * 2
-        + [pltpu.VMEM(array.shape, array.dtype) for array in raw[:-1]]
-        + [pltpu.SMEM(raw[-1].shape, raw[-1].dtype)],
-        in_specs=[pl.BlockSpec(memory_space=pltpu.HBM)] * 6,
-        out_specs=vmem(7) + [smem],
-        scratch_shapes=[pltpu.SemaphoreType.DMA((6,))],
+        + [pltpu.VMEM(array.shape, array.dtype) for array in raw[:5]]
+        + [pltpu.SMEM(array.shape, array.dtype) for array in raw[5:]],
+        in_specs=[pl.BlockSpec(memory_space=pltpu.HBM)] * 7,
+        out_specs=vmem(7) + [smem] * 2,
+        scratch_shapes=[pltpu.SemaphoreType.DMA((7,))],
         compiler_params=params(),
         name="pack",
     )(*[pltpu.with_memory_space_constraint(array, pltpu.HBM) for array in raw])
@@ -447,7 +465,7 @@
         compiler_params=params(),
         cost_estimate=pl.CostEstimate(flops=4 * 2**20, bytes_accessed=2**20, transcendentals=0),
         name="own",
-    )(*held(*local[:-1]), local[-1])
+    )(*held(*local[:5]), local[5])
 
     kinds_y = [0] if box_rows == 2 else [0, 1]
     kinds = [(kind, None) for kind in kinds_y] + [(None, 0), (None, 1)]
@@ -476,29 +494,40 @@
         lax.ppermute(send, "box", lateral_pairs(box_rows, box_cols, *kind))
         for send, kind in zip(sends, kinds, strict=True)
     ]
-    planes_shape = (2, COEFS, pairs_of(box_rows) * XPOS, LANES)
-    planes = pl.pallas_call(
+    sides = [array for array, kind in zip(arrived, kinds, strict=True) if None in kind]
+    arrived = [array for array, kind in zip(arrived, kinds, strict=True) if None not in kind]
+    kinds = [kind for kind in kinds if None not in kind]
+    cells = pairs_of(box_rows) * XPOS
+    grid_shapes = [pltpu.VMEM((2, COEFS - 1, cells, LANES), F32)] + [pltpu.VMEM((cells, LANES), F32)] * 2
+    grid = pl.pallas_call(
         lambda *refs: prepare_kernel(box_rows, box_cols, *refs),
-        out_shape=pltpu.VMEM(planes_shape, F32),
+        out_shape=grid_shapes,
         in_specs=vmem(1),
-        out_specs=vmem(1)[0],
+        out_specs=vmem(3),
         compiler_params=params(),
         cost_estimate=pl.CostEstimate(flops=8 * 2**20, bytes_accessed=2**20, transcendentals=0),
         name="prepare",
     )(*held(turned))
-    smoothed, _ = pl.pallas_call(
+    grid = pl.pallas_call(
+        lambda *refs: sides_kernel(box_rows, box_cols, *refs),
+        out_shape=grid_shapes,
+        in_specs=vmem(3 + len(sides)),
+        out_specs=vmem(3),
+        input_output_aliases={0: 0, 1: 1, 2: 2},
+        compiler_params=params(),
+        cost_estimate=pl.CostEstimate(flops=2**10, bytes_accessed=2**10, transcendentals=0),
+        name="sides",
+    )(*held(*grid, *sides))
+    smoothed, *_ = pl.pallas_call(
         lambda *refs: smooth_kernel(box_rows, box_cols, kinds, *refs),
-        out_shape=[
-            jax.ShapeDtypeStruct((2 * OUT_ROWS, LANES), F32),
-            pltpu.VMEM(planes_shape, F32),
-        ],
-        in_specs=vmem(1 + len(kinds)) + [smem],
-        out_specs=vmem(2),
+        out_shape=[jax.ShapeDtypeStruct((2 * OUT_ROWS, LANES), F32)] + grid_shapes,
+        in_specs=vmem(3 + len(kinds)) + [smem],
+        out_specs=vmem(4),
         scratch_shapes=[pltpu.VMEM((REACH + SIDE + OUT_ROWS, CELLS), F32)],
-        input_output_aliases={0: 1},
+        input_output_aliases={0: 1, 1: 2, 2: 3},
         compiler_params=params(),
         name="smooth",
-    )(*held(planes, *arrived), new_group)
+    )(*held(*grid, *arrived), local[6])
     return smoothed.reshape(OUT_ROWS, 1, CELLS)
 
 

time: 28.8 us -> 26.8 us (0.931)
  Pallas kernels: 6.11 us -> 4.83 us
  waiting for transfers between devices: 8.15 us -> 7.38 us
    pallas_call x1, Pallas kernels: 3.8 us -> 1.76 us  [per_device(): pl.pallas_call(lambda *refs: smooth_kernel(box_rows, box_cols, kinds, *re...]
    ppermute x5, waiting for transfers between devices: 3.65 us -> 2.87 us  [per_device(): lax.ppermute(send, 'box', lateral_pairs(box_rows, box_cols, *kind))]
    pallas_call x0 -> x1, Pallas kernels: none -> 0.75 us  [per_device(): pl.pallas_call(lambda *refs: sides_kernel(box_rows, box_cols, *refs), out...]
  transfers between devices with their start and end apart: 7 -> 7, of which waited for: 4 -> 4; matrix products, arithmetic and copies ran while one was open for 0% -> 0% of each run, Pallas kernels for 3% -> 6%
where the time goes in v5:
time: 26.8 us; the launch traced here: 26.6 us
  starting transfers between devices  14.3 us (53%)
  waiting for transfers between devices  7.38 us (28%)
  Pallas kernels  4.83 us (18%)
    ppermute x5, starting transfers between devices, per_device(): lax.ppermute(send, 'box', lateral_pairs(box_rows, box_cols, *kind))  11.1 us
    ppermute x1, waiting for transfers between devices, per_device(): from_b = lax.ppermute(send_b, 'grp', swaps(group_count, 1))  3.53 us
    ppermute x5, waiting for transfers between devices, per_device(): lax.ppermute(send, 'box', lateral_pairs(box_rows, box_cols, *kind))  2.87 us
    ppermute x1, starting transfers between devices, per_device(): from_b = lax.ppermute(send_b, 'grp', swaps(group_count, 1))  1.91 us
    pallas_call x1, Pallas kernels, per_device(): pl.pallas_call(lambda *refs: smooth_kernel(box_rows, box_cols, kinds, *re...  1.76 us
    ppermute x1, starting transfers between devices, per_device(): from_a = lax.ppermute(send_a, 'grp', swaps(group_count, 0))  1.27 us
    pallas_call x1, Pallas kernels, per_device(): pl.pallas_call(pack_kernel, out_shape=[pltpu.VMEM((10, REACH, CELLS), BF1...  1.16 us
    ppermute x1, waiting for transfers between devices, per_device(): from_a = lax.ppermute(send_a, 'grp', swaps(group_count, 0))  0.97 us
  transfers between devices with their start and end apart: 7, of which 4 were waited for; matrix products, arithmetic and copies ran while one was open for 0% of the time, Pallas kernels for 6%

profile of v5, /device:TPU:5, one launch (start us, length us, event | category | flops | bytes accessed | tf_op | source)
XLA Modules:
  0.0 26.6 jit_solution(8999757035813078377)
XLA Ops:
  0.0 1.2 %pack.1 = (bf16[10,24,256]{2,1,0:T(8,128)(2,1)S(1)}, bf16[10,24,256]{2,1,0:T(8,128)(2,1)S(1)}, bf16[64,256]{1,0:T(8,128)(2,1)S(1)}, bf16[6,64,256]{2,1,0:T(8,128...) custom-call(bf16[64,256]{1,0:T(8,128)(2,1)} %bitcast.10, ...), custom_call_target="tpu_custom_call" | custom-call | tf_op jit(solution)/shard_map/pack/pallas_call | solution.py:447
  1.2 1.3 %collective-permute-start = (bf16[10,24,256]{2,1,0:T(8,128)(2,1)S(1)}, bf16[10,24,256]{2,1,0:T(8,128)(2,1)S(1)}, u32[]{:S(2)}, u32[]{:S(2)}) collective-permute-start(bf16[10,24,256]{2,1,0:T(8,128)(2,1)S(1)} %get-tuple-element.33), channel_id=1, source_target_pairs={{0,8},{8,0},{16,24},{24,16},{1,9},{9,1},{17,25},{25,17},{2,10},{10... | collective-permute-start | bytes 368648 | tf_op jit(solution)/shard_map/ppermute | solution.py:458
  2.4 1.9 %collective-permute-start.1 = (bf16[10,24,256]{2,1,0:T(8,128)(2,1)S(1)}, bf16[10,24,256]{2,1,0:T(8,128)(2,1)S(1)}, u32[]{:S(2)}, u32[]{:S(2)}) collective-permute-start(bf16[10,24,256]{2,1,0:T(8,128)(2,1)S(1)} %get-tuple-element.34), channel_id=1, source_target_pairs={{8,16},{16,8},{9,17},{17,9},{10,18},{18,10},{11,19},{19,11},{12,20... | collective-permute-start | bytes 368648 | tf_op jit(solution)/shard_map/ppermute | solution.py:459
  4.4 0.1 own.1.refs_0_
  4.4 1.0 %collective-permute-done.refs_1_ = bf16[10,24,256]{2,1,0:T(8,128)(2,1)S(1)} collective-permute-done((bf16[10,24,256]{2,1,0:T(8,128)(2,1)S(1)}, bf16[10,24,256]{2,1,0:T(8,128)(2,1)S(1)}, u32[]{:S(2)}, u32[]{:S(2)}) %collective-permute-start) | collective-permute-done | bytes 122912 | tf_op jit(solution)/shard_map/ppermute | solution.py:458
  5.4 3.5 %collective-permute-done.1.refs_2_ = bf16[10,24,256]{2,1,0:T(8,128)(2,1)S(1)} collective-permute-done((bf16[10,24,256]{2,1,0:T(8,128)(2,1)S(1)}, bf16[10,24,256]{2,1,0:T(8,128)(2,1)S(1)}, u32[]{:S(2)}, u32[]{:S(2)}) %collective-permute-start.1) | collective-permute-done | bytes 122912 | tf_op jit(solution)/shard_map/ppermute | solution.py:459
  9.0 0.4 %turn.1 = (f32[9,256,128]{2,1,0:T(8,128)S(1)}, bf16[736,128]{1,0:T(8,128)(2,1)S(1)}) custom-call(f32[9,64,256]{2,1,0:T(8,128)S(1)} %own.1.refs_0_, bf16[10,24,256]{2,1,0:T(8,128)(2,1)S(1)} %collective-permute-done.refs_1_, bf16[10,24,256]{2,1,0:T(8,128)(2,1)S(1)} %collective-permute-done.1.refs_2_), custom_call_target="tpu_custom_call" | custom-call | tf_op jit(solution)/shard_map/turn/pallas_call | solution.py:474
  9.3 2.4 %collective-permute-start.2 = (bf16[736,128]{1,0:T(8,128)(2,1)S(1)}, bf16[736,128]{1,0:T(8,128)(2,1)S(1)}, u32[]{:S(2)}, u32[]{:S(2)}) collective-permute-start(bf16[736,128]{1,0:T(8,128)(2,1)S(1)} %get-tuple-element.39), channel_id=1, source_target_pairs={{0,4},{1,5},{2,6},{3,7},{4,0},{5,1},{6,2},{7,3},{8,12},{9,13},{10,... | collective-permute-start | bytes 565256 | tf_op jit(solution)/shard_map/ppermute | solution.py:494
  11.7 0.5 %rims.1 = (bf16[736,128]{1,0:T(8,128)(2,1)S(1)}, bf16[736,128]{1,0:T(8,128)(2,1)S(1)}, bf16[120,128]{1,0:T(8,128)(2,1)S(1)}, bf16[120,128]{1,0:T(8,128)(2,1)S(1)}) custom-call(f32[9,256,128]{2,1,0:T(8,128)S(1)} %get-tuple-element.35.refs_0_), custom_call_target="tpu_custom_call" | custom-call | flops 1048576 | bytes 1048576 | tf_op jit(solution)/shard_map/rims/pallas_call | solution.py:483
  12.2 2.5 %collective-permute-start.3 = (bf16[736,128]{1,0:T(8,128)(2,1)S(1)}, bf16[736,128]{1,0:T(8,128)(2,1)S(1)}, u32[]{:S(2)}, u32[]{:S(2)}) collective-permute-start(bf16[736,128]{1,0:T(8,128)(2,1)S(1)} %get-tuple-element.40), channel_id=1, source_target_pairs={{0,1},{1,0},{2,3},{3,2},{4,5},{5,4},{6,7},{7,6},{8,9},{9,8},{10,11... | collective-permute-start | bytes 565256 | tf_op jit(solution)/shard_map/ppermute | solution.py:494
  14.7 3.1 %collective-permute-start.4 = (bf16[736,128]{1,0:T(8,128)(2,1)S(1)}, bf16[736,128]{1,0:T(8,128)(2,1)S(1)}, u32[]{:S(2)}, u32[]{:S(2)}) collective-permute-start(bf16[736,128]{1,0:T(8,128)(2,1)S(1)} %get-tuple-element.41), channel_id=1, source_target_pairs={{1,2},{2,1},{5,6},{6,5},{9,10},{10,9},{13,14},{14,13},{17,18},{18,... | collective-permute-start | bytes 565256 | tf_op jit(solution)/shard_map/ppermute | solution.py:494
  17.8 0.1 collective-permute-start.5
  17.9 3.1 %collective-permute-start.6 = (bf16[120,128]{1,0:T(8,128)(2,1)S(1)}, bf16[120,128]{1,0:T(8,128)(2,1)S(1)}, u32[]{:S(2)}, u32[]{:S(2)}) collective-permute-start(bf16[120,128]{1,0:T(8,128)(2,1)S(1)} %get-tuple-element.46), channel_id=1, source_target_pairs={{1,6},{2,5},{5,2},{6,1},{9,14},{10,13},{13,10},{14,9},{17,22},{18,... | collective-permute-start | bytes 92168 | tf_op jit(solution)/shard_map/ppermute | solution.py:494
  21.0 0.2 prepare.1
  21.2 0.0 collective-permute-done.2.refs_3_
  21.2 0.0 collective-permute-done.3.refs_4_
  21.2 2.2 %collective-permute-done.4.refs_5_ = bf16[736,128]{1,0:T(8,128)(2,1)S(1)} collective-permute-done((bf16[736,128]{1,0:T(8,128)(2,1)S(1)}, bf16[736,128]{1,0:T(8,128)(2,1)S(1)}, u32[]{:S(2)}, u32[]{:S(2)}) %collective-permute-start.4) | collective-permute-done | bytes 188448 | tf_op jit(solution)/shard_map/ppermute | solution.py:494
  23.5 0.7 %sides.1 = (f32[2,7,352,128]{3,2,1,0:T(8,128)S(1)}, f32[352,128]{1,0:T(8,128)S(1)}, f32[352,128]{1,0:T(8,128)S(1)}) custom-call(f32[2,7,352,128]{3,2,1,0:T(8,128)S(1)} %get-tuple-element.36.refs_0_, f32[352,128]{1,0:T(8,128)S(1)} %get-tuple-element.37.refs_1_, ...), custom_call_target="tpu_custom_call", output_to_operand_aliasing={{0}: (0, {}), {1}: (1, {}), {2}: (2, {})} | custom-call | flops 1024 | bytes 1024 | tf_op jit(solution)/shard_map/sides/pallas_call | solution.py:511
  24.2 0.0 collective-permute-done.5.refs_3_
  24.2 0.6 %collective-permute-done.6.refs_4_ = bf16[120,128]{1,0:T(8,128)(2,1)S(1)} collective-permute-done((bf16[120,128]{1,0:T(8,128)(2,1)S(1)}, bf16[120,128]{1,0:T(8,128)(2,1)S(1)}, u32[]{:S(2)}, u32[]{:S(2)}) %collective-permute-start.6) | collective-permute-done | bytes 30752 | tf_op jit(solution)/shard_map/ppermute | solution.py:494
  24.9 1.8 %smooth.1 = (f32[192,128]{1,0:T(8,128)}, f32[2,7,352,128]{3,2,1,0:T(8,128)S(1)}, f32[352,128]{1,0:T(8,128)S(1)}, f32[352,128]{1,0:T(8,128)S(1)}) custom-call(f32[2,7,352,128]{3,2,1,0:T(8,128)S(1)} %get-tuple-element.42.refs_0_, f32[352,128]{1,0:T(8,128)S(1)} %get-tuple-element.43.refs_1_, ...), custom_call_target="tpu_custom_call", output_to_operand_aliasing={{1}: (0, {}), {2}: (1, {}), {3}: (2, {})} | custom-call | tf_op jit(solution)/shard_map/smooth/pallas_call | solution.py:521
Async XLA Ops:
  1.2 4.3 %collective-permute-start = (bf16[10,24,256]{2,1,0:T(8,128)(2,1)S(1)}, bf16[10,24,256]{2,1,0:T(8,128)(2,1)S(1)}, u32[]{:S(2)}, u32[]{:S(2)}) collective-permute-start(bf16[10,24,256]{2,1,0:T(8,128)(2,1)S(1)} %get-tuple-element.33), channel_id=1, source_target_pairs={{0,8},{8,0},{16,24},{24,16},{1,9},{9,1},{17,25},{25,17},{2,10},{10... | collective-permute-start | bytes 368648 | tf_op jit(solution)/shard_map/ppermute | solution.py:458
  2.4 6.5 %collective-permute-start.1 = (bf16[10,24,256]{2,1,0:T(8,128)(2,1)S(1)}, bf16[10,24,256]{2,1,0:T(8,128)(2,1)S(1)}, u32[]{:S(2)}, u32[]{:S(2)}) collective-permute-start(bf16[10,24,256]{2,1,0:T(8,128)(2,1)S(1)} %get-tuple-element.34), channel_id=1, source_target_pairs={{8,16},{16,8},{9,17},{17,9},{10,18},{18,10},{11,19},{19,11},{12,20... | collective-permute-start | bytes 368648 | tf_op jit(solution)/shard_map/ppermute | solution.py:459
  9.3 11.9 %collective-permute-start.2 = (bf16[736,128]{1,0:T(8,128)(2,1)S(1)}, bf16[736,128]{1,0:T(8,128)(2,1)S(1)}, u32[]{:S(2)}, u32[]{:S(2)}) collective-permute-start(bf16[736,128]{1,0:T(8,128)(2,1)S(1)} %get-tuple-element.39), channel_id=1, source_target_pairs={{0,4},{1,5},{2,6},{3,7},{4,0},{5,1},{6,2},{7,3},{8,12},{9,13},{10,... | collective-permute-start | bytes 565256 | tf_op jit(solution)/shard_map/ppermute | solution.py:494
  12.2 9.0 %collective-permute-start.3 = (bf16[736,128]{1,0:T(8,128)(2,1)S(1)}, bf16[736,128]{1,0:T(8,128)(2,1)S(1)}, u32[]{:S(2)}, u32[]{:S(2)}) collective-permute-start(bf16[736,128]{1,0:T(8,128)(2,1)S(1)} %get-tuple-element.40), channel_id=1, source_target_pairs={{0,1},{1,0},{2,3},{3,2},{4,5},{5,4},{6,7},{7,6},{8,9},{9,8},{10,11... | collective-permute-start | bytes 565256 | tf_op jit(solution)/shard_map/ppermute | solution.py:494
  14.7 8.8 %collective-permute-start.4 = (bf16[736,128]{1,0:T(8,128)(2,1)S(1)}, bf16[736,128]{1,0:T(8,128)(2,1)S(1)}, u32[]{:S(2)}, u32[]{:S(2)}) collective-permute-start(bf16[736,128]{1,0:T(8,128)(2,1)S(1)} %get-tuple-element.41), channel_id=1, source_target_pairs={{1,2},{2,1},{5,6},{6,5},{9,10},{10,9},{13,14},{14,13},{17,18},{18,... | collective-permute-start | bytes 565256 | tf_op jit(solution)/shard_map/ppermute | solution.py:494
  17.8 6.5 %collective-permute-start.5 = (bf16[120,128]{1,0:T(8,128)(2,1)S(1)}, bf16[120,128]{1,0:T(8,128)(2,1)S(1)}, u32[]{:S(2)}, u32[]{:S(2)}) collective-permute-start(bf16[120,128]{1,0:T(8,128)(2,1)S(1)} %get-tuple-element.45), channel_id=1, source_target_pairs={{0,5},{1,4},{2,7},{3,6},{4,1},{5,0},{6,3},{7,2},{8,13},{9,12},{10,... | collective-permute-start | bytes 92168 | tf_op jit(solution)/shard_map/ppermute | solution.py:494
  17.9 7.0 %collective-permute-start.6 = (bf16[120,128]{1,0:T(8,128)(2,1)S(1)}, bf16[120,128]{1,0:T(8,128)(2,1)S(1)}, u32[]{:S(2)}, u32[]{:S(2)}) collective-permute-start(bf16[120,128]{1,0:T(8,128)(2,1)S(1)} %get-tuple-element.46), channel_id=1, source_target_pairs={{1,6},{2,5},{5,2},{6,1},{9,14},{10,13},{13,10},{14,9},{17,22},{18,... | collective-permute-start | bytes 92168 | tf_op jit(solution)/shard_map/ppermute | solution.py:494

commit v6 on v5

--- a/solution.py
+++ b/solution.py
@@ -17,8 +17,12 @@
 LANES = 128
 XPOS = 32
 COEFS = 8
-RIM = COEFS * (DEPTH - 1) * SIDE + DEPTH * SIDE
 CORNER = 120
+NEAR = DEPTH - 2
+USED = REACH + ROWS + REACH
+SPARE = LANES - USED
+RIM_SLABS = COEFS * NEAR + COEFS // 2 + DEPTH
+RIM = RIM_SLABS * SIDE
 F32 = jnp.float32
 BF16 = jnp.bfloat16
 
@@ -113,12 +117,54 @@
     return runs
 
 
+def odd_cells(count, first_x):
+    shape = (count, LANES)
+    cells = lax.broadcasted_iota(jnp.int32, shape, 0) + lax.broadcasted_iota(jnp.int32, shape, 1)
+    return (cells + first_x) % 2 == 1
+
+
+def odd_lanes(count, x):
+    return (lax.broadcasted_iota(jnp.int32, (count, LANES), 1) + x) % 2 == 1
+
+
+def odd_split(x):
+    row = lax.broadcasted_iota(jnp.int32, (SIDE, LANES), 0) // (SIDE // 2)
+    return (row + lax.broadcasted_iota(jnp.int32, (SIDE, LANES), 1) + x) % 2 == 1
+
+
+def write_rim(out, at, high, odd_far):
+    values = []
+    for i in range(1, DEPTH - 1) if high else range(NEAR):
+        values += [at(plane, i) for plane in range(COEFS)]
+    far = 0 if high else NEAR
+    for plane in range(0, COEFS, 2):
+        values.append(jnp.where(odd_far, pltpu.roll(at(plane + 1, far), 1, 1), at(plane, far)))
+    for i in range(DEPTH):
+        values.append(at(COEFS, i - 1 if high else i))
+    for index, value in enumerate(values):
+        out[pl.ds(index * SIDE, SIDE), :] = value.astype(BF16)
+
+
+def slab(rim, index):
+    return rim[pl.ds(index * SIDE, SIDE), :].astype(F32)
+
+
+def read_rim(rim, i, high, odd_far):
+    if i == (NEAR if high else 0):
+        values = []
+        for plane in range(COEFS // 2):
+            both = slab(rim, COEFS * NEAR + plane)
+            values += [jnp.where(odd_far, 0.0, both), jnp.where(odd_far, 0.0, pltpu.roll(both, LANES - 1, 1))]
+        return normal(values)
+    start = (i if high else i - 1) * COEFS
+    return normal([slab(rim, start + plane) for plane in range(COEFS)])
+
+
 def turn_kernel(box_rows, box_cols, own, from_a, from_b, turned, *refs):
     rims, stage = refs[:-1], refs[-1]
     even_group = lax.axis_index("grp") % 2 == 0
     box_y = lax.axis_index("box") // box_cols
-    used = REACH + ROWS + REACH
-    stage[pl.ds(used, LANES - used), :] = jnp.zeros((LANES - used, CELLS), F32)
+    stage[pl.ds(USED, SPARE), :] = jnp.zeros((SPARE, CELLS), F32)
     for plane in range(9):
         a = from_a[plane, :, :].astype(F32)
         b = from_b[plane, :, :].astype(F32)
@@ -132,12 +178,12 @@
             turned[plane, pl.ds(half * LANES, LANES), :] = stage[:, pl.ds(half * LANES, LANES)].T
 
     def rim(out, high):
-        for plane in range(COEFS + 1):
-            reach = DEPTH - 1 if plane < COEFS else DEPTH
-            start = (SIDE - reach) * SIDE if high else 0
-            out[pl.ds(plane * (DEPTH - 1) * SIDE, reach * SIDE), :] = turned[
-                plane, pl.ds(start, reach * SIDE), :
-            ].astype(BF16)
+        first = SIDE - DEPTH + 1 if high else 0
+
+        def at(plane, i):
+            return turned[plane, pl.ds((first + i) * SIDE, SIDE), :]
+
+        write_rim(out, at, high, odd_cells(SIDE, first if high else NEAR))
 
     for odd in (0, 1):
 
@@ -147,18 +193,33 @@
                 rim(out, odd == kind)
 
 
-def rims_kernel(box_rows, box_cols, turned, *refs):
-    rims, corners, stage = refs[:2], refs[2:-1], refs[-1]
+def rims_kernel(box_cols, turned, *refs):
+    rims = refs[-2:]
+    box_x = lax.axis_index("box") % box_cols
+
+    def rim(out, high):
+        first = SIDE - DEPTH + 1 if high else 0
+
+        def at(plane, i):
+            pair = [
+                turned[plane, pl.ds(first + i + odd * SIDE, SIDE // 2, stride=2 * SIDE), :] for odd in (0, 1)
+            ]
+            return jnp.concatenate(pair, axis=0)
+
+        write_rim(out, at, high, odd_split(first if high else NEAR))
+
+    for odd_x in (0, 1):
+
+        @pl.when(box_x % 2 == odd_x)
+        def _():
+            rim(rims[0], odd_x == 0)
+            rim(rims[1], odd_x == 1)
+
+
+def corners_kernel(box_cols, turned, *refs):
+    corners, stage = refs[:-1], refs[-1]
     box_x = lax.axis_index("box") % box_cols
     box_y = lax.axis_index("box") // box_cols
-
-    def rim(out, high):
-        for plane in range(COEFS + 1):
-            reach = DEPTH - 1 if plane < COEFS else DEPTH
-            for i in range(reach):
-                x = SIDE - reach + i if high else i
-                pair = [turned[plane, pl.ds(x + odd * SIDE, SIDE // 2, stride=2 * SIDE), :] for odd in (0, 1)]
-                out[pl.ds((plane * (DEPTH - 1) + i) * SIDE, SIDE), :] = jnp.concatenate(pair, axis=0).astype(BF16)
 
     def corner(out, high_y, high_x):
         for plane, dy, run, row in corner_runs():
@@ -170,12 +231,6 @@
         out[...] = stage[...].astype(BF16)
 
     for odd_x in (0, 1):
-
-        @pl.when(box_x % 2 == odd_x)
-        def _():
-            rim(rims[0], odd_x == 0)
-            rim(rims[1], odd_x == 1)
-
         for odd_y in (0, 1):
 
             @pl.when((box_y % 2 == odd_y) & (box_x % 2 == odd_x))
@@ -198,16 +253,6 @@
 
 def pairs_of(box_rows):
     return rows_of(box_rows) // 2
-
-
-def odd_cells(count, first_x):
-    shape = (count, LANES)
-    cells = lax.broadcasted_iota(jnp.int32, shape, 0) + lax.broadcasted_iota(jnp.int32, shape, 1)
-    return (cells + first_x) % 2 == 1
-
-
-def odd_lanes(count, x):
-    return (lax.broadcasted_iota(jnp.int32, (count, LANES), 1) + x) % 2 == 1
 
 
 def put_pair(grid, plane, rows, odd, low, high):
@@ -221,10 +266,6 @@
         planes[1, plane, rows, :] = black
 
 
-def slab(rim, index):
-    return rim[pl.ds(index * SIDE, SIDE), :].astype(F32)
-
-
 def prepare_kernel(box_rows, box_cols, turned, *grid):
     box_y = lax.axis_index("box") // box_cols
     low_open = jnp.where(box_y > 0, 1.0, 0.0).astype(F32)
@@ -262,14 +303,14 @@
         empty = jnp.zeros((SIDE, LANES), F32)
 
         def weights_at(i):
-            i = i if high else i - 1
-            if not 0 <= i < DEPTH - 1:
+            at = i if high else i - 1
+            if not 0 <= at < DEPTH - 1:
                 return [empty] * (COEFS - 1)
-            return normal([slab(rim, plane * (DEPTH - 1) + i) for plane in range(COEFS)])
+            return read_rim(rim, at, high, odd_cells(SIDE, i))
 
         for j in range(DEPTH // 2):
             rows = pl.ds(((high_pair if high else low_pair) + j) * XPOS, SIDE)
-            two = [weights_at(2 * j + i) + [slab(rim, COEFS * (DEPTH - 1) + 2 * j + i)] for i in (0, 1)]
+            two = [weights_at(2 * j + i) + [slab(rim, RIM_SLABS - DEPTH + 2 * j + i)] for i in (0, 1)]
             for plane, (low_value, high_value) in enumerate(zip(*two, strict=True)):
                 put_pair(grid, plane, rows, odd, low_value, high_value)
 
@@ -281,9 +322,9 @@
             rows = pl.ds(x, half, stride=XPOS)
             odd = odd_lanes(half, x)
             if 0 <= at < DEPTH - 1:
-                for plane, value in enumerate(normal([slab(rim, plane * (DEPTH - 1) + at) for plane in range(COEFS)])):
+                for plane, value in enumerate(read_rim(rim, at, high, odd_split(x))):
                     put_pair(grid, plane, rows, odd, value[:half], value[half:])
-            value = slab(rim, COEFS * (DEPTH - 1) + i)
+            value = slab(rim, RIM_SLABS - DEPTH + i)
             put_pair(grid, 7, rows, odd, value[:half], value[half:])
 
     for odd_x in (0, 1):
@@ -480,16 +521,26 @@
         compiler_params=params(),
         name="turn",
     )(*held(own, from_a, from_b))
+    corners = pl.pallas_call(
+        lambda *refs: corners_kernel(box_cols, *refs),
+        out_shape=shapes[len(kinds_y) + 2 :],
+        in_specs=vmem(1),
+        out_specs=vmem(2 * len(kinds_y)),
+        scratch_shapes=[pltpu.VMEM((CORNER, LANES), F32)],
+        compiler_params=params(),
+        cost_estimate=pl.CostEstimate(flops=2**10, bytes_accessed=2**10, transcendentals=0),
+        name="corners",
+    )(*held(turned))
     sends += pl.pallas_call(
-        lambda *refs: rims_kernel(box_rows, box_cols, *refs),
-        out_shape=shapes[len(kinds_y) :],
-        in_specs=vmem(1),
-        out_specs=vmem(len(shapes) - len(kinds_y)),
-        scratch_shapes=[pltpu.VMEM((CORNER, LANES), F32)],
+        lambda *refs: rims_kernel(box_cols, *refs),
+        out_shape=shapes[len(kinds_y) : len(kinds_y) + 2],
+        in_specs=vmem(2),
+        out_specs=vmem(2),
         compiler_params=params(),
         cost_estimate=pl.CostEstimate(flops=2**20, bytes_accessed=2**20, transcendentals=0),
         name="rims",
-    )(*held(turned))
+    )(*held(turned, corners[0]))
+    sends += corners
     arrived = [
         lax.ppermute(send, "box", lateral_pairs(box_rows, box_cols, *kind))
         for send, kind in zip(sends, kinds, strict=True)

time: 26.8 us -> 26.8 us (level)
  starting transfers between devices: 14.3 us -> 13.4 us
  waiting for transfers between devices: 7.38 us -> 8.09 us
    ppermute x5, starting transfers between devices: 11.1 us -> 10.2 us  [per_device(): lax.ppermute(send, 'box', lateral_pairs(box_rows, box_cols, *kind))]
    ppermute x5, waiting for transfers between devices: 2.87 us -> 3.59 us  [per_device(): lax.ppermute(send, 'box', lateral_pairs(box_rows, box_cols, *kind))]
where the time goes in v6:
time: 26.8 us; the launch traced here: 26.6 us
  starting transfers between devices  13.4 us (50%)
  waiting for transfers between devices  8.09 us (30%)
  Pallas kernels  5.02 us (19%)
    ppermute x5, starting transfers between devices, per_device(): lax.ppermute(send, 'box', lateral_pairs(box_rows, box_cols, *kind))  10.2 us
    ppermute x5, waiting for transfers between devices, per_device(): lax.ppermute(send, 'box', lateral_pairs(box_rows, box_cols, *kind))  3.59 us
    ppermute x1, waiting for transfers between devices, per_device(): from_b = lax.ppermute(send_b, 'grp', swaps(group_count, 1))  3.53 us
    ppermute x1, starting transfers between devices, per_device(): from_b = lax.ppermute(send_b, 'grp', swaps(group_count, 1))  1.91 us
    pallas_call x1, Pallas kernels, per_device(): pl.pallas_call(lambda *refs: smooth_kernel(box_rows, box_cols, kinds, *re...  1.76 us
    ppermute x1, starting transfers between devices, per_device(): from_a = lax.ppermute(send_a, 'grp', swaps(group_count, 0))  1.27 us
    pallas_call x1, Pallas kernels, per_device(): pl.pallas_call(pack_kernel, out_shape=[pltpu.VMEM((10, REACH, CELLS), BF1...  1.16 us
    ppermute x1, waiting for transfers between devices, per_device(): from_a = lax.ppermute(send_a, 'grp', swaps(group_count, 0))  0.97 us
  transfers between devices with their start and end apart: 7, of which 4 were waited for; matrix products, arithmetic and copies ran while one was open for 0% of the time, Pallas kernels for 6%

profile of v6, /device:TPU:5, one launch (start us, length us, event | category | flops | bytes accessed | tf_op | source)
XLA Modules:
  0.0 26.6 jit_solution(14687242570096939474)
XLA Ops:
  0.0 1.2 %pack.1 = (bf16[10,24,256]{2,1,0:T(8,128)(2,1)S(1)}, bf16[10,24,256]{2,1,0:T(8,128)(2,1)S(1)}, bf16[64,256]{1,0:T(8,128)(2,1)S(1)}, bf16[6,64,256]{2,1,0:T(8,128...) custom-call(bf16[64,256]{1,0:T(8,128)(2,1)} %bitcast.10, ...), custom_call_target="tpu_custom_call" | custom-call | tf_op jit(solution)/shard_map/pack/pallas_call | solution.py:488
  1.2 1.3 %collective-permute-start = (bf16[10,24,256]{2,1,0:T(8,128)(2,1)S(1)}, bf16[10,24,256]{2,1,0:T(8,128)(2,1)S(1)}, u32[]{:S(2)}, u32[]{:S(2)}) collective-permute-start(bf16[10,24,256]{2,1,0:T(8,128)(2,1)S(1)} %get-tuple-element.33), channel_id=1, source_target_pairs={{0,8},{8,0},{16,24},{24,16},{1,9},{9,1},{17,25},{25,17},{2,10},{10... | collective-permute-start | bytes 368648 | tf_op jit(solution)/shard_map/ppermute | solution.py:499
  2.4 1.9 %collective-permute-start.1 = (bf16[10,24,256]{2,1,0:T(8,128)(2,1)S(1)}, bf16[10,24,256]{2,1,0:T(8,128)(2,1)S(1)}, u32[]{:S(2)}, u32[]{:S(2)}) collective-permute-start(bf16[10,24,256]{2,1,0:T(8,128)(2,1)S(1)} %get-tuple-element.34), channel_id=1, source_target_pairs={{8,16},{16,8},{9,17},{17,9},{10,18},{18,10},{11,19},{19,11},{12,20... | collective-permute-start | bytes 368648 | tf_op jit(solution)/shard_map/ppermute | solution.py:500
  4.4 0.1 own.1.refs_0_
  4.4 1.0 %collective-permute-done.refs_1_ = bf16[10,24,256]{2,1,0:T(8,128)(2,1)S(1)} collective-permute-done((bf16[10,24,256]{2,1,0:T(8,128)(2,1)S(1)}, bf16[10,24,256]{2,1,0:T(8,128)(2,1)S(1)}, u32[]{:S(2)}, u32[]{:S(2)}) %collective-permute-start) | collective-permute-done | bytes 122912 | tf_op jit(solution)/shard_map/ppermute | solution.py:499
  5.4 3.5 %collective-permute-done.1.refs_2_ = bf16[10,24,256]{2,1,0:T(8,128)(2,1)S(1)} collective-permute-done((bf16[10,24,256]{2,1,0:T(8,128)(2,1)S(1)}, bf16[10,24,256]{2,1,0:T(8,128)(2,1)S(1)}, u32[]{:S(2)}, u32[]{:S(2)}) %collective-permute-start.1) | collective-permute-done | bytes 122912 | tf_op jit(solution)/shard_map/ppermute | solution.py:500
  9.0 0.4 %turn.1 = (f32[9,256,128]{2,1,0:T(8,128)S(1)}, bf16[672,128]{1,0:T(8,128)(2,1)S(1)}) custom-call(f32[9,64,256]{2,1,0:T(8,128)S(1)} %own.1.refs_0_, bf16[10,24,256]{2,1,0:T(8,128)(2,1)S(1)} %collective-permute-done.refs_1_, bf16[10,24,256]{2,1,0:T(8,128)(2,1)S(1)} %collective-permute-done.1.refs_2_), custom_call_target="tpu_custom_call" | custom-call | tf_op jit(solution)/shard_map/turn/pallas_call | solution.py:515
  9.4 0.1 corners.1
  9.5 2.4 %collective-permute-start.2 = (bf16[672,128]{1,0:T(8,128)(2,1)S(1)}, bf16[672,128]{1,0:T(8,128)(2,1)S(1)}, u32[]{:S(2)}, u32[]{:S(2)}) collective-permute-start(bf16[672,128]{1,0:T(8,128)(2,1)S(1)} %get-tuple-element.39), channel_id=1, source_target_pairs={{0,4},{1,5},{2,6},{3,7},{4,0},{5,1},{6,2},{7,3},{8,12},{9,13},{10,... | collective-permute-start | bytes 516104 | tf_op jit(solution)/shard_map/ppermute | solution.py:545
  11.8 0.4 %rims.1 = (bf16[672,128]{1,0:T(8,128)(2,1)S(1)}, bf16[672,128]{1,0:T(8,128)(2,1)S(1)}) custom-call(f32[9,256,128]{2,1,0:T(8,128)S(1)} %get-tuple-element.35.refs_0_, bf16[120,128]{1,0:T(8,128)(2,1)S(1)} %get-tuple-element.40.refs_1_), custom_call_target="tpu_custom_call" | custom-call | flops 1048576 | bytes 1048576 | tf_op jit(solution)/shard_map/rims/pallas_call | solution.py:534
  12.3 2.5 %collective-permute-start.3 = (bf16[672,128]{1,0:T(8,128)(2,1)S(1)}, bf16[672,128]{1,0:T(8,128)(2,1)S(1)}, u32[]{:S(2)}, u32[]{:S(2)}) collective-permute-start(bf16[672,128]{1,0:T(8,128)(2,1)S(1)} %get-tuple-element.41), channel_id=1, source_target_pairs={{0,1},{1,0},{2,3},{3,2},{4,5},{5,4},{6,7},{7,6},{8,9},{9,8},{10,11... | collective-permute-start | bytes 516104 | tf_op jit(solution)/shard_map/ppermute | solution.py:545
  14.7 3.1 %collective-permute-start.4 = (bf16[672,128]{1,0:T(8,128)(2,1)S(1)}, bf16[672,128]{1,0:T(8,128)(2,1)S(1)}, u32[]{:S(2)}, u32[]{:S(2)}) collective-permute-start(bf16[672,128]{1,0:T(8,128)(2,1)S(1)} %get-tuple-element.42), channel_id=1, source_target_pairs={{1,2},{2,1},{5,6},{6,5},{9,10},{10,9},{13,14},{14,13},{17,18},{18,... | collective-permute-start | bytes 516104 | tf_op jit(solution)/shard_map/ppermute | solution.py:545
  17.8 2.2 %collective-permute-start.6 = (bf16[120,128]{1,0:T(8,128)(2,1)S(1)}, bf16[120,128]{1,0:T(8,128)(2,1)S(1)}, u32[]{:S(2)}, u32[]{:S(2)}) collective-permute-start(bf16[120,128]{1,0:T(8,128)(2,1)S(1)} %get-tuple-element.46), channel_id=1, source_target_pairs={{1,6},{2,5},{5,2},{6,1},{9,14},{10,13},{13,10},{14,9},{17,22},{18,... | collective-permute-start | bytes 92168 | tf_op jit(solution)/shard_map/ppermute | solution.py:545
  20.1 0.1 collective-permute-start.5
  20.1 0.2 prepare.1
  20.4 0.0 collective-permute-done.2.refs_3_
  20.4 0.0 collective-permute-done.3.refs_4_
  20.4 1.6 %collective-permute-done.4.refs_5_ = bf16[672,128]{1,0:T(8,128)(2,1)S(1)} collective-permute-done((bf16[672,128]{1,0:T(8,128)(2,1)S(1)}, bf16[672,128]{1,0:T(8,128)(2,1)S(1)}, u32[]{:S(2)}, u32[]{:S(2)}) %collective-permute-start.4) | collective-permute-done | bytes 172064 | tf_op jit(solution)/shard_map/ppermute | solution.py:545
  22.0 0.8 %sides.1 = (f32[2,7,352,128]{3,2,1,0:T(8,128)S(1)}, f32[352,128]{1,0:T(8,128)S(1)}, f32[352,128]{1,0:T(8,128)S(1)}) custom-call(f32[2,7,352,128]{3,2,1,0:T(8,128)S(1)} %get-tuple-element.36.refs_0_, f32[352,128]{1,0:T(8,128)S(1)} %get-tuple-element.37.refs_1_, ...), custom_call_target="tpu_custom_call", output_to_operand_aliasing={{0}: (0, {}), {1}: (1, {}), {2}: (2, {})} | custom-call | flops 1024 | bytes 1024 | tf_op jit(solution)/shard_map/sides/pallas_call | solution.py:562
  22.9 1.9 %collective-permute-done.6.refs_4_ = bf16[120,128]{1,0:T(8,128)(2,1)S(1)} collective-permute-done((bf16[120,128]{1,0:T(8,128)(2,1)S(1)}, bf16[120,128]{1,0:T(8,128)(2,1)S(1)}, u32[]{:S(2)}, u32[]{:S(2)}) %collective-permute-start.6) | collective-permute-done | bytes 30752 | tf_op jit(solution)/shard_map/ppermute | solution.py:545
  24.9 0.0 collective-permute-done.5.refs_3_
  24.9 1.8 %smooth.1 = (f32[192,128]{1,0:T(8,128)}, f32[2,7,352,128]{3,2,1,0:T(8,128)S(1)}, f32[352,128]{1,0:T(8,128)S(1)}, f32[352,128]{1,0:T(8,128)S(1)}) custom-call(f32[2,7,352,128]{3,2,1,0:T(8,128)S(1)} %get-tuple-element.43.refs_0_, f32[352,128]{1,0:T(8,128)S(1)} %get-tuple-element.44.refs_1_, ...), custom_call_target="tpu_custom_call", output_to_operand_aliasing={{1}: (0, {}), {2}: (1, {}), {3}: (2, {})} | custom-call | tf_op jit(solution)/shard_map/smooth/pallas_call | solution.py:572
Async XLA Ops:
  1.2 4.3 %collective-permute-start = (bf16[10,24,256]{2,1,0:T(8,128)(2,1)S(1)}, bf16[10,24,256]{2,1,0:T(8,128)(2,1)S(1)}, u32[]{:S(2)}, u32[]{:S(2)}) collective-permute-start(bf16[10,24,256]{2,1,0:T(8,128)(2,1)S(1)} %get-tuple-element.33), channel_id=1, source_target_pairs={{0,8},{8,0},{16,24},{24,16},{1,9},{9,1},{17,25},{25,17},{2,10},{10... | collective-permute-start | bytes 368648 | tf_op jit(solution)/shard_map/ppermute | solution.py:499
  2.4 6.5 %collective-permute-start.1 = (bf16[10,24,256]{2,1,0:T(8,128)(2,1)S(1)}, bf16[10,24,256]{2,1,0:T(8,128)(2,1)S(1)}, u32[]{:S(2)}, u32[]{:S(2)}) collective-permute-start(bf16[10,24,256]{2,1,0:T(8,128)(2,1)S(1)} %get-tuple-element.34), channel_id=1, source_target_pairs={{8,16},{16,8},{9,17},{17,9},{10,18},{18,10},{11,19},{19,11},{12,20... | collective-permute-start | bytes 368648 | tf_op jit(solution)/shard_map/ppermute | solution.py:500
  9.5 10.9 %collective-permute-start.2 = (bf16[672,128]{1,0:T(8,128)(2,1)S(1)}, bf16[672,128]{1,0:T(8,128)(2,1)S(1)}, u32[]{:S(2)}, u32[]{:S(2)}) collective-permute-start(bf16[672,128]{1,0:T(8,128)(2,1)S(1)} %get-tuple-element.39), channel_id=1, source_target_pairs={{0,4},{1,5},{2,6},{3,7},{4,0},{5,1},{6,2},{7,3},{8,12},{9,13},{10,... | collective-permute-start | bytes 516104 | tf_op jit(solution)/shard_map/ppermute | solution.py:545
  12.3 8.1 %collective-permute-start.3 = (bf16[672,128]{1,0:T(8,128)(2,1)S(1)}, bf16[672,128]{1,0:T(8,128)(2,1)S(1)}, u32[]{:S(2)}, u32[]{:S(2)}) collective-permute-start(bf16[672,128]{1,0:T(8,128)(2,1)S(1)} %get-tuple-element.41), channel_id=1, source_target_pairs={{0,1},{1,0},{2,3},{3,2},{4,5},{5,4},{6,7},{7,6},{8,9},{9,8},{10,11... | collective-permute-start | bytes 516104 | tf_op jit(solution)/shard_map/ppermute | solution.py:545
  14.7 7.3 %collective-permute-start.4 = (bf16[672,128]{1,0:T(8,128)(2,1)S(1)}, bf16[672,128]{1,0:T(8,128)(2,1)S(1)}, u32[]{:S(2)}, u32[]{:S(2)}) collective-permute-start(bf16[672,128]{1,0:T(8,128)(2,1)S(1)} %get-tuple-element.42), channel_id=1, source_target_pairs={{1,2},{2,1},{5,6},{6,5},{9,10},{10,9},{13,14},{14,13},{17,18},{18,... | collective-permute-start | bytes 516104 | tf_op jit(solution)/shard_map/ppermute | solution.py:545
  17.8 7.0 %collective-permute-start.6 = (bf16[120,128]{1,0:T(8,128)(2,1)S(1)}, bf16[120,128]{1,0:T(8,128)(2,1)S(1)}, u32[]{:S(2)}, u32[]{:S(2)}) collective-permute-start(bf16[120,128]{1,0:T(8,128)(2,1)S(1)} %get-tuple-element.46), channel_id=1, source_target_pairs={{1,6},{2,5},{5,2},{6,1},{9,14},{10,13},{13,10},{14,9},{17,22},{18,... | collective-permute-start | bytes 92168 | tf_op jit(solution)/shard_map/ppermute | solution.py:545
  20.1 4.8 %collective-permute-start.5 = (bf16[120,128]{1,0:T(8,128)(2,1)S(1)}, bf16[120,128]{1,0:T(8,128)(2,1)S(1)}, u32[]{:S(2)}, u32[]{:S(2)}) collective-permute-start(bf16[120,128]{1,0:T(8,128)(2,1)S(1)} %get-tuple-element.40.refs_1_), channel_id=1, source_target_pairs={{0,5},{1,4},{2,7},{3,6},{4,1},{5,0},{6,3},{7,2},{8,13},{9,12},{10,... | collective-permute-start | bytes 92168 | tf_op jit(solution)/shard_map/ppermute | solution.py:545

commit v7 on v5

--- a/solution.py
+++ b/solution.py
@@ -342,26 +342,27 @@
 
     odd = odd_cells(XPOS, 0)
 
-    def update(colour, k):
+    def update(colour, k, count=XPOS):
         def at(offset):
             if isinstance(k, int):
-                return pl.ds((k + offset) % pair_count * XPOS, XPOS)
+                return pl.ds((k + offset) % pair_count * XPOS, count)
             return pl.ds(pl.multiple_of(lax.rem(k + (offset + pair_count), pair_count) * XPOS, XPOS), XPOS)
 
-        here = states[1 - colour][at(0), :]
+        wide = states[1 - colour][pl.ds(k * XPOS, XPOS) if count < XPOS else at(0), :]
+        here = wide[:count]
         below = states[1 - colour][at(-1), :]
         above = states[1 - colour][at(1), :]
         if colour == 0:
-            low, high = jnp.where(odd, here, below), jnp.where(odd, above, here)
+            low, high = jnp.where(odd[:count], here, below), jnp.where(odd[:count], above, here)
         else:
-            low, high = jnp.where(odd, below, here), jnp.where(odd, here, above)
+            low, high = jnp.where(odd[:count], below, here), jnp.where(odd[:count], here, above)
         adjacent = (
             pltpu.roll(here, 1, 1),
             pltpu.roll(here, LANES - 1, 1),
             low,
             high,
-            pltpu.roll(here, 1, 0),
-            pltpu.roll(here, XPOS - 1, 0),
+            pltpu.roll(wide, 1, 0)[:count],
+            pltpu.roll(wide, XPOS - 1, 0)[:count],
         )
         gathered = planes[colour, 6, at(0), :]
         for face in range(6):
@@ -372,7 +373,7 @@
     for half_sweep in range(2 * SWEEPS):
         colour = half_sweep % 2
         for k in range(high_pair):
-            update(colour, k)
+            update(colour, k, XPOS if half_sweep < DEPTH - 1 else SIDE)
         for j in range((DEPTH - half_sweep) // 2):
             if box_rows == 2:
                 update(colour, jnp.where(even_row, high_pair + j, pair_count - 1 - j))

time: 26.8 us -> 26.8 us (level)
  no operation moved by 1% of the time
where the time goes in v7:
time: 26.8 us; the launch traced here: 26.6 us
  starting transfers between devices  14.3 us (53%)
  waiting for transfers between devices  7.38 us (28%)
  Pallas kernels  4.84 us (18%)
    ppermute x5, starting transfers between devices, per_device(): lax.ppermute(send, 'box', lateral_pairs(box_rows, box_cols, *kind))  11.1 us
    ppermute x1, waiting for transfers between devices, per_device(): from_b = lax.ppermute(send_b, 'grp', swaps(group_count, 1))  3.53 us
    ppermute x5, waiting for transfers between devices, per_device(): lax.ppermute(send, 'box', lateral_pairs(box_rows, box_cols, *kind))  2.87 us
    ppermute x1, starting transfers between devices, per_device(): from_b = lax.ppermute(send_b, 'grp', swaps(group_count, 1))  1.91 us
    pallas_call x1, Pallas kernels, per_device(): pl.pallas_call(lambda *refs: smooth_kernel(box_rows, box_cols, kinds, *re...  1.77 us
    ppermute x1, starting transfers between devices, per_device(): from_a = lax.ppermute(send_a, 'grp', swaps(group_count, 0))  1.27 us
    pallas_call x1, Pallas kernels, per_device(): pl.pallas_call(pack_kernel, out_shape=[pltpu.VMEM((10, REACH, CELLS), BF1...  1.16 us
    ppermute x1, waiting for transfers between devices, per_device(): from_a = lax.ppermute(send_a, 'grp', swaps(group_count, 0))  0.97 us
  transfers between devices with their start and end apart: 7, of which 4 were waited for; matrix products, arithmetic and copies ran while one was open for 0% of the time, Pallas kernels for 6%

profile of v7, /device:TPU:5, one launch (start us, length us, event | category | flops | bytes accessed | tf_op | source)
XLA Modules:
  0.0 26.6 jit_solution(4472819732716689191)
XLA Ops:
  0.0 1.2 %pack.1 = (bf16[10,24,256]{2,1,0:T(8,128)(2,1)S(1)}, bf16[10,24,256]{2,1,0:T(8,128)(2,1)S(1)}, bf16[64,256]{1,0:T(8,128)(2,1)S(1)}, bf16[6,64,256]{2,1,0:T(8,128...) custom-call(bf16[64,256]{1,0:T(8,128)(2,1)} %bitcast.10, ...), custom_call_target="tpu_custom_call" | custom-call | tf_op jit(solution)/shard_map/pack/pallas_call | solution.py:448
  1.2 1.3 %collective-permute-start = (bf16[10,24,256]{2,1,0:T(8,128)(2,1)S(1)}, bf16[10,24,256]{2,1,0:T(8,128)(2,1)S(1)}, u32[]{:S(2)}, u32[]{:S(2)}) collective-permute-start(bf16[10,24,256]{2,1,0:T(8,128)(2,1)S(1)} %get-tuple-element.33), channel_id=1, source_target_pairs={{0,8},{8,0},{16,24},{24,16},{1,9},{9,1},{17,25},{25,17},{2,10},{10... | collective-permute-start | bytes 368648 | tf_op jit(solution)/shard_map/ppermute | solution.py:459
  2.4 1.9 %collective-permute-start.1 = (bf16[10,24,256]{2,1,0:T(8,128)(2,1)S(1)}, bf16[10,24,256]{2,1,0:T(8,128)(2,1)S(1)}, u32[]{:S(2)}, u32[]{:S(2)}) collective-permute-start(bf16[10,24,256]{2,1,0:T(8,128)(2,1)S(1)} %get-tuple-element.34), channel_id=1, source_target_pairs={{8,16},{16,8},{9,17},{17,9},{10,18},{18,10},{11,19},{19,11},{12,20... | collective-permute-start | bytes 368648 | tf_op jit(solution)/shard_map/ppermute | solution.py:460
  4.4 0.1 own.1.refs_0_
  4.4 1.0 %collective-permute-done.refs_1_ = bf16[10,24,256]{2,1,0:T(8,128)(2,1)S(1)} collective-permute-done((bf16[10,24,256]{2,1,0:T(8,128)(2,1)S(1)}, bf16[10,24,256]{2,1,0:T(8,128)(2,1)S(1)}, u32[]{:S(2)}, u32[]{:S(2)}) %collective-permute-start) | collective-permute-done | bytes 122912 | tf_op jit(solution)/shard_map/ppermute | solution.py:459
  5.4 3.5 %collective-permute-done.1.refs_2_ = bf16[10,24,256]{2,1,0:T(8,128)(2,1)S(1)} collective-permute-done((bf16[10,24,256]{2,1,0:T(8,128)(2,1)S(1)}, bf16[10,24,256]{2,1,0:T(8,128)(2,1)S(1)}, u32[]{:S(2)}, u32[]{:S(2)}) %collective-permute-start.1) | collective-permute-done | bytes 122912 | tf_op jit(solution)/shard_map/ppermute | solution.py:460
  9.0 0.4 %turn.1 = (f32[9,256,128]{2,1,0:T(8,128)S(1)}, bf16[736,128]{1,0:T(8,128)(2,1)S(1)}) custom-call(f32[9,64,256]{2,1,0:T(8,128)S(1)} %own.1.refs_0_, bf16[10,24,256]{2,1,0:T(8,128)(2,1)S(1)} %collective-permute-done.refs_1_, bf16[10,24,256]{2,1,0:T(8,128)(2,1)S(1)} %collective-permute-done.1.refs_2_), custom_call_target="tpu_custom_call" | custom-call | tf_op jit(solution)/shard_map/turn/pallas_call | solution.py:475
  9.3 2.4 %collective-permute-start.2 = (bf16[736,128]{1,0:T(8,128)(2,1)S(1)}, bf16[736,128]{1,0:T(8,128)(2,1)S(1)}, u32[]{:S(2)}, u32[]{:S(2)}) collective-permute-start(bf16[736,128]{1,0:T(8,128)(2,1)S(1)} %get-tuple-element.39), channel_id=1, source_target_pairs={{0,4},{1,5},{2,6},{3,7},{4,0},{5,1},{6,2},{7,3},{8,12},{9,13},{10,... | collective-permute-start | bytes 565256 | tf_op jit(solution)/shard_map/ppermute | solution.py:495
  11.7 0.5 %rims.1 = (bf16[736,128]{1,0:T(8,128)(2,1)S(1)}, bf16[736,128]{1,0:T(8,128)(2,1)S(1)}, bf16[120,128]{1,0:T(8,128)(2,1)S(1)}, bf16[120,128]{1,0:T(8,128)(2,1)S(1)}) custom-call(f32[9,256,128]{2,1,0:T(8,128)S(1)} %get-tuple-element.35.refs_0_), custom_call_target="tpu_custom_call" | custom-call | flops 1048576 | bytes 1048576 | tf_op jit(solution)/shard_map/rims/pallas_call | solution.py:484
  12.2 2.5 %collective-permute-start.3 = (bf16[736,128]{1,0:T(8,128)(2,1)S(1)}, bf16[736,128]{1,0:T(8,128)(2,1)S(1)}, u32[]{:S(2)}, u32[]{:S(2)}) collective-permute-start(bf16[736,128]{1,0:T(8,128)(2,1)S(1)} %get-tuple-element.40), channel_id=1, source_target_pairs={{0,1},{1,0},{2,3},{3,2},{4,5},{5,4},{6,7},{7,6},{8,9},{9,8},{10,11... | collective-permute-start | bytes 565256 | tf_op jit(solution)/shard_map/ppermute | solution.py:495
  14.7 3.1 %collective-permute-start.4 = (bf16[736,128]{1,0:T(8,128)(2,1)S(1)}, bf16[736,128]{1,0:T(8,128)(2,1)S(1)}, u32[]{:S(2)}, u32[]{:S(2)}) collective-permute-start(bf16[736,128]{1,0:T(8,128)(2,1)S(1)} %get-tuple-element.41), channel_id=1, source_target_pairs={{1,2},{2,1},{5,6},{6,5},{9,10},{10,9},{13,14},{14,13},{17,18},{18,... | collective-permute-start | bytes 565256 | tf_op jit(solution)/shard_map/ppermute | solution.py:495
  17.8 0.1 collective-permute-start.5
  17.9 3.1 %collective-permute-start.6 = (bf16[120,128]{1,0:T(8,128)(2,1)S(1)}, bf16[120,128]{1,0:T(8,128)(2,1)S(1)}, u32[]{:S(2)}, u32[]{:S(2)}) collective-permute-start(bf16[120,128]{1,0:T(8,128)(2,1)S(1)} %get-tuple-element.46), channel_id=1, source_target_pairs={{1,6},{2,5},{5,2},{6,1},{9,14},{10,13},{13,10},{14,9},{17,22},{18,... | collective-permute-start | bytes 92168 | tf_op jit(solution)/shard_map/ppermute | solution.py:495
  21.0 0.2 prepare.1
  21.2 0.0 collective-permute-done.2.refs_3_
  21.2 0.0 collective-permute-done.3.refs_4_
  21.2 2.2 %collective-permute-done.4.refs_5_ = bf16[736,128]{1,0:T(8,128)(2,1)S(1)} collective-permute-done((bf16[736,128]{1,0:T(8,128)(2,1)S(1)}, bf16[736,128]{1,0:T(8,128)(2,1)S(1)}, u32[]{:S(2)}, u32[]{:S(2)}) %collective-permute-start.4) | collective-permute-done | bytes 188448 | tf_op jit(solution)/shard_map/ppermute | solution.py:495
  23.5 0.7 %sides.1 = (f32[2,7,352,128]{3,2,1,0:T(8,128)S(1)}, f32[352,128]{1,0:T(8,128)S(1)}, f32[352,128]{1,0:T(8,128)S(1)}) custom-call(f32[2,7,352,128]{3,2,1,0:T(8,128)S(1)} %get-tuple-element.36.refs_0_, f32[352,128]{1,0:T(8,128)S(1)} %get-tuple-element.37.refs_1_, ...), custom_call_target="tpu_custom_call", output_to_operand_aliasing={{0}: (0, {}), {1}: (1, {}), {2}: (2, {})} | custom-call | flops 1024 | bytes 1024 | tf_op jit(solution)/shard_map/sides/pallas_call | solution.py:512
  24.2 0.0 collective-permute-done.5.refs_3_
  24.2 0.6 %collective-permute-done.6.refs_4_ = bf16[120,128]{1,0:T(8,128)(2,1)S(1)} collective-permute-done((bf16[120,128]{1,0:T(8,128)(2,1)S(1)}, bf16[120,128]{1,0:T(8,128)(2,1)S(1)}, u32[]{:S(2)}, u32[]{:S(2)}) %collective-permute-start.6) | collective-permute-done | bytes 30752 | tf_op jit(solution)/shard_map/ppermute | solution.py:495
  24.9 1.8 %smooth.1 = (f32[192,128]{1,0:T(8,128)}, f32[2,7,352,128]{3,2,1,0:T(8,128)S(1)}, f32[352,128]{1,0:T(8,128)S(1)}, f32[352,128]{1,0:T(8,128)S(1)}) custom-call(f32[2,7,352,128]{3,2,1,0:T(8,128)S(1)} %get-tuple-element.42.refs_0_, f32[352,128]{1,0:T(8,128)S(1)} %get-tuple-element.43.refs_1_, ...), custom_call_target="tpu_custom_call", output_to_operand_aliasing={{1}: (0, {}), {2}: (1, {}), {3}: (2, {})} | custom-call | tf_op jit(solution)/shard_map/smooth/pallas_call | solution.py:522
Async XLA Ops:
  1.2 4.3 %collective-permute-start = (bf16[10,24,256]{2,1,0:T(8,128)(2,1)S(1)}, bf16[10,24,256]{2,1,0:T(8,128)(2,1)S(1)}, u32[]{:S(2)}, u32[]{:S(2)}) collective-permute-start(bf16[10,24,256]{2,1,0:T(8,128)(2,1)S(1)} %get-tuple-element.33), channel_id=1, source_target_pairs={{0,8},{8,0},{16,24},{24,16},{1,9},{9,1},{17,25},{25,17},{2,10},{10... | collective-permute-start | bytes 368648 | tf_op jit(solution)/shard_map/ppermute | solution.py:459
  2.4 6.5 %collective-permute-start.1 = (bf16[10,24,256]{2,1,0:T(8,128)(2,1)S(1)}, bf16[10,24,256]{2,1,0:T(8,128)(2,1)S(1)}, u32[]{:S(2)}, u32[]{:S(2)}) collective-permute-start(bf16[10,24,256]{2,1,0:T(8,128)(2,1)S(1)} %get-tuple-element.34), channel_id=1, source_target_pairs={{8,16},{16,8},{9,17},{17,9},{10,18},{18,10},{11,19},{19,11},{12,20... | collective-permute-start | bytes 368648 | tf_op jit(solution)/shard_map/ppermute | solution.py:460
  9.3 11.9 %collective-permute-start.2 = (bf16[736,128]{1,0:T(8,128)(2,1)S(1)}, bf16[736,128]{1,0:T(8,128)(2,1)S(1)}, u32[]{:S(2)}, u32[]{:S(2)}) collective-permute-start(bf16[736,128]{1,0:T(8,128)(2,1)S(1)} %get-tuple-element.39), channel_id=1, source_target_pairs={{0,4},{1,5},{2,6},{3,7},{4,0},{5,1},{6,2},{7,3},{8,12},{9,13},{10,... | collective-permute-start | bytes 565256 | tf_op jit(solution)/shard_map/ppermute | solution.py:495
  12.2 9.0 %collective-permute-start.3 = (bf16[736,128]{1,0:T(8,128)(2,1)S(1)}, bf16[736,128]{1,0:T(8,128)(2,1)S(1)}, u32[]{:S(2)}, u32[]{:S(2)}) collective-permute-start(bf16[736,128]{1,0:T(8,128)(2,1)S(1)} %get-tuple-element.40), channel_id=1, source_target_pairs={{0,1},{1,0},{2,3},{3,2},{4,5},{5,4},{6,7},{7,6},{8,9},{9,8},{10,11... | collective-permute-start | bytes 565256 | tf_op jit(solution)/shard_map/ppermute | solution.py:495
  14.7 8.8 %collective-permute-start.4 = (bf16[736,128]{1,0:T(8,128)(2,1)S(1)}, bf16[736,128]{1,0:T(8,128)(2,1)S(1)}, u32[]{:S(2)}, u32[]{:S(2)}) collective-permute-start(bf16[736,128]{1,0:T(8,128)(2,1)S(1)} %get-tuple-element.41), channel_id=1, source_target_pairs={{1,2},{2,1},{5,6},{6,5},{9,10},{10,9},{13,14},{14,13},{17,18},{18,... | collective-permute-start | bytes 565256 | tf_op jit(solution)/shard_map/ppermute | solution.py:495
  17.8 6.5 %collective-permute-start.5 = (bf16[120,128]{1,0:T(8,128)(2,1)S(1)}, bf16[120,128]{1,0:T(8,128)(2,1)S(1)}, u32[]{:S(2)}, u32[]{:S(2)}) collective-permute-start(bf16[120,128]{1,0:T(8,128)(2,1)S(1)} %get-tuple-element.45), channel_id=1, source_target_pairs={{0,5},{1,4},{2,7},{3,6},{4,1},{5,0},{6,3},{7,2},{8,13},{9,12},{10,... | collective-permute-start | bytes 92168 | tf_op jit(solution)/shard_map/ppermute | solution.py:495
  17.9 7.0 %collective-permute-start.6 = (bf16[120,128]{1,0:T(8,128)(2,1)S(1)}, bf16[120,128]{1,0:T(8,128)(2,1)S(1)}, u32[]{:S(2)}, u32[]{:S(2)}) collective-permute-start(bf16[120,128]{1,0:T(8,128)(2,1)S(1)} %get-tuple-element.46), channel_id=1, source_target_pairs={{1,6},{2,5},{5,2},{6,1},{9,14},{10,13},{13,10},{14,9},{17,22},{18,... | collective-permute-start | bytes 92168 | tf_op jit(solution)/shard_map/ppermute | solution.py:495
